TPU v7x, 768 devices: a whole 4x8x12 slice. The times are simulated.
768 devices in a mesh: tm: 24 (over z, x_hi), space: 32 (over x_lo, y, core).
Axes of the slice: x: 4 (x_hi: 2, x_lo: 2; x = x_hi * 2 + x_lo), y: 8, z: 12, core: 2. Of those that a mesh axis runs over, the one named last changes fastest.
Arguments:
- noise_field: float32 [8, 24, 32, 6, 256], P(None, 'tm', 'space'), may hold values from -6 to 6
- gauge_links: float32 [4, 3, 24, 32, 6, 256], P(None, None, 'tm', 'space'), may hold values from -2.5 to 2.5
- clover: float32 [2, 6, 24, 32, 12, 256], P(None, None, 'tm', 'space'), may hold values from -0.9 to 0.9
- eigvecs: float32 [48, 24, 32, 6, 256], P(None, 'tm', 'space'), may hold values from -0.02734375 to 0.02734375
- partner: int32 [48], replicated, may hold values from 0 to 47, each once
- dilution: int32 [8], replicated, may hold values from 0 to 3
- boundary: int32 [4], replicated, may hold values from 0 to 1
Outputs:
- perambulator: float32 [32, 24, 96], P('space', 'tm')
- correlator: float32 [32, 24, 24], P('space', 'tm')
Inputs may be any that keep to these rules, and one draw needn't show every extreme that they name: `partner`: each of 0 to 47 once.
All inputs are finite; a program needn't handle non-finite values.
Results may differ from a plain program's by a relative error of at most 0.00029.
Values sent between devices are 32-bit elements; how exact they have to be, the bound alone decides.
No kernel may reach another device: no remote copies, remote signals or barrier semaphores. Data moves between devices by JAX's collectives and lax.ppermute only.
A program may use at most 64 MiB of HBM per device.

v0:
```python
import jax
import jax.numpy as jnp
from jax import lax
from jax.sharding import PartitionSpec as P

ITERS = 4
DILUTE = 4
SIDE = 16


diag_term = 4.1
step_size = 0.2
twist_table = (
    (((1, 0, -1), (0, 0, -1)), ((1, 0, 1), (0, 0, 1))),
    (((1, -1, 0), (0, 1, 0)), ((1, 1, 0), (0, -1, 0))),
    (((0, 0, -1), (1, 0, 1)), ((0, 0, 1), (1, 0, -1))),
    (((0, 1, 0), (1, 1, 0)), ((0, 1, 0), (1, 1, 0))),
)


def from_behind(block, axis, distance):
    devices = range(lax.axis_size(axis))
    route = [((i - distance) % len(devices), i) for i in devices]
    return lax.ppermute(block, axis, route)


def padded_2(array, sides, width):
    for axis, dim in sides:
        size, length = (lax.axis_size(axis), array.shape[dim])
        up = [(i, (i + 1) % size) for i in range(size)]
        down = [(j, i) for i, j in up]
        last = lax.slice_in_dim(array, length - width, length, axis=dim)
        initial = lax.slice_in_dim(array, 0, width, axis=dim)
        before = lax.ppermute(last, axis, up)
        after = lax.ppermute(initial, axis, down)
        array = jnp.concatenate([before, array, after], axis=dim)
    return array


def pair_add(first_pair, second_pair):
    return (first_pair[0] + second_pair[0], first_pair[1] + second_pair[1])


def pair_sub(first_pair, second_pair):
    return (first_pair[0] - second_pair[0], first_pair[1] - second_pair[1])


def pair_scale(factor, value_pair):
    return (factor * value_pair[0], factor * value_pair[1])


def pair_map(function_one, value_pair):
    return (function_one(value_pair[0]), function_one(value_pair[1]))


def scaled(value_pair, real_coef, imag_coef):
    if imag_coef == 0:
        return (real_coef * value_pair[0], real_coef * value_pair[1])
    return (-imag_coef * value_pair[1], imag_coef * value_pair[0])


def spin_twist(direction, adjoint, half_pair):
    outputs = []
    for source_spin, real_coef, imag_coef in twist_table[direction][adjoint]:
        picked = (half_pair[0][:, source_spin], half_pair[1][:, source_spin])
        outputs.append(scaled(picked, real_coef, imag_coef))
    return (
        jnp.stack([outputs[0][0], outputs[1][0]], 1),
        jnp.stack([outputs[0][1], outputs[1][1]], 1),
    )


def split_spins(spinor_pair):
    upper_half = (spinor_pair[0][:, 0:2], spinor_pair[1][:, 0:2])
    lower_half = (spinor_pair[0][:, 2:4], spinor_pair[1][:, 2:4])
    return (upper_half, lower_half)


def link_apply(link_real, link_imag, half_pair):
    total_real = 0.0
    total_imag = 0.0
    for column in range(3):
        matrix_real = jnp.moveaxis(link_real[:, :, :, column, :], 0, 2)
        matrix_imag = jnp.moveaxis(link_imag[:, :, :, column, :], 0, 2)
        vector_real = half_pair[0][..., column : column + 1, :]
        vector_imag = half_pair[1][..., column : column + 1, :]
        total_real = total_real + matrix_real * vector_real - matrix_imag * vector_imag
        total_imag = total_imag + matrix_real * vector_imag + matrix_imag * vector_real
    return (total_real, total_imag)


def link_adjoint(link_real, link_imag, half_pair):
    total_real = 0.0
    total_imag = 0.0
    for matrix_row in range(3):
        matrix_real = link_real[matrix_row]
        matrix_imag = link_imag[matrix_row]
        vector_real = half_pair[0][..., matrix_row : matrix_row + 1, :]
        vector_imag = half_pair[1][..., matrix_row : matrix_row + 1, :]
        total_real = total_real + matrix_real * vector_real + matrix_imag * vector_imag
        total_imag = total_imag + matrix_real * vector_imag - matrix_imag * vector_real
    return (total_real, total_imag)


def plane_shift(values, direction, forward, edge_sign):
    flat_index = lax.broadcasted_iota(jnp.int32, values.shape, values.ndim - 1)
    if direction == 0:
        coordinate = flat_index % SIDE
        if forward:
            return jnp.where(
                coordinate == SIDE - 1,
                edge_sign * jnp.roll(values, SIDE - 1, axis=-1),
                jnp.roll(values, -1, axis=-1),
            )
        return jnp.where(
            coordinate == 0,
            edge_sign * jnp.roll(values, 1 - SIDE, axis=-1),
            jnp.roll(values, 1, axis=-1),
        )
    coordinate = flat_index // SIDE
    if forward:
        rolled = jnp.roll(values, -SIDE, axis=-1)
        return jnp.where(coordinate == SIDE - 1, edge_sign * rolled, rolled)
    rolled = jnp.roll(values, SIDE, axis=-1)
    return jnp.where(coordinate == 0, edge_sign * rolled, rolled)


def clover_apply(clover, spinor_pair):
    parts_real = []
    parts_imag = []
    for chiral in range(2):
        block_real = clover[chiral][:, :, :, 0::2, :]
        block_imag = clover[chiral][:, :, :, 1::2, :]
        total_real = 0.0
        total_imag = 0.0
        for column in range(6):
            spin_index = 2 * chiral + column // 3
            color_index = column % 3
            vector_real = spinor_pair[0][:, spin_index, :, :, color_index, :][:, None]
            vector_imag = spinor_pair[1][:, spin_index, :, :, color_index, :][:, None]
            entry_real = block_real[:, :, :, column, :]
            entry_imag = block_imag[:, :, :, column, :]
            total_real = total_real + entry_real * vector_real - entry_imag * vector_imag
            total_imag = total_imag + entry_real * vector_imag + entry_imag * vector_real
        counts = total_real.shape
        new_shape = (counts[0], 2, 3) + counts[2:]
        parts_real.append(total_real.reshape(new_shape).transpose(0, 1, 3, 4, 2, 5))
        parts_imag.append(total_imag.reshape(new_shape).transpose(0, 1, 3, 4, 2, 5))
    return (jnp.concatenate(parts_real, 1), jnp.concatenate(parts_imag, 1))


def recombine(direction, ahead_linked, behind_moved):
    top_part = pair_add(ahead_linked, behind_moved)
    bottom_part = pair_sub(
        spin_twist(direction, 1, behind_moved), spin_twist(direction, 1, ahead_linked)
    )
    return (
        jnp.concatenate([top_part[0], bottom_part[0]], 1),
        jnp.concatenate([top_part[1], bottom_part[1]], 1),
    )


def build_source(noise_field, dilution, time_index):
    sources = noise_field.shape[0]
    spin_mask = (
        lax.broadcasted_iota(jnp.int32, (sources, 4), 1)
        == lax.broadcasted_iota(jnp.int32, (sources, 4), 0) % 4
    ).astype(jnp.float32)
    time_mask = (time_index[None, :] % DILUTE == dilution[:, None]).astype(jnp.float32)
    source_weight = (
        spin_mask[:, :, None, None, None, None] * time_mask[:, None, :, None, None, None]
    )
    return (
        source_weight * noise_field[:, None, :, :, 0::2, :],
        source_weight * noise_field[:, None, :, :, 1::2, :],
    )


def project(solution, eigvecs):
    counts = solution[0].shape
    flat_shape = (counts[0] * counts[1], counts[2], counts[3] * counts[4] * counts[5])
    solve_result_real = solution[0].reshape(flat_shape)
    solve_result_imag = solution[1].reshape(flat_shape)
    eig_shape = (eigvecs.shape[0], eigvecs.shape[1], flat_shape[2])
    eigenmode_real = eigvecs[:, :, :, 0::2, :].reshape(eig_shape)
    eigenmode_imag = eigvecs[:, :, :, 1::2, :].reshape(eig_shape)
    highest_value = lax.Precision.HIGHEST
    real_component = jnp.einsum(
        "gdc,xdc->xdg", eigenmode_real, solve_result_real, precision=highest_value
    ) + jnp.einsum("gdc,xdc->xdg", eigenmode_imag, solve_result_imag, precision=highest_value)
    imaginary_component = jnp.einsum(
        "gdc,xdc->xdg", eigenmode_real, solve_result_imag, precision=highest_value
    ) - jnp.einsum("gdc,xdc->xdg", eigenmode_imag, solve_result_real, precision=highest_value)
    return jnp.concatenate([real_component, imaginary_component], 2)


def weigh_pairs(peram_block, partner):
    vectors = partner.shape[0]
    onehot = (partner[:, None] == lax.broadcasted_iota(jnp.int32, (vectors, vectors), 1)).astype(
        jnp.float32
    )
    highest_value = lax.Precision.HIGHEST
    real_component = jnp.einsum(
        "jtk,kl->jtl", peram_block[:, :, :vectors], onehot, precision=highest_value
    )
    imaginary_component = jnp.einsum(
        "jtk,kl->jtl", peram_block[:, :, vectors:], onehot, precision=highest_value
    )
    return jnp.concatenate([real_component, imaginary_component], 2)


def shards(noise_field, gauge_links, clover, eigvecs, partner, dilution, boundary):
    phase_signs = 1.0 - 2.0 * boundary.astype(jnp.float32)
    local_times = noise_field.shape[1]
    local_planes = noise_field.shape[2]
    time_rank = lax.axis_index("tm")
    space_rank = lax.axis_index("space")
    time_index = time_rank * local_times + jnp.arange(local_times, dtype=jnp.int32)
    time_low = jnp.where(time_rank == 0, phase_signs[3], 1.0)
    time_high = jnp.where(time_rank == lax.axis_size("tm") - 1, phase_signs[3], 1.0)
    space_low = jnp.where(space_rank == 0, phase_signs[2], 1.0)
    space_high = jnp.where(space_rank == lax.axis_size("space") - 1, phase_signs[2], 1.0)
    link_time_low = from_behind(gauge_links[3], "tm", 1)
    link_space_low = from_behind(gauge_links[2], "space", 1)
    behind_time_link = jnp.concatenate([link_time_low, gauge_links[3][:, : local_times - 1]], 1)
    behind_space_link = jnp.concatenate(
        [link_space_low, gauge_links[2][:, :, : local_planes - 1]], 2
    )
    source = build_source(noise_field, dilution, time_index)
    solution = pair_scale(step_size, source)
    for iteration in range(ITERS):
        upper_half, lower_half = split_spins(solution)
        stacked = jnp.stack([solution[0], solution[1]])
        padded = padded_2(stacked, (("tm", 3), ("space", 4)), 1)
        interior = padded[:, :, :, :, 1 : local_planes + 1]
        time_above = interior[:, :, :, local_times + 1 :] * time_high
        time_below = interior[:, :, :, :1] * time_low
        ahead_time = jnp.concatenate([stacked[:, :, :, 1:], time_above], 3)
        behind_time = jnp.concatenate([time_below, stacked[:, :, :, : local_times - 1]], 3)
        columns = padded[:, :, :, 1 : local_times + 1]
        plane_above = columns[:, :, :, :, local_planes + 1 :] * space_high
        plane_below = columns[:, :, :, :, :1] * space_low
        ahead_space = jnp.concatenate([stacked[:, :, :, :, 1:], plane_above], 4)
        behind_space = jnp.concatenate([plane_below, stacked[:, :, :, :, : local_planes - 1]], 4)
        hopping = (0.0, 0.0)
        for direction in range(4):
            link_real = gauge_links[direction][:, :, :, 0::2, :]
            link_imag = gauge_links[direction][:, :, :, 1::2, :]
            if direction < 2:
                twisted = spin_twist(direction, 0, lower_half)
                ahead_half = pair_sub(upper_half, twisted)
                behind_half = link_adjoint(link_real, link_imag, pair_add(upper_half, twisted))
                edge_sign = phase_signs[direction]
                ahead_moved = pair_map(
                    lambda values: plane_shift(values, direction, True, edge_sign), ahead_half
                )
                behind_moved = pair_map(
                    lambda values: plane_shift(values, direction, False, edge_sign), behind_half
                )
            else:
                ahead_full = ahead_time if direction == 3 else ahead_space
                behind_full = behind_time if direction == 3 else behind_space
                behind_link = behind_time_link if direction == 3 else behind_space_link
                ahead_upper, ahead_lower = split_spins((ahead_full[0], ahead_full[1]))
                ahead_moved = pair_sub(ahead_upper, spin_twist(direction, 0, ahead_lower))
                behind_upper, behind_lower = split_spins((behind_full[0], behind_full[1]))
                behind_twisted = spin_twist(direction, 0, behind_lower)
                behind_moved = link_adjoint(
                    behind_link[:, :, :, 0::2, :],
                    behind_link[:, :, :, 1::2, :],
                    pair_add(behind_upper, behind_twisted),
                )
            ahead_linked = link_apply(link_real, link_imag, ahead_moved)
            hopping = pair_add(hopping, recombine(direction, ahead_linked, behind_moved))
        clovered = clover_apply(clover, solution)
        result = pair_add(pair_scale(diag_term, solution), clovered)
        applied = pair_sub(result, pair_scale(0.5, hopping))
        solution = pair_add(solution, pair_scale(step_size, pair_sub(source, applied)))
    partial_sums = project(solution, eigvecs)
    share_rows = partial_sums.shape[0] // lax.axis_size("space")
    summed = lax.psum(partial_sums, "space")
    own_block = lax.dynamic_slice_in_dim(summed, space_rank * share_rows, share_rows, 0)
    weighted = weigh_pairs(own_block, partner)
    correlator = jnp.einsum(
        "jac,jbc->jab",
        weighted,
        lax.all_gather(own_block, "tm", axis=1, tiled=True),
        precision=lax.Precision.HIGHEST,
    )
    return (own_block, correlator)


def solution(mesh):
    return jax.shard_map(
        shards,
        mesh=mesh,
        in_specs=(
            P(None, "tm", "space", None, None),
            P(None, None, "tm", "space", None, None),
            P(None, None, "tm", "space", None, None),
            P(None, "tm", "space", None, None),
            P(),
            P(),
            P(),
        ),
        out_specs=(P("space", "tm", None), P("space", "tm", None)),
        check_vma=False,
    )
```

profile of v0, /device:TPU:2, one launch (start us, length us, event | category | flops | bytes accessed | tf_op | source)
XLA Modules:
  0.0 411.7 jit_solution(12290971923057667902)
XLA Ops:
  0.7 0.8 fusion.443
  2.3 16.1 %collective-permute-start.1 = (f32[2,8,4,1,1,3,256]{6,1,5,2,4,3,0:T(8,128)S(1)}, f32[2,8,4,1,1,3,256]{6,1,5,2,4,3,0:T(8,128)S(1)}, u32[]{:S(2)}, u32[]{:S(2)}) collective-permute-start(f32[2,8,4,1,1,3,256]{6,1,5,2,4,3,0:T(8,128)S(1)} %pad_maximum_fusion.4), channel_id=1, source_target_pairs={{32,0},{64,32},{96,64},{128,96},{160,128},{192,160},{224,192},{256... | collective-permute-start | bytes 589832 | tf_op jit(solution)/shard_map/ppermute | solution.py:35
  18.4 1.9 collective-permute-start
  21.0 1.9 collective-permute-start.5
  22.9 1.9 collective-permute-start.3
  25.0 0.8 fusion.444
  33.8 0.7 fusion.159
  34.7 1.4 add_bitcast_fusion.4
  38.1 1.2 add_bitcast_fusion.3
  44.6 1.3 bitcast_add_fusion.10
  46.0 1.3 fusion.373
  47.3 0.9 copy-done
  48.2 0.8 slice_reduce_fusion
  68.2 3.6 collective-permute-start.4
  71.8 4.1 collective-permute-start.2
  76.7 4.8 %collective-permute-done.4 = f32[2,8,4,3,1,3,256]{6,1,5,2,4,3,0:T(8,128)S(1)} collective-permute-done((f32[2,8,4,3,1,3,256]{6,1,5,2,4,3,0:T(8,128)S(1)}, f32[2,8,4,3,1,3,256]{6,1,5,2,4,3,0:T(8,128)S(1)}, u32[]{:S(2)}, u32[]{:S(2)}) %collective-permute-start.4) | collective-permute-done | bytes 589856 | tf_op jit(solution)/shard_map/ppermute | solution.py:34
  81.7 1.6 collective-permute-done.2
  96.5 1.3 add_bitcast_fusion.1
  99.0 1.3 add_bitcast_fusion.7
  101.8 7.5 %collective-permute-start.7 = (f32[2,8,4,1,1,3,256]{6,1,5,2,4,3,0:T(8,128)S(1)}, f32[2,8,4,1,1,3,256]{6,1,5,2,4,3,0:T(8,128)S(1)}, u32[]{:S(2)}, u32[]{:S(2)}) collective-permute-start(f32[2,8,4,1,1,3,256]{6,1,5,2,4,3,0:T(8,128)S(1)} %pad_maximum_fusion.5), channel_id=1, source_target_pairs={{32,0},{64,32},{96,64},{128,96},{160,128},{192,160},{224,192},{256... | collective-permute-start | bytes 589832 | tf_op jit(solution)/shard_map/ppermute | solution.py:35
  109.4 1.9 collective-permute-start.6
  113.2 1.3 bitcast_add_fusion.5
  115.3 1.3 bitcast_add_fusion.9
  116.7 0.8 copy-done.2
  130.3 1.9 collective-permute-start.9
  132.2 6.4 %collective-permute-start.8 = (f32[2,8,4,3,1,3,256]{6,1,5,2,4,3,0:T(8,128)S(1)}, f32[2,8,4,3,1,3,256]{6,1,5,2,4,3,0:T(8,128)S(1)}, u32[]{:S(2)}, u32[]{:S(2)}) collective-permute-start(f32[2,8,4,3,1,3,256]{6,1,5,2,4,3,0:T(8,128)S(1)} %pad_maximum_fusion.1), channel_id=1, source_target_pairs={{1,0},{2,1},{3,2},{4,3},{5,4},{6,5},{7,6},{8,7},{9,8},{10,9},{11,1... | collective-permute-start | bytes 1769480 | tf_op jit(solution)/shard_map/ppermute | solution.py:35
  139.5 4.6 %collective-permute-done.9 = f32[2,8,4,3,1,3,256]{6,1,5,2,4,3,0:T(8,128)S(1)} collective-permute-done((f32[2,8,4,3,1,3,256]{6,1,5,2,4,3,0:T(8,128)S(1)}, f32[2,8,4,3,1,3,256]{6,1,5,2,4,3,0:T(8,128)S(1)}, u32[]{:S(2)}, u32[]{:S(2)}) %collective-permute-start.9) | collective-permute-done | bytes 589856 | tf_op jit(solution)/shard_map/ppermute | solution.py:34
  144.3 1.6 collective-permute-done.8
  160.2 0.7 fusion.155
  161.7 1.3 fusion.390
  165.7 0.8 copy-done.3
  166.5 1.2 add_bitcast_fusion.6
  169.2 7.0 %collective-permute-start.11 = (f32[2,8,4,1,1,3,256]{6,1,5,2,4,3,0:T(8,128)S(1)}, f32[2,8,4,1,1,3,256]{6,1,5,2,4,3,0:T(8,128)S(1)}, u32[]{:S(2)}, u32[]{:S(2)}) collective-permute-start(f32[2,8,4,1,1,3,256]{6,1,5,2,4,3,0:T(8,128)S(1)} %pad_maximum_fusion.6), channel_id=1, source_target_pairs={{32,0},{64,32},{96,64},{128,96},{160,128},{192,160},{224,192},{256... | collective-permute-start | bytes 589832 | tf_op jit(solution)/shard_map/ppermute | solution.py:35
  176.2 1.9 collective-permute-start.10
  189.9 1.9 collective-permute-start.13
  191.9 6.2 %collective-permute-start.12 = (f32[2,8,4,3,1,3,256]{6,1,5,2,4,3,0:T(8,128)S(1)}, f32[2,8,4,3,1,3,256]{6,1,5,2,4,3,0:T(8,128)S(1)}, u32[]{:S(2)}, u32[]{:S(2)}) collective-permute-start(f32[2,8,4,3,1,3,256]{6,1,5,2,4,3,0:T(8,128)S(1)} %pad_maximum_fusion.2), channel_id=1, source_target_pairs={{1,0},{2,1},{3,2},{4,3},{5,4},{6,5},{7,6},{8,7},{9,8},{10,9},{11,1... | collective-permute-start | bytes 1769480 | tf_op jit(solution)/shard_map/ppermute | solution.py:35
  198.3 5.4 %collective-permute-done.13 = f32[2,8,4,3,1,3,256]{6,1,5,2,4,3,0:T(8,128)S(1)} collective-permute-done((f32[2,8,4,3,1,3,256]{6,1,5,2,4,3,0:T(8,128)S(1)}, f32[2,8,4,3,1,3,256]{6,1,5,2,4,3,0:T(8,128)S(1)}, u32[]{:S(2)}, u32[]{:S(2)}) %collective-permute-start.13) | collective-permute-done | bytes 589856 | tf_op jit(solution)/shard_map/ppermute | solution.py:34
  203.9 1.6 collective-permute-done.12
  208.4 7.0 %collective-permute-start.15 = (f32[2,8,4,1,1,3,256]{6,1,5,2,4,3,0:T(8,128)S(1)}, f32[2,8,4,1,1,3,256]{6,1,5,2,4,3,0:T(8,128)S(1)}, u32[]{:S(2)}, u32[]{:S(2)}) collective-permute-start(f32[2,8,4,1,1,3,256]{6,1,5,2,4,3,0:T(8,128)S(1)} %pad_maximum_fusion.7), channel_id=1, source_target_pairs={{32,0},{64,32},{96,64},{128,96},{160,128},{192,160},{224,192},{256... | collective-permute-start | bytes 589832 | tf_op jit(solution)/shard_map/ppermute | solution.py:35
  215.4 1.9 collective-permute-start.14
  222.7 3.9 collective-permute-done.14
  226.6 1.9 collective-permute-start.17
  228.6 5.8 %collective-permute-start.16 = (f32[2,8,4,3,1,3,256]{6,1,5,2,4,3,0:T(8,128)S(1)}, f32[2,8,4,3,1,3,256]{6,1,5,2,4,3,0:T(8,128)S(1)}, u32[]{:S(2)}, u32[]{:S(2)}) collective-permute-start(f32[2,8,4,3,1,3,256]{6,1,5,2,4,3,0:T(8,128)S(1)} %pad_maximum_fusion.3), channel_id=1, source_target_pairs={{1,0},{2,1},{3,2},{4,3},{5,4},{6,5},{7,6},{8,7},{9,8},{10,9},{11,1... | collective-permute-start | bytes 1769480 | tf_op jit(solution)/shard_map/ppermute | solution.py:35
  234.8 5.2 %collective-permute-done.17 = f32[2,8,4,3,1,3,256]{6,1,5,2,4,3,0:T(8,128)S(1)} collective-permute-done((f32[2,8,4,3,1,3,256]{6,1,5,2,4,3,0:T(8,128)S(1)}, f32[2,8,4,3,1,3,256]{6,1,5,2,4,3,0:T(8,128)S(1)}, u32[]{:S(2)}, u32[]{:S(2)}) %collective-permute-start.17) | collective-permute-done | bytes 589856 | tf_op jit(solution)/shard_map/ppermute | solution.py:34
  240.1 1.6 collective-permute-done.16
  244.5 1.0 fusion.51
  246.7 108.4 %psum.7 = f32[32,1,96]{2,0,1:T(8,128)S(1)} all-reduce(f32[32,1,96]{2,0,1:T(8,128)S(1)} %pad_maximum_fusion.24), channel_id=1, replica_groups=mesh['tm'=24,'space'=32] {'space'}, use_global_device_ids=true, to_apply=%region_0.1 | all-reduce | flops 3072 | bytes 24576 | tf_op jit(solution)/shard_map/psum | solution.py:281
  356.2 54.8 %all_gather.3 = f32[1,24,96]{2,0,1:T(1,128)S(1)} all-gather(f32[1,1,96]{2,0,1:T(1,128)S(1)} %constant_dynamic-slice_fusion), channel_id=1, replica_groups=mesh['tm'=24,'space'=32] {'tm'}, dimensions={1}, use_global_device_ids=true | all-gather | bytes 9600 | tf_op jit(solution)/shard_map/all_gather | solution.py:287
  (910 shorter events, 109.6 us)
Async XLA Ops:
  2.2 18.1 %copy-start.114 = (f32[4,3,1,1,6,256]{5,3,4,2,1,0:T(1,128)S(1)}, f32[4,3,1,1,6,256]{5,3,4,2,1,0:T(1,128)}, u32[]{:S(2)}) copy-start(f32[4,3,1,1,6,256]{5,3,4,2,1,0:T(1,128)} %param.8) | copy-start | bytes 221188
  2.3 63.3 %collective-permute-start.1 = (f32[2,8,4,1,1,3,256]{6,1,5,2,4,3,0:T(8,128)S(1)}, f32[2,8,4,1,1,3,256]{6,1,5,2,4,3,0:T(8,128)S(1)}, u32[]{:S(2)}, u32[]{:S(2)}) collective-permute-start(f32[2,8,4,1,1,3,256]{6,1,5,2,4,3,0:T(8,128)S(1)} %pad_maximum_fusion.4), channel_id=1, source_target_pairs={{32,0},{64,32},{96,64},{128,96},{160,128},{192,160},{224,192},{256... | collective-permute-start | bytes 589832 | tf_op jit(solution)/shard_map/ppermute | solution.py:35
  18.4 47.3 %collective-permute-start = (f32[2,8,4,1,1,3,256]{6,1,5,2,4,3,0:T(8,128)S(1)}, f32[2,8,4,1,1,3,256]{6,1,5,2,4,3,0:T(8,128)S(1)}, u32[]{:S(2)}, u32[]{:S(2)}) collective-permute-start(f32[2,8,4,1,1,3,256]{6,1,5,2,4,3,0:T(8,128)S(1)} %pad_maximum_fusion.4), channel_id=1, source_target_pairs={{0,32},{32,64},{64,96},{96,128},{128,160},{160,192},{192,224},{224... | collective-permute-start | bytes 589832 | tf_op jit(solution)/shard_map/ppermute | solution.py:34
  21.0 43.0 %collective-permute-start.5 = (f32[3,1,1,6,256]{4,2,3,1,0:T(1,128)}, f32[3,1,1,6,256]{4,2,3,1,0:T(1,128)}, u32[]{:S(2)}, u32[]{:S(2)}) collective-permute-start(f32[3,1,1,6,256]{4,2,3,1,0:T(1,128)} %get-tuple-element.390), channel_id=1, source_target_pairs={{736,0},{0,32},{32,64},{64,96},{96,128},{128,160},{160,192},{192,2... | collective-permute-start | bytes 55304 | tf_op jit(solution)/shard_map/ppermute | solution.py:24
  22.9 41.9 %collective-permute-start.3 = (f32[3,1,1,6,256]{4,2,3,1,0:T(1,128)}, f32[3,1,1,6,256]{4,2,3,1,0:T(1,128)}, u32[]{:S(2)}, u32[]{:S(2)}) collective-permute-start(f32[3,1,1,6,256]{4,2,3,1,0:T(1,128)} %get-tuple-element.393), channel_id=1, source_target_pairs={{31,0},{0,1},{1,2},{2,3},{3,4},{4,5},{5,6},{6,7},{7,8},{8,9},{9,10... | collective-permute-start | bytes 55304 | tf_op jit(solution)/shard_map/ppermute | solution.py:24
  26.2 0.9 copy-start.47
  31.4 60.8 %copy-start.48 = (f32[1,1,1,3,256]{4,3,2,1,0:T(4,128)}, f32[1,1,1,3,256]{4,3,2,1,0:T(4,128)S(1)}, u32[]{:S(2)}) copy-start(f32[1,1,1,3,256]{4,3,2,1,0:T(4,128)S(1)} %copy.870) | copy-start | bytes 9220
  31.4 60.8 %copy-start.51 = (f32[1,1,1,3,256]{4,3,2,1,0:T(4,128)}, f32[1,1,1,3,256]{4,3,2,1,0:T(4,128)S(1)}, u32[]{:S(2)}) copy-start(f32[1,1,1,3,256]{4,3,2,1,0:T(4,128)S(1)} %copy.866) | copy-start | bytes 9220
  31.4 60.8 %copy-start.54 = (f32[1,1,1,3,256]{4,3,2,1,0:T(4,128)}, f32[1,1,1,3,256]{4,3,2,1,0:T(4,128)S(1)}, u32[]{:S(2)}) copy-start(f32[1,1,1,3,256]{4,3,2,1,0:T(4,128)S(1)} %copy.868) | copy-start | bytes 9220
  47.2 1.0 copy-start
  57.2 1.3 copy-start.123
  68.2 13.3 %collective-permute-start.4 = (f32[2,8,4,3,1,3,256]{6,1,5,2,4,3,0:T(8,128)S(1)}, f32[2,8,4,3,1,3,256]{6,1,5,2,4,3,0:T(8,128)S(1)}, u32[]{:S(2)}, u32[]{:S(2)}) collective-permute-start(f32[2,8,4,3,1,3,256]{6,1,5,2,4,3,0:T(8,128)S(1)} %pad_maximum_fusion), channel_id=1, source_target_pairs={{0,1},{1,2},{2,3},{3,4},{4,5},{5,6},{6,7},{7,8},{8,9},{9,10},{10,1... | collective-permute-start | bytes 1769480 | tf_op jit(solution)/shard_map/ppermute | solution.py:34
  71.8 11.5 %collective-permute-start.2 = (f32[2,8,4,3,1,3,256]{6,1,5,2,4,3,0:T(8,128)S(1)}, f32[2,8,4,3,1,3,256]{6,1,5,2,4,3,0:T(8,128)S(1)}, u32[]{:S(2)}, u32[]{:S(2)}) collective-permute-start(f32[2,8,4,3,1,3,256]{6,1,5,2,4,3,0:T(8,128)S(1)} %pad_maximum_fusion), channel_id=1, source_target_pairs={{1,0},{2,1},{3,2},{4,3},{5,4},{6,5},{7,6},{8,7},{9,8},{10,9},{11,1... | collective-permute-start | bytes 1769480 | tf_op jit(solution)/shard_map/ppermute | solution.py:35
  101.8 25.8 %collective-permute-start.7 = (f32[2,8,4,1,1,3,256]{6,1,5,2,4,3,0:T(8,128)S(1)}, f32[2,8,4,1,1,3,256]{6,1,5,2,4,3,0:T(8,128)S(1)}, u32[]{:S(2)}, u32[]{:S(2)}) collective-permute-start(f32[2,8,4,1,1,3,256]{6,1,5,2,4,3,0:T(8,128)S(1)} %pad_maximum_fusion.5), channel_id=1, source_target_pairs={{32,0},{64,32},{96,64},{128,96},{160,128},{192,160},{224,192},{256... | collective-permute-start | bytes 589832 | tf_op jit(solution)/shard_map/ppermute | solution.py:35
  109.4 18.4 %collective-permute-start.6 = (f32[2,8,4,1,1,3,256]{6,1,5,2,4,3,0:T(8,128)S(1)}, f32[2,8,4,1,1,3,256]{6,1,5,2,4,3,0:T(8,128)S(1)}, u32[]{:S(2)}, u32[]{:S(2)}) collective-permute-start(f32[2,8,4,1,1,3,256]{6,1,5,2,4,3,0:T(8,128)S(1)} %pad_maximum_fusion.5), channel_id=1, source_target_pairs={{0,32},{32,64},{64,96},{96,128},{128,160},{160,192},{192,224},{224... | collective-permute-start | bytes 589832 | tf_op jit(solution)/shard_map/ppermute | solution.py:34
  118.9 1.4 copy-start.71
  119.0 1.4 copy-start.72
  130.3 13.8 %collective-permute-start.9 = (f32[2,8,4,3,1,3,256]{6,1,5,2,4,3,0:T(8,128)S(1)}, f32[2,8,4,3,1,3,256]{6,1,5,2,4,3,0:T(8,128)S(1)}, u32[]{:S(2)}, u32[]{:S(2)}) collective-permute-start(f32[2,8,4,3,1,3,256]{6,1,5,2,4,3,0:T(8,128)S(1)} %pad_maximum_fusion.1), channel_id=1, source_target_pairs={{0,1},{1,2},{2,3},{3,4},{4,5},{5,6},{6,7},{7,8},{8,9},{9,10},{10,1... | collective-permute-start | bytes 1769480 | tf_op jit(solution)/shard_map/ppermute | solution.py:34
  132.2 13.6 %collective-permute-start.8 = (f32[2,8,4,3,1,3,256]{6,1,5,2,4,3,0:T(8,128)S(1)}, f32[2,8,4,3,1,3,256]{6,1,5,2,4,3,0:T(8,128)S(1)}, u32[]{:S(2)}, u32[]{:S(2)}) collective-permute-start(f32[2,8,4,3,1,3,256]{6,1,5,2,4,3,0:T(8,128)S(1)} %pad_maximum_fusion.1), channel_id=1, source_target_pairs={{1,0},{2,1},{3,2},{4,3},{5,4},{6,5},{7,6},{8,7},{9,8},{10,9},{11,1... | collective-permute-start | bytes 1769480 | tf_op jit(solution)/shard_map/ppermute | solution.py:35
  169.2 9.0 %copy-start.124 = (f32[8,2,1,1,3,1]{0,1,5,4,3,2:T(2,128)S(1)}, f32[8,2,1,1,3,1]{0,1,5,4,3,2:T(2,128)}, u32[]{:S(2)}) copy-start(f32[8,2,1,1,3,1]{0,1,5,4,3,2:T(2,128)} %copy.601) | copy-start | bytes 580
  169.2 9.1 %copy-start.104 = (f32[8,2,1,1,3,1]{5,0,4,1,3,2:T(8,128)S(1)}, f32[8,2,1,1,3,1]{5,0,4,1,3,2:T(8,128)}, u32[]{:S(2)}) copy-start(f32[8,2,1,1,3,1]{5,0,4,1,3,2:T(8,128)} %get-tuple-element.616) | copy-start | bytes 580
  169.2 19.9 %collective-permute-start.11 = (f32[2,8,4,1,1,3,256]{6,1,5,2,4,3,0:T(8,128)S(1)}, f32[2,8,4,1,1,3,256]{6,1,5,2,4,3,0:T(8,128)S(1)}, u32[]{:S(2)}, u32[]{:S(2)}) collective-permute-start(f32[2,8,4,1,1,3,256]{6,1,5,2,4,3,0:T(8,128)S(1)} %pad_maximum_fusion.6), channel_id=1, source_target_pairs={{32,0},{64,32},{96,64},{128,96},{160,128},{192,160},{224,192},{256... | collective-permute-start | bytes 589832 | tf_op jit(solution)/shard_map/ppermute | solution.py:35
  176.2 13.0 %collective-permute-start.10 = (f32[2,8,4,1,1,3,256]{6,1,5,2,4,3,0:T(8,128)S(1)}, f32[2,8,4,1,1,3,256]{6,1,5,2,4,3,0:T(8,128)S(1)}, u32[]{:S(2)}, u32[]{:S(2)}) collective-permute-start(f32[2,8,4,1,1,3,256]{6,1,5,2,4,3,0:T(8,128)S(1)} %pad_maximum_fusion.6), channel_id=1, source_target_pairs={{0,32},{32,64},{64,96},{96,128},{128,160},{160,192},{192,224},{224... | collective-permute-start | bytes 589832 | tf_op jit(solution)/shard_map/ppermute | solution.py:34
  189.9 13.8 %collective-permute-start.13 = (f32[2,8,4,3,1,3,256]{6,1,5,2,4,3,0:T(8,128)S(1)}, f32[2,8,4,3,1,3,256]{6,1,5,2,4,3,0:T(8,128)S(1)}, u32[]{:S(2)}, u32[]{:S(2)}) collective-permute-start(f32[2,8,4,3,1,3,256]{6,1,5,2,4,3,0:T(8,128)S(1)} %pad_maximum_fusion.2), channel_id=1, source_target_pairs={{0,1},{1,2},{2,3},{3,4},{4,5},{5,6},{6,7},{7,8},{8,9},{9,10},{10,1... | collective-permute-start | bytes 1769480 | tf_op jit(solution)/shard_map/ppermute | solution.py:34
  191.9 13.6 %collective-permute-start.12 = (f32[2,8,4,3,1,3,256]{6,1,5,2,4,3,0:T(8,128)S(1)}, f32[2,8,4,3,1,3,256]{6,1,5,2,4,3,0:T(8,128)S(1)}, u32[]{:S(2)}, u32[]{:S(2)}) collective-permute-start(f32[2,8,4,3,1,3,256]{6,1,5,2,4,3,0:T(8,128)S(1)} %pad_maximum_fusion.2), channel_id=1, source_target_pairs={{1,0},{2,1},{3,2},{4,3},{5,4},{6,5},{7,6},{8,7},{9,8},{10,9},{11,1... | collective-permute-start | bytes 1769480 | tf_op jit(solution)/shard_map/ppermute | solution.py:35
  208.4 14.3 %collective-permute-start.15 = (f32[2,8,4,1,1,3,256]{6,1,5,2,4,3,0:T(8,128)S(1)}, f32[2,8,4,1,1,3,256]{6,1,5,2,4,3,0:T(8,128)S(1)}, u32[]{:S(2)}, u32[]{:S(2)}) collective-permute-start(f32[2,8,4,1,1,3,256]{6,1,5,2,4,3,0:T(8,128)S(1)} %pad_maximum_fusion.7), channel_id=1, source_target_pairs={{32,0},{64,32},{96,64},{128,96},{160,128},{192,160},{224,192},{256... | collective-permute-start | bytes 589832 | tf_op jit(solution)/shard_map/ppermute | solution.py:35
  215.4 11.2 %collective-permute-start.14 = (f32[2,8,4,1,1,3,256]{6,1,5,2,4,3,0:T(8,128)S(1)}, f32[2,8,4,1,1,3,256]{6,1,5,2,4,3,0:T(8,128)S(1)}, u32[]{:S(2)}, u32[]{:S(2)}) collective-permute-start(f32[2,8,4,1,1,3,256]{6,1,5,2,4,3,0:T(8,128)S(1)} %pad_maximum_fusion.7), channel_id=1, source_target_pairs={{0,32},{32,64},{64,96},{96,128},{128,160},{160,192},{192,224},{224... | collective-permute-start | bytes 589832 | tf_op jit(solution)/shard_map/ppermute | solution.py:34
  226.6 13.3 %collective-permute-start.17 = (f32[2,8,4,3,1,3,256]{6,1,5,2,4,3,0:T(8,128)S(1)}, f32[2,8,4,3,1,3,256]{6,1,5,2,4,3,0:T(8,128)S(1)}, u32[]{:S(2)}, u32[]{:S(2)}) collective-permute-start(f32[2,8,4,3,1,3,256]{6,1,5,2,4,3,0:T(8,128)S(1)} %pad_maximum_fusion.3), channel_id=1, source_target_pairs={{0,1},{1,2},{2,3},{3,4},{4,5},{5,6},{6,7},{7,8},{8,9},{9,10},{10,1... | collective-permute-start | bytes 1769480 | tf_op jit(solution)/shard_map/ppermute | solution.py:34
  228.6 13.1 %collective-permute-start.16 = (f32[2,8,4,3,1,3,256]{6,1,5,2,4,3,0:T(8,128)S(1)}, f32[2,8,4,3,1,3,256]{6,1,5,2,4,3,0:T(8,128)S(1)}, u32[]{:S(2)}, u32[]{:S(2)}) collective-permute-start(f32[2,8,4,3,1,3,256]{6,1,5,2,4,3,0:T(8,128)S(1)} %pad_maximum_fusion.3), channel_id=1, source_target_pairs={{1,0},{2,1},{3,2},{4,3},{5,4},{6,5},{7,6},{8,7},{9,8},{10,9},{11,1... | collective-permute-start | bytes 1769480 | tf_op jit(solution)/shard_map/ppermute | solution.py:35
  241.9 0.9 copy-start.28
  241.9 0.9 copy-start.29
  241.9 0.9 copy-start.38
  241.9 0.9 copy-start.39
  241.9 1.0 copy-start.41
  242.0 0.9 copy-start.16
  242.0 0.9 copy-start.18
  242.0 0.9 copy-start.44
  242.1 0.9 copy-start.45
  242.1 1.0 copy-start.46
  242.2 0.9 copy-start.8
  242.2 0.9 copy-start.9
  243.1 0.9 copy-start.34
  243.2 0.9 copy-start.36
  243.2 0.9 copy-start.37
  243.2 0.9 copy-start.40
  243.2 1.0 copy-start.42
  243.2 1.0 copy-start.43
  243.6 0.9 copy-start.7
  (98 other events, 75.2 us)
where the time goes:
time: 415 us; the launch traced here: 412 us
  blocking collectives  163 us (39%)
  starting transfers between devices  81.1 us (20%)
  other arithmetic  72.9 us (18%)
  local copies, waits for them, and re-layouts  54.8 us (13%)
  waiting for transfers between devices  30.5 us (7%)
  between operations  7.03 us (2%)
    psum x1, blocking collectives, shards(): summed = lax.psum(partial_sums, 'space')  108 us
    ppermute x8, starting transfers between devices, padded_2(): after = lax.ppermute(initial, axis, down)  60.3 us
    all_gather x1, blocking collectives, shards(): lax.all_gather(own_block, 'tm', axis=1, tiled=True)  54.8 us
    add x76, other arithmetic, pair_add(): return (first_pair[0] + second_pair[0], first_pair[1] + second_pair[1])  33.8 us
    unnamed x309, local copies, waits for them, and re-layouts  27.1 us
    ppermute x8, waiting for transfers between devices, padded_2(): before = lax.ppermute(last, axis, up)  24 us
    ppermute x8, starting transfers between devices, padded_2(): before = lax.ppermute(last, axis, up)  17 us
    sub x54, other arithmetic, pair_sub(): return (first_pair[0] - second_pair[0], first_pair[1] - second_pair[1])  9.53 us
  transfers between devices with their start and end apart: 18, of which 9 were waited for; matrix products, arithmetic and copies ran while one was open for 13% of the time, Pallas kernels for 0%

commit v1 on v0

v1 whole, which is shorter than its diff:
```python
import jax
import jax.numpy as jnp
from jax import lax
from jax.experimental import pallas as pl
from jax.experimental.pallas import tpu as pltpu
from jax.sharding import PartitionSpec as P

ITERS = 4
DILUTE = 4
SIDE = 16
LANES = 128
diag_term = 4.1
step_size = 0.2
F32 = jnp.float32

twist_table = (
    (((1, 0, -1), (0, 0, -1)), ((1, 0, 1), (0, 0, 1))),
    (((1, -1, 0), (0, 1, 0)), ((1, 1, 0), (0, -1, 0))),
    (((0, 0, -1), (1, 0, 1)), ((0, 0, 1), (1, 0, -1))),
    (((0, 1, 0), (1, 1, 0)), ((0, 1, 0), (1, 1, 0))),
)


def add_scaled(pair, sign, coef, other):
    real_coef, imag_coef = coef
    if imag_coef == 0:
        if sign * real_coef > 0:
            return (pair[0] + other[0], pair[1] + other[1])
        return (pair[0] - other[0], pair[1] - other[1])
    if sign * imag_coef > 0:
        return (pair[0] - other[1], pair[1] + other[0])
    return (pair[0] + other[1], pair[1] - other[0])


def row8(ref, row):
    return ref[pl.ds(row, 8, stride=0), :]


def link_times(links, mu, half, vector, adjoint):
    out = []
    for i in range(3):
        real, imag = None, None
        for k in range(3):
            row, col = (k, i) if adjoint else (i, k)
            base = ((mu * 3 + row) * 6 + 2 * col) * 2 + half
            mr, mi = row8(links, base), row8(links, base + 2)
            vr, vi = vector[k]
            if adjoint:
                r, m = mr * vr + mi * vi, mr * vi - mi * vr
            else:
                r, m = mr * vr - mi * vi, mr * vi + mi * vr
            real = r if real is None else real + r
            imag = m if imag is None else imag + m
        out.append((real, imag))
    return out


def spinor_at(spin, color, part, half):
    return ((spin * 3 + color) * 2 + part) * 2 + half


def load_spin(ref, spin, half):
    return [
        tuple(ref[spinor_at(spin, c, p, half)] for p in range(2)) for c in range(3)
    ]


def store_spin(ref, spin, half, value):
    for c in range(3):
        for p in range(2):
            ref[spinor_at(spin, c, p, half)] = value[c][p]


def half_spin(mu, comp, sign, upper, lower):
    _, real_coef, imag_coef = twist_table[mu][0][comp]
    return [
        add_scaled(upper[c], sign, (real_coef, imag_coef), lower[c]) for c in range(3)
    ]


def lower_target(mu, comp):
    for target in range(2):
        source, real_coef, imag_coef = twist_table[mu][1][target]
        if source == comp:
            return target, (real_coef, imag_coef)
    raise ValueError


def lower_source(mu, comp):
    return twist_table[mu][0][comp][0]


def accumulate(top, bottom, mu, comp, sign, hopped):
    _, coef = lower_target(mu, comp)
    top = [(top[c][0] + hopped[c][0], top[c][1] + hopped[c][1]) for c in range(3)]
    bottom = [add_scaled(bottom[c], sign, coef, hopped[c]) for c in range(3)]
    return top, bottom


def source_rows(shape):
    return lax.broadcasted_iota(jnp.int32, shape, 0)


def spin_mask(spin):
    return source_rows((8, LANES)) % 4 == spin


def prepare_kernel(time_rank, space_rank, last_time, last_space, bounds, dilution, noise, links_in,
                   links, source, behind_time, behind_space):
    lane = lax.broadcasted_iota(jnp.int32, (8, LANES), 1)
    row = lax.broadcasted_iota(jnp.int32, (8, LANES), 0)
    phases = [(1 - 2 * bounds[mu]).astype(F32) * (0.5 * step_size) for mu in range(4)]
    plain = 0.5 * step_size
    at_x = jnp.where(lane % SIDE == SIDE - 1, phases[0], plain)
    at_y = jnp.where((lane >= LANES - SIDE) & (row % 2 == 1), phases[1], plain)
    at_z = jnp.full((8, LANES), jnp.where(space_rank[0] == last_space, phases[2], plain))
    at_t = jnp.full((8, LANES), jnp.where(time_rank[0] == last_time, phases[3], plain))
    scales = (at_x, at_y, at_z, at_t)
    for block in range(18):
        first, last = (block * 8) // 36, (block * 8 + 7) // 36
        scale = scales[first]
        if last != first:
            scale = jnp.where(row + block * 8 >= last * 36, scales[last], scale)
        links[block * 8 : block * 8 + 8, :] = links_in[block * 8 : block * 8 + 8, :] * scale
    weight = jnp.zeros((8, LANES), F32)
    for j in range(8):
        on = jnp.where(time_rank[0] % DILUTE == dilution[j], step_size, 0.0)
        weight = jnp.where(row == j, on, weight)
    for half in range(2):
        vector = []
        for c in range(3):
            pair = []
            for p in range(2):
                plane = (c * 2 + p) * 2 + half
                value = noise[pl.ds(plane, 8, stride=12), :] * weight
                source[plane] = value
                pair.append(value)
            vector.append(tuple(pair))
        for mu, out in ((3, behind_time), (2, behind_space)):
            moved = link_times(links, mu, half, vector, True)
            store_spin(out, 0, half, moved)


def shift_x(value, forward):
    lane = lax.broadcasted_iota(jnp.int32, (8, LANES), 1) % SIDE
    if forward:
        return jnp.where(
            lane == SIDE - 1,
            pltpu.roll(value, SIDE - 1, 1),
            pltpu.roll(value, LANES - 1, 1),
        )
    return jnp.where(
        lane == 0, pltpu.roll(value, LANES - SIDE + 1, 1), pltpu.roll(value, 1, 1)
    )


def shift_y(low, high, forward):
    lane = lax.broadcasted_iota(jnp.int32, (8, LANES), 1)
    if forward:
        a, b = pltpu.roll(low, LANES - SIDE, 1), pltpu.roll(high, LANES - SIDE, 1)
        keep = lane < LANES - SIDE
    else:
        a, b = pltpu.roll(low, SIDE, 1), pltpu.roll(high, SIDE, 1)
        keep = lane >= SIDE
    return jnp.where(keep, a, b), jnp.where(keep, b, a)


def shift_plane(mu, pair_of_halves, forward):
    moved = ([], [])
    for c in range(3):
        parts = ([], [])
        for p in range(2):
            low, high = pair_of_halves[0][c][p], pair_of_halves[1][c][p]
            if mu == 0:
                low, high = shift_x(low, forward), shift_x(high, forward)
            else:
                low, high = shift_y(low, high, forward)
            parts[0].append(low)
            parts[1].append(high)
        moved[0].append(tuple(parts[0]))
        moved[1].append(tuple(parts[1]))
    return moved


def local_body(load, links, clover, source, out):
    for chiral in range(2):
        for half in range(2):
            vector = load(2 * chiral, half) + load(2 * chiral + 1, half)
            for a in range(6):
                real, imag = None, None
                for b in range(6):
                    base = ((chiral * 6 + a) * 12 + 2 * b) * 2 + half
                    mr, mi = row8(clover, base), row8(clover, base + 2)
                    vr, vi = vector[b]
                    r, m = mr * vr - mi * vi, mr * vi + mi * vr
                    real = r if real is None else real + r
                    imag = m if imag is None else imag + m
                spin, color = 2 * chiral + a // 3, a % 3
                here = spin_mask(spin)
                keep = 1.0 - step_size * diag_term
                for p, total in ((0, real), (1, imag)):
                    value = keep * vector[a][p] - step_size * total
                    value = value + jnp.where(here, source[(color * 2 + p) * 2 + half], 0.0)
                    out[spinor_at(spin, color, p, half)] = value
    for comp in range(2):
        low_spin = 2 + lower_source(0, comp)
        upper = [load(comp, half) for half in range(2)]
        lower = [load(low_spin, half) for half in range(2)]
        top = [load_spin(out, comp, half) for half in range(2)]
        bottom = [load_spin(out, low_spin, half) for half in range(2)]
        for mu in range(2):
            ahead = [half_spin(mu, comp, -1, upper[h], lower[h]) for h in range(2)]
            ahead = shift_plane(mu, ahead, True)
            for h in range(2):
                hopped = link_times(links, mu, h, ahead[h], False)
                top[h], bottom[h] = accumulate(top[h], bottom[h], mu, comp, -1, hopped)
            behind = [
                link_times(links, mu, h, half_spin(mu, comp, 1, upper[h], lower[h]), True)
                for h in range(2)
            ]
            behind = shift_plane(mu, behind, False)
            for h in range(2):
                top[h], bottom[h] = accumulate(top[h], bottom[h], mu, comp, 1, behind[h])
        for h in range(2):
            store_spin(out, comp, h, top[h])
            store_spin(out, low_spin, h, bottom[h])


def source_spinor(source):
    def load(spin, half):
        here = spin_mask(spin)
        return [
            tuple(jnp.where(here, source[(c * 2 + p) * 2 + half], 0.0) for p in range(2))
            for c in range(3)
        ]

    return load


def local_first_kernel(links, clover, source, out):
    local_body(source_spinor(source), links, clover, source, out)


def local_kernel(solution, links, clover, source, out):
    local_body(lambda spin, half: load_spin(solution, spin, half), links, clover, source, out)


def hops(local, links, received, comp, half):
    top, bottom = load_spin(local, comp, half), load_spin(local, 2 + comp, half)
    for mu, ahead, behind in received:
        hopped = link_times(links, mu, half, ahead(comp, half, mu, -1), False)
        top, bottom = accumulate(top, bottom, mu, comp, -1, hopped)
        top, bottom = accumulate(top, bottom, mu, comp, 1, behind(comp, half, mu, 1))
    return top, bottom


def from_halves(ref):
    return lambda comp, half, mu, sign: load_spin(ref, comp, half)


def from_source(ref):
    def load(comp, half, mu, sign):
        whole = source_spinor(ref)
        return half_spin(mu, comp, sign, whole(comp, half), whole(2 + comp, half))

    return load


def step_body(kind, local, links, at, bt, az, bz, solution, sat, sbt, saz, sbz):
    received = ((3, kind(at), kind(bt)), (2, kind(az), kind(bz)))
    for comp in range(2):
        for half in range(2):
            top, bottom = hops(local, links, received, comp, half)
            store_spin(solution, comp, half, top)
            store_spin(solution, 2 + comp, half, bottom)
            for mu, ahead, behind in ((3, sat, sbt), (2, saz, sbz)):
                store_spin(ahead, comp, half, half_spin(mu, comp, -1, top, bottom))
                plus = half_spin(mu, comp, 1, top, bottom)
                store_spin(behind, comp, half, link_times(links, mu, half, plus, True))


def step_first_kernel(*refs):
    step_body(from_source, *refs)


def step_kernel(*refs):
    step_body(from_halves, *refs)


def modes_kernel(modes, out):
    count = modes.shape[0] // 12
    out[...] = jnp.zeros(out.shape, out.dtype)
    for c in range(3):
        for half in range(2):
            real = modes[pl.ds(4 * c + half, count, stride=12), :]
            imag = modes[pl.ds(4 * c + 2 + half, count, stride=12), :]
            lanes = slice(half * LANES, half * LANES + LANES)
            for p, upper, lower in ((0, real, -imag), (1, imag, real)):
                for start, value in ((0, upper), (count, lower)):
                    high = value.astype(jnp.bfloat16)
                    low = (value - high.astype(F32)).astype(jnp.bfloat16)
                    out[2 * c + p, start : start + count, lanes] = high
                    out[2 * c + p, 128 + start : 128 + start + count, lanes] = low


def last_kernel(local, links, at, bt, az, bz, modes, out, rows):
    received = (
        (3, from_halves(at), from_halves(bt)),
        (2, from_halves(az), from_halves(bz)),
    )
    for comp in range(2):
        for half in range(2):
            pair = hops(local, links, received, comp, half)
            for spin, value in zip((comp, 2 + comp), pair, strict=True):
                for c in range(3):
                    for p in range(2):
                        rows[2 * c + p, 8 * spin : 8 * spin + 8, half * LANES : half * LANES + LANES] = value[c][p]
    total = None
    for plane in range(6):
        value = rows[plane]
        high = value.astype(jnp.bfloat16)
        low = (value - high.astype(F32)).astype(jnp.bfloat16)
        product = lax.dot_general(
            jnp.concatenate([high, low], 0),
            modes[plane],
            (((1,), (1,)), ((), ())),
            preferred_element_type=F32,
        )
        total = product if total is None else total + product
    total = total[:32, :128] + (total[:32, 128:] + total[32:, :128])
    for spin in range(4):
        out[pl.ds(spin, 8, stride=4), :] = total[8 * spin : 8 * spin + 8, : out.shape[1]]


def sum_kernel(parts, out):
    out[...] = jnp.sum(parts[...], axis=0, keepdims=True)


def correlate_kernel(row, rows, partner, out):
    size = row.shape[1]
    onehot = (
        partner[...] == lax.broadcasted_iota(jnp.int32, (size, size), 0)
    ).astype(F32)
    contract = (((1,), (1,)), ((), ()))
    own = jnp.broadcast_to(row[...], (8, size))
    weighted = lax.dot_general(
        own, onehot, contract, precision=lax.Precision.HIGHEST, preferred_element_type=F32
    )
    found = lax.dot_general(
        weighted, rows[...], contract, precision=lax.Precision.HIGHEST, preferred_element_type=F32
    )
    out[...] = found[:1]


def call(kernel, outs, flops, scalars, *args, scratch=()):
    vmem = pl.BlockSpec(memory_space=pltpu.VMEM)
    smem = pl.BlockSpec(memory_space=pltpu.SMEM)
    single = not isinstance(outs, (list, tuple))
    shapes = [outs] if single else list(outs)
    moved = 4 * sum(a.size for a in args) + 4 * sum(s.size for s in shapes)
    out = pl.pallas_call(
        kernel,
        out_shape=outs,
        in_specs=[smem] * len(scalars) + [vmem] * len(args),
        out_specs=vmem if single else [vmem] * len(shapes),
        scratch_shapes=scratch,
        compiler_params=pltpu.CompilerParams(vmem_limit_bytes=16 << 20),
        cost_estimate=pl.CostEstimate(flops=flops, bytes_accessed=moved, transcendentals=0),
    )(*scalars, *args)
    return out


def vectors(count):
    return jax.ShapeDtypeStruct((count, 8, LANES), F32)


def exchange(ahead_time, behind_time, ahead_space, behind_space):
    def ring(axis, step):
        size = lax.axis_size(axis)
        return [(i, (i + step) % size) for i in range(size)]

    az = lax.ppermute(ahead_space, "space", ring("space", -1))
    bz = lax.ppermute(behind_space, "space", ring("space", 1))
    at = lax.ppermute(ahead_time, "tm", ring("tm", -1))
    bt = lax.ppermute(behind_time, "tm", ring("tm", 1))
    return at, bt, az, bz


def partial_rows(noise_field, gauge_links, clover, eigvecs, dilution, boundary):
    count = eigvecs.shape[0]
    noise = noise_field.reshape(-1, LANES)
    links_in = gauge_links.reshape(-1, LANES)
    clover = clover.reshape(-1, LANES)
    modes_in = eigvecs.reshape(-1, LANES)
    time_rank = lax.axis_index("tm").astype(jnp.int32).reshape(1)
    space_rank = lax.axis_index("space").astype(jnp.int32).reshape(1)
    last_time, last_space = lax.axis_size("tm") - 1, lax.axis_size("space") - 1

    def prepare(tr, sr, *refs):
        prepare_kernel(tr, sr, last_time, last_space, *refs)

    links, source, behind_time, behind_space = call(
        prepare,
        [jax.ShapeDtypeStruct(links_in.shape, F32), vectors(12), vectors(12), vectors(12)],
        10**6,
        (time_rank, space_rank, boundary, dilution),
        noise,
        links_in,
    )
    sends = (source, behind_time, source, behind_space)
    solution = None
    for iteration in range(ITERS):
        at, bt, az, bz = exchange(*sends)
        if iteration == 0:
            local = call(local_first_kernel, vectors(48), 5 * 10**6, (), links, clover, source)
            modes = call(
                modes_kernel,
                jax.ShapeDtypeStruct((6, 256, 256), jnp.bfloat16),
                10**6,
                (),
                modes_in,
            )
        else:
            local = call(local_kernel, vectors(48), 5 * 10**6, (), solution, links, clover, source)
        if iteration < ITERS - 1:
            body = step_first_kernel if iteration == 0 else step_kernel
            solution, *sends = call(
                body,
                [vectors(48)] + [vectors(24)] * 4,
                3 * 10**6,
                (),
                local, links, at, bt, az, bz,
            )
        else:
            partial_sums = call(
                last_kernel,
                jax.ShapeDtypeStruct((32, 2 * count), F32),
                10**7,
                (),
                local, links, at, bt, az, bz, modes,
                scratch=[pltpu.VMEM((6, 32, 256), F32)],
            )
    return partial_sums


def shards(noise_field, gauge_links, clover, eigvecs, partner, dilution, boundary):
    count = eigvecs.shape[0]
    partial_sums = partial_rows(
        noise_field, gauge_links, clover, eigvecs, dilution, boundary
    )
    parts = lax.all_to_all(partial_sums, "space", 0, 0, tiled=True)
    row = call(sum_kernel, jax.ShapeDtypeStruct((1, 2 * count), F32), 10**4, (), parts)
    times = lax.axis_size("tm")
    rows = lax.all_to_all(jnp.broadcast_to(row, (times, 2 * count)), "tm", 0, 0, tiled=True)
    both = jnp.concatenate([partner, partner + count]).reshape(1, 2 * count)
    correlator = call(
        correlate_kernel, jax.ShapeDtypeStruct((1, times), F32), 10**5, (), row, rows, both
    )
    return row.reshape(1, 1, 2 * count), correlator.reshape(1, 1, times)


def solution(mesh):
    return jax.shard_map(
        shards,
        mesh=mesh,
        in_specs=(
            P(None, "tm", "space", None, None),
            P(None, None, "tm", "space", None, None),
            P(None, None, "tm", "space", None, None),
            P(None, "tm", "space", None, None),
            P(),
            P(),
            P(),
        ),
        out_specs=(P("space", "tm", None), P("space", "tm", None)),
        check_vma=False,
    )
```

time: 415 us -> 130 us (0.31)
  the two profiles are of different devices: /device:TPU:2 before, /device:TPU:1 now
where the time goes in v1:
time: 130 us; the launch traced here: 129 us
  starting transfers between devices  87.5 us (67%)
  waiting for transfers between devices  30.4 us (23%)
  Pallas kernels  5.61 us (4%)
  local copies, waits for them, and re-layouts  4.29 us (3%)
    ppermute x4, starting transfers between devices, exchange(): at = lax.ppermute(ahead_time, 'tm', ring('tm', -1))  33.8 us
    ppermute x4, starting transfers between devices, exchange(): az = lax.ppermute(ahead_space, 'space', ring('space', -1))  20.8 us
    all_to_all x1, waiting for transfers between devices, shards(): lax.all_to_all(jnp.broadcast_to(row, (times, 2 * count)), 'tm', 0, 0, til...  11.1 us
    all_to_all x1, starting transfers between devices, shards(): parts = lax.all_to_all(partial_sums, 'space', 0, 0, tiled=True)  9.57 us
    ppermute x4, starting transfers between devices, exchange(): bt = lax.ppermute(behind_time, 'tm', ring('tm', 1))  9.57 us
    ppermute x4, waiting for transfers between devices, exchange(): bt = lax.ppermute(behind_time, 'tm', ring('tm', 1))  9.46 us
    ppermute x4, starting transfers between devices, exchange(): bz = lax.ppermute(behind_space, 'space', ring('space', 1))  8.86 us
    all_to_all x1, waiting for transfers between devices, shards(): parts = lax.all_to_all(partial_sums, 'space', 0, 0, tiled=True)  7.83 us
  transfers between devices with their start and end apart: 18, of which 6 were waited for; matrix products, arithmetic and copies ran while one was open for 0% of the time, Pallas kernels for 2%

profile of v1, /device:TPU:1, one launch (start us, length us, event | category | flops | bytes accessed | tf_op | source)
XLA Modules:
  0.0 128.9 jit_solution(10100005743599723886)
XLA Ops:
  0.7 0.9 copy-done.2
  1.6 0.8 copy-done.3
  2.4 0.7 copy-done.5
  3.0 0.7 copy-done.6
  3.7 0.6 shard_map.86
  4.3 17.6 %collective-permute-start = (f32[12,8,128]{2,1,0:T(8,128)S(1)}, f32[12,8,128]{2,1,0:T(8,128)S(1)}, u32[]{:S(2)}, u32[]{:S(2)}) collective-permute-start(f32[12,8,128]{2,1,0:T(8,128)S(1)} %get-tuple-element.22.source), channel_id=1, source_target_pairs={{0,736},{32,0},{64,32},{96,64},{128,96},{160,128},{192,160},{224,1... | collective-permute-start | bytes 147464 | tf_op jit(solution)/shard_map/ppermute | solution.py:384
  21.9 2.9 %collective-permute-start.2 = (f32[12,8,128]{2,1,0:T(8,128)S(1)}, f32[12,8,128]{2,1,0:T(8,128)S(1)}, u32[]{:S(2)}, u32[]{:S(2)}) collective-permute-start(f32[12,8,128]{2,1,0:T(8,128)S(1)} %get-tuple-element.22.source), channel_id=1, source_target_pairs={{0,31},{1,0},{2,1},{3,2},{4,3},{5,4},{6,5},{7,6},{8,7},{9,8},{10,9... | collective-permute-start | bytes 147464 | tf_op jit(solution)/shard_map/ppermute | solution.py:382
  24.8 1.9 %collective-permute-start.1 = (f32[12,8,128]{2,1,0:T(8,128)S(1)}, f32[12,8,128]{2,1,0:T(8,128)S(1)}, u32[]{:S(2)}, u32[]{:S(2)}) collective-permute-start(f32[12,8,128]{2,1,0:T(8,128)S(1)} %get-tuple-element.23), channel_id=1, source_target_pairs={{0,32},{32,64},{64,96},{96,128},{128,160},{160,192},{192,224},{224... | collective-permute-start | bytes 147464 | tf_op jit(solution)/shard_map/ppermute | solution.py:385
  26.7 3.1 %collective-permute-start.3 = (f32[12,8,128]{2,1,0:T(8,128)S(1)}, f32[12,8,128]{2,1,0:T(8,128)S(1)}, u32[]{:S(2)}, u32[]{:S(2)}) collective-permute-start(f32[12,8,128]{2,1,0:T(8,128)S(1)} %get-tuple-element.24), channel_id=1, source_target_pairs={{0,1},{1,2},{2,3},{3,4},{4,5},{5,6},{6,7},{7,8},{8,9},{9,10},{10,1... | collective-permute-start | bytes 147464 | tf_op jit(solution)/shard_map/ppermute | solution.py:383
  29.8 0.4 shard_map.87.refs_0_
  30.2 0.0 collective-permute-done.refs_2_
  30.3 2.9 %collective-permute-done.1.refs_3_ = f32[12,8,128]{2,1,0:T(8,128)S(1)} collective-permute-done((f32[12,8,128]{2,1,0:T(8,128)S(1)}, f32[12,8,128]{2,1,0:T(8,128)S(1)}, u32[]{:S(2)}, u32[]{:S(2)}) %collective-permute-start.1) | collective-permute-done | bytes 49184 | tf_op jit(solution)/shard_map/ppermute | solution.py:385
  33.2 0.0 collective-permute-done.3.refs_5_
  33.2 0.2 shard_map.88
  33.4 6.0 %collective-permute-start.4 = (f32[24,8,128]{2,1,0:T(8,128)S(1)}, f32[24,8,128]{2,1,0:T(8,128)S(1)}, u32[]{:S(2)}, u32[]{:S(2)}) collective-permute-start(f32[24,8,128]{2,1,0:T(8,128)S(1)} %get-tuple-element.26), channel_id=1, source_target_pairs={{0,736},{32,0},{64,32},{96,64},{128,96},{160,128},{192,160},{224,1... | collective-permute-start | bytes 294920 | tf_op jit(solution)/shard_map/ppermute | solution.py:384
  39.5 1.9 %collective-permute-start.5 = (f32[24,8,128]{2,1,0:T(8,128)S(1)}, f32[24,8,128]{2,1,0:T(8,128)S(1)}, u32[]{:S(2)}, u32[]{:S(2)}) collective-permute-start(f32[24,8,128]{2,1,0:T(8,128)S(1)} %get-tuple-element.27), channel_id=1, source_target_pairs={{0,32},{32,64},{64,96},{96,128},{128,160},{160,192},{192,224},{224... | collective-permute-start | bytes 294920 | tf_op jit(solution)/shard_map/ppermute | solution.py:385
  41.4 7.1 %collective-permute-start.6 = (f32[24,8,128]{2,1,0:T(8,128)S(1)}, f32[24,8,128]{2,1,0:T(8,128)S(1)}, u32[]{:S(2)}, u32[]{:S(2)}) collective-permute-start(f32[24,8,128]{2,1,0:T(8,128)S(1)} %get-tuple-element.28), channel_id=1, source_target_pairs={{0,31},{1,0},{2,1},{3,2},{4,3},{5,4},{6,5},{7,6},{8,7},{9,8},{10,9... | collective-permute-start | bytes 294920 | tf_op jit(solution)/shard_map/ppermute | solution.py:382
  48.5 1.9 %collective-permute-start.7 = (f32[24,8,128]{2,1,0:T(8,128)S(1)}, f32[24,8,128]{2,1,0:T(8,128)S(1)}, u32[]{:S(2)}, u32[]{:S(2)}) collective-permute-start(f32[24,8,128]{2,1,0:T(8,128)S(1)} %get-tuple-element.29), channel_id=1, source_target_pairs={{0,1},{1,2},{2,3},{3,4},{4,5},{5,6},{6,7},{7,8},{8,9},{9,10},{10,1... | collective-permute-start | bytes 294920 | tf_op jit(solution)/shard_map/ppermute | solution.py:383
  50.4 0.5 shard_map.89.refs_0_
  50.9 0.0 collective-permute-done.5.refs_3_
  50.9 0.0 collective-permute-done.6.refs_4_
  50.9 1.1 collective-permute-done.7.refs_5_
  52.0 0.2 shard_map.90
  52.2 6.4 %collective-permute-start.10 = (f32[24,8,128]{2,1,0:T(8,128)S(1)}, f32[24,8,128]{2,1,0:T(8,128)S(1)}, u32[]{:S(2)}, u32[]{:S(2)}) collective-permute-start(f32[24,8,128]{2,1,0:T(8,128)S(1)} %get-tuple-element.33), channel_id=1, source_target_pairs={{0,31},{1,0},{2,1},{3,2},{4,3},{5,4},{6,5},{7,6},{8,7},{9,8},{10,9... | collective-permute-start | bytes 294920 | tf_op jit(solution)/shard_map/ppermute | solution.py:382
  58.7 1.9 %collective-permute-start.11 = (f32[24,8,128]{2,1,0:T(8,128)S(1)}, f32[24,8,128]{2,1,0:T(8,128)S(1)}, u32[]{:S(2)}, u32[]{:S(2)}) collective-permute-start(f32[24,8,128]{2,1,0:T(8,128)S(1)} %get-tuple-element.34), channel_id=1, source_target_pairs={{0,1},{1,2},{2,3},{3,4},{4,5},{5,6},{6,7},{7,8},{8,9},{9,10},{10,1... | collective-permute-start | bytes 294920 | tf_op jit(solution)/shard_map/ppermute | solution.py:383
  60.6 7.3 %collective-permute-start.8 = (f32[24,8,128]{2,1,0:T(8,128)S(1)}, f32[24,8,128]{2,1,0:T(8,128)S(1)}, u32[]{:S(2)}, u32[]{:S(2)}) collective-permute-start(f32[24,8,128]{2,1,0:T(8,128)S(1)} %get-tuple-element.31), channel_id=1, source_target_pairs={{0,736},{32,0},{64,32},{96,64},{128,96},{160,128},{192,160},{224,1... | collective-permute-start | bytes 294920 | tf_op jit(solution)/shard_map/ppermute | solution.py:384
  67.8 1.9 %collective-permute-start.9 = (f32[24,8,128]{2,1,0:T(8,128)S(1)}, f32[24,8,128]{2,1,0:T(8,128)S(1)}, u32[]{:S(2)}, u32[]{:S(2)}) collective-permute-start(f32[24,8,128]{2,1,0:T(8,128)S(1)} %get-tuple-element.32), channel_id=1, source_target_pairs={{0,32},{32,64},{64,96},{96,128},{128,160},{160,192},{192,224},{224... | collective-permute-start | bytes 294920 | tf_op jit(solution)/shard_map/ppermute | solution.py:385
  69.8 0.5 shard_map.91.refs_0_
  70.3 0.0 copy-start.1
  70.3 6.5 %collective-permute-done.9.refs_3_ = f32[24,8,128]{2,1,0:T(8,128)S(1)} collective-permute-done((f32[24,8,128]{2,1,0:T(8,128)S(1)}, f32[24,8,128]{2,1,0:T(8,128)S(1)}, u32[]{:S(2)}, u32[]{:S(2)}) %collective-permute-start.9) | collective-permute-done | bytes 98336 | tf_op jit(solution)/shard_map/ppermute | solution.py:385
  76.8 0.2 shard_map.92
  77.0 3.0 %collective-permute-start.12 = (f32[24,8,128]{2,1,0:T(8,128)S(1)}, f32[24,8,128]{2,1,0:T(8,128)S(1)}, u32[]{:S(2)}, u32[]{:S(2)}) collective-permute-start(f32[24,8,128]{2,1,0:T(8,128)S(1)} %get-tuple-element.36), channel_id=1, source_target_pairs={{0,736},{32,0},{64,32},{96,64},{128,96},{160,128},{192,160},{224,1... | collective-permute-start | bytes 294920 | tf_op jit(solution)/shard_map/ppermute | solution.py:384
  80.0 3.8 %collective-permute-start.13 = (f32[24,8,128]{2,1,0:T(8,128)S(1)}, f32[24,8,128]{2,1,0:T(8,128)S(1)}, u32[]{:S(2)}, u32[]{:S(2)}) collective-permute-start(f32[24,8,128]{2,1,0:T(8,128)S(1)} %get-tuple-element.37), channel_id=1, source_target_pairs={{0,32},{32,64},{64,96},{96,128},{128,160},{160,192},{192,224},{224... | collective-permute-start | bytes 294920 | tf_op jit(solution)/shard_map/ppermute | solution.py:385
  83.8 4.4 %collective-permute-start.14 = (f32[24,8,128]{2,1,0:T(8,128)S(1)}, f32[24,8,128]{2,1,0:T(8,128)S(1)}, u32[]{:S(2)}, u32[]{:S(2)}) collective-permute-start(f32[24,8,128]{2,1,0:T(8,128)S(1)} %get-tuple-element.38), channel_id=1, source_target_pairs={{0,31},{1,0},{2,1},{3,2},{4,3},{5,4},{6,5},{7,6},{8,7},{9,8},{10,9... | collective-permute-start | bytes 294920 | tf_op jit(solution)/shard_map/ppermute | solution.py:382
  88.2 1.9 %collective-permute-start.15 = (f32[24,8,128]{2,1,0:T(8,128)S(1)}, f32[24,8,128]{2,1,0:T(8,128)S(1)}, u32[]{:S(2)}, u32[]{:S(2)}) collective-permute-start(f32[24,8,128]{2,1,0:T(8,128)S(1)} %get-tuple-element.39), channel_id=1, source_target_pairs={{0,1},{1,2},{2,3},{3,4},{4,5},{5,6},{6,7},{7,8},{8,9},{9,10},{10,1... | collective-permute-start | bytes 294920 | tf_op jit(solution)/shard_map/ppermute | solution.py:383
  90.2 0.1 shard_map.94.modes
  90.3 0.5 shard_map.93.local
  90.8 1.0 collective-permute-done.15.bz
  91.8 1.0 shard_map.95
  92.8 9.6 %all-to-all-start = ((f32[32,1,96]{2,1,0:T(1,128)}), f32[32,1,96]{2,1,0:T(1,128)S(1)}, u32[]{:S(2)}, u32[]{:S(2)}) async-start(f32[32,1,96]{2,1,0:T(1,128)} %bitcast.7), calls=%async_computation | async-start | bytes 32768 | tf_op jit(solution)/shard_map/all_to_all | solution.py:451
  102.4 7.8 %all-to-all-done = f32[32,1,96]{2,1,0:T(1,128)S(1)} async-done(((f32[32,1,96]{2,1,0:T(1,128)}), f32[32,1,96]{2,1,0:T(1,128)S(1)}, u32[]{:S(2)}, u32[]{:S(2)}) %all-to-all-start) | async-done | bytes 12320 | tf_op jit(solution)/shard_map/all_to_all | solution.py:451
  110.2 0.5 shard_map.96.row
  110.7 0.7 copy-done.4
  111.4 0.6 broadcast_in_dim.2
  112.0 4.9 %all-to-all-start.1 = ((f32[24,1,96]{2,1,0:T(1,128)}), f32[24,1,96]{2,1,0:T(1,128)S(1)}, u32[]{:S(2)}, u32[]{:S(2)}) async-start(f32[24,1,96]{2,1,0:T(1,128)} %broadcast_in_dim.2), calls=%async_computation.1 | async-start | bytes 24576 | tf_op jit(solution)/shard_map/all_to_all | solution.py:454
  116.9 0.1 add_bitcast_fusion.partner
  116.9 11.1 %all-to-all-done.1 = f32[24,1,96]{2,1,0:T(1,128)S(1)} async-done(((f32[24,1,96]{2,1,0:T(1,128)}), f32[24,1,96]{2,1,0:T(1,128)S(1)}, u32[]{:S(2)}, u32[]{:S(2)}) %all-to-all-start.1) | async-done | bytes 9248 | tf_op jit(solution)/shard_map/all_to_all | solution.py:454
  128.0 0.9 shard_map.97
  (19 shorter events, 0.0 us)
Async XLA Ops:
  0.6 29.2 %copy-start = (f32[2,6,1,1,12,256]{5,3,4,2,1,0:T(1,128)S(1)}, f32[2,6,1,1,12,256]{5,3,4,2,1,0:T(1,128)}, u32[]{:S(2)}) copy-start(f32[2,6,1,1,12,256]{5,3,4,2,1,0:T(1,128)} %param.9) | copy-start | bytes 442372
  0.7 0.9 copy-start.2
  1.6 0.8 copy-start.3
  2.4 0.7 copy-start.5
  3.0 0.7 copy-start.6
  4.3 26.0 %collective-permute-start = (f32[12,8,128]{2,1,0:T(8,128)S(1)}, f32[12,8,128]{2,1,0:T(8,128)S(1)}, u32[]{:S(2)}, u32[]{:S(2)}) collective-permute-start(f32[12,8,128]{2,1,0:T(8,128)S(1)} %get-tuple-element.22.source), channel_id=1, source_target_pairs={{0,736},{32,0},{64,32},{96,64},{128,96},{160,128},{192,160},{224,1... | collective-permute-start | bytes 147464 | tf_op jit(solution)/shard_map/ppermute | solution.py:384
  21.9 8.4 %collective-permute-start.2 = (f32[12,8,128]{2,1,0:T(8,128)S(1)}, f32[12,8,128]{2,1,0:T(8,128)S(1)}, u32[]{:S(2)}, u32[]{:S(2)}) collective-permute-start(f32[12,8,128]{2,1,0:T(8,128)S(1)} %get-tuple-element.22.source), channel_id=1, source_target_pairs={{0,31},{1,0},{2,1},{3,2},{4,3},{5,4},{6,5},{7,6},{8,7},{9,8},{10,9... | collective-permute-start | bytes 147464 | tf_op jit(solution)/shard_map/ppermute | solution.py:382
  24.8 8.4 %collective-permute-start.1 = (f32[12,8,128]{2,1,0:T(8,128)S(1)}, f32[12,8,128]{2,1,0:T(8,128)S(1)}, u32[]{:S(2)}, u32[]{:S(2)}) collective-permute-start(f32[12,8,128]{2,1,0:T(8,128)S(1)} %get-tuple-element.23), channel_id=1, source_target_pairs={{0,32},{32,64},{64,96},{96,128},{128,160},{160,192},{192,224},{224... | collective-permute-start | bytes 147464 | tf_op jit(solution)/shard_map/ppermute | solution.py:385
  26.7 6.5 %collective-permute-start.3 = (f32[12,8,128]{2,1,0:T(8,128)S(1)}, f32[12,8,128]{2,1,0:T(8,128)S(1)}, u32[]{:S(2)}, u32[]{:S(2)}) collective-permute-start(f32[12,8,128]{2,1,0:T(8,128)S(1)} %get-tuple-element.24), channel_id=1, source_target_pairs={{0,1},{1,2},{2,3},{3,4},{4,5},{5,6},{6,7},{7,8},{8,9},{9,10},{10,1... | collective-permute-start | bytes 147464 | tf_op jit(solution)/shard_map/ppermute | solution.py:383
  33.4 17.4 %collective-permute-start.4 = (f32[24,8,128]{2,1,0:T(8,128)S(1)}, f32[24,8,128]{2,1,0:T(8,128)S(1)}, u32[]{:S(2)}, u32[]{:S(2)}) collective-permute-start(f32[24,8,128]{2,1,0:T(8,128)S(1)} %get-tuple-element.26), channel_id=1, source_target_pairs={{0,736},{32,0},{64,32},{96,64},{128,96},{160,128},{192,160},{224,1... | collective-permute-start | bytes 294920 | tf_op jit(solution)/shard_map/ppermute | solution.py:384
  39.5 11.4 %collective-permute-start.5 = (f32[24,8,128]{2,1,0:T(8,128)S(1)}, f32[24,8,128]{2,1,0:T(8,128)S(1)}, u32[]{:S(2)}, u32[]{:S(2)}) collective-permute-start(f32[24,8,128]{2,1,0:T(8,128)S(1)} %get-tuple-element.27), channel_id=1, source_target_pairs={{0,32},{32,64},{64,96},{96,128},{128,160},{160,192},{192,224},{224... | collective-permute-start | bytes 294920 | tf_op jit(solution)/shard_map/ppermute | solution.py:385
  41.4 9.5 %collective-permute-start.6 = (f32[24,8,128]{2,1,0:T(8,128)S(1)}, f32[24,8,128]{2,1,0:T(8,128)S(1)}, u32[]{:S(2)}, u32[]{:S(2)}) collective-permute-start(f32[24,8,128]{2,1,0:T(8,128)S(1)} %get-tuple-element.28), channel_id=1, source_target_pairs={{0,31},{1,0},{2,1},{3,2},{4,3},{5,4},{6,5},{7,6},{8,7},{9,8},{10,9... | collective-permute-start | bytes 294920 | tf_op jit(solution)/shard_map/ppermute | solution.py:382
  48.5 3.5 %collective-permute-start.7 = (f32[24,8,128]{2,1,0:T(8,128)S(1)}, f32[24,8,128]{2,1,0:T(8,128)S(1)}, u32[]{:S(2)}, u32[]{:S(2)}) collective-permute-start(f32[24,8,128]{2,1,0:T(8,128)S(1)} %get-tuple-element.29), channel_id=1, source_target_pairs={{0,1},{1,2},{2,3},{3,4},{4,5},{5,6},{6,7},{7,8},{8,9},{9,10},{10,1... | collective-permute-start | bytes 294920 | tf_op jit(solution)/shard_map/ppermute | solution.py:383
  52.2 18.0 %collective-permute-start.10 = (f32[24,8,128]{2,1,0:T(8,128)S(1)}, f32[24,8,128]{2,1,0:T(8,128)S(1)}, u32[]{:S(2)}, u32[]{:S(2)}) collective-permute-start(f32[24,8,128]{2,1,0:T(8,128)S(1)} %get-tuple-element.33), channel_id=1, source_target_pairs={{0,31},{1,0},{2,1},{3,2},{4,3},{5,4},{6,5},{7,6},{8,7},{9,8},{10,9... | collective-permute-start | bytes 294920 | tf_op jit(solution)/shard_map/ppermute | solution.py:382
  58.7 11.6 %collective-permute-start.11 = (f32[24,8,128]{2,1,0:T(8,128)S(1)}, f32[24,8,128]{2,1,0:T(8,128)S(1)}, u32[]{:S(2)}, u32[]{:S(2)}) collective-permute-start(f32[24,8,128]{2,1,0:T(8,128)S(1)} %get-tuple-element.34), channel_id=1, source_target_pairs={{0,1},{1,2},{2,3},{3,4},{4,5},{5,6},{6,7},{7,8},{8,9},{9,10},{10,1... | collective-permute-start | bytes 294920 | tf_op jit(solution)/shard_map/ppermute | solution.py:383
  60.6 9.7 %collective-permute-start.8 = (f32[24,8,128]{2,1,0:T(8,128)S(1)}, f32[24,8,128]{2,1,0:T(8,128)S(1)}, u32[]{:S(2)}, u32[]{:S(2)}) collective-permute-start(f32[24,8,128]{2,1,0:T(8,128)S(1)} %get-tuple-element.31), channel_id=1, source_target_pairs={{0,736},{32,0},{64,32},{96,64},{128,96},{160,128},{192,160},{224,1... | collective-permute-start | bytes 294920 | tf_op jit(solution)/shard_map/ppermute | solution.py:384
  67.8 9.0 %collective-permute-start.9 = (f32[24,8,128]{2,1,0:T(8,128)S(1)}, f32[24,8,128]{2,1,0:T(8,128)S(1)}, u32[]{:S(2)}, u32[]{:S(2)}) collective-permute-start(f32[24,8,128]{2,1,0:T(8,128)S(1)} %get-tuple-element.32), channel_id=1, source_target_pairs={{0,32},{32,64},{64,96},{96,128},{128,160},{160,192},{192,224},{224... | collective-permute-start | bytes 294920 | tf_op jit(solution)/shard_map/ppermute | solution.py:385
  70.3 19.9 %copy-start.1 = (f32[48,1,1,6,256]{4,2,3,1,0:T(1,128)S(1)}, f32[48,1,1,6,256]{4,2,3,1,0:T(1,128)}, u32[]{:S(2)}) copy-start(f32[48,1,1,6,256]{4,2,3,1,0:T(1,128)} %param.10) | copy-start | bytes 884740
  77.0 13.8 %collective-permute-start.12 = (f32[24,8,128]{2,1,0:T(8,128)S(1)}, f32[24,8,128]{2,1,0:T(8,128)S(1)}, u32[]{:S(2)}, u32[]{:S(2)}) collective-permute-start(f32[24,8,128]{2,1,0:T(8,128)S(1)} %get-tuple-element.36), channel_id=1, source_target_pairs={{0,736},{32,0},{64,32},{96,64},{128,96},{160,128},{192,160},{224,1... | collective-permute-start | bytes 294920 | tf_op jit(solution)/shard_map/ppermute | solution.py:384
  80.0 10.8 %collective-permute-start.13 = (f32[24,8,128]{2,1,0:T(8,128)S(1)}, f32[24,8,128]{2,1,0:T(8,128)S(1)}, u32[]{:S(2)}, u32[]{:S(2)}) collective-permute-start(f32[24,8,128]{2,1,0:T(8,128)S(1)} %get-tuple-element.37), channel_id=1, source_target_pairs={{0,32},{32,64},{64,96},{96,128},{128,160},{160,192},{192,224},{224... | collective-permute-start | bytes 294920 | tf_op jit(solution)/shard_map/ppermute | solution.py:385
  83.8 7.0 %collective-permute-start.14 = (f32[24,8,128]{2,1,0:T(8,128)S(1)}, f32[24,8,128]{2,1,0:T(8,128)S(1)}, u32[]{:S(2)}, u32[]{:S(2)}) collective-permute-start(f32[24,8,128]{2,1,0:T(8,128)S(1)} %get-tuple-element.38), channel_id=1, source_target_pairs={{0,31},{1,0},{2,1},{3,2},{4,3},{5,4},{6,5},{7,6},{8,7},{9,8},{10,9... | collective-permute-start | bytes 294920 | tf_op jit(solution)/shard_map/ppermute | solution.py:382
  88.2 3.5 %collective-permute-start.15 = (f32[24,8,128]{2,1,0:T(8,128)S(1)}, f32[24,8,128]{2,1,0:T(8,128)S(1)}, u32[]{:S(2)}, u32[]{:S(2)}) collective-permute-start(f32[24,8,128]{2,1,0:T(8,128)S(1)} %get-tuple-element.39), channel_id=1, source_target_pairs={{0,1},{1,2},{2,3},{3,4},{4,5},{5,6},{6,7},{7,8},{8,9},{9,10},{10,1... | collective-permute-start | bytes 294920 | tf_op jit(solution)/shard_map/ppermute | solution.py:383
  92.8 9.6 %copy-start.7 = (s32[48]{0:T(128)S(1)}, s32[48]{0:T(128)}, u32[]{:S(2)}) copy-start(s32[48]{0:T(128)} %param.11) | copy-start | bytes 580
  92.8 17.4 %all-to-all-start = ((f32[32,1,96]{2,1,0:T(1,128)}), f32[32,1,96]{2,1,0:T(1,128)S(1)}, u32[]{:S(2)}, u32[]{:S(2)}) async-start(f32[32,1,96]{2,1,0:T(1,128)} %bitcast.7), calls=%async_computation | async-start | bytes 32768 | tf_op jit(solution)/shard_map/all_to_all | solution.py:451
  110.7 0.7 copy-start.4
  112.0 16.0 %all-to-all-start.1 = ((f32[24,1,96]{2,1,0:T(1,128)}), f32[24,1,96]{2,1,0:T(1,128)S(1)}, u32[]{:S(2)}, u32[]{:S(2)}) async-start(f32[24,1,96]{2,1,0:T(1,128)} %broadcast_in_dim.2), calls=%async_computation.1 | async-start | bytes 24576 | tf_op jit(solution)/shard_map/all_to_all | solution.py:454

commit v2 on v1

--- a/solution.py
+++ b/solution.py
@@ -105,11 +105,31 @@
     return source_rows((8, LANES)) % 4 == spin
 
 
-def prepare_kernel(time_rank, space_rank, last_time, last_space, bounds, dilution, noise, links_in,
-                   links, source, behind_time, behind_space):
+class Pick:
+    def __init__(self, first, here, there):
+        self.first, self.here, self.there = first, here, there
+
+    def __getitem__(self, index):
+        return jnp.where(self.first, self.here[index], self.there[index])
+
+
+def is_even(rank):
+    return jnp.full((8, LANES), rank[0], jnp.int32) % 2 == 0
+
+
+def store_sends(inner, outer, even, comp, half, behind, ahead):
+    for c in range(3):
+        for p in range(2):
+            up, down = behind[c][p], ahead[c][p]
+            inner[spinor_at(comp, c, p, half)] = jnp.where(even, up, down)
+            outer[spinor_at(comp, c, p, half)] = jnp.where(even, down, up)
+
+
+def prepare_kernel(last_time, last_space, time_rank, space_rank, bits, noise, links_in,
+                   links, source, t_inner, t_outer, z_inner, z_outer):
     lane = lax.broadcasted_iota(jnp.int32, (8, LANES), 1)
     row = lax.broadcasted_iota(jnp.int32, (8, LANES), 0)
-    phases = [(1 - 2 * bounds[mu]).astype(F32) * (0.5 * step_size) for mu in range(4)]
+    phases = [(1 - 2 * bits[mu]).astype(F32) * (0.5 * step_size) for mu in range(4)]
     plain = 0.5 * step_size
     at_x = jnp.where(lane % SIDE == SIDE - 1, phases[0], plain)
     at_y = jnp.where((lane >= LANES - SIDE) & (row % 2 == 1), phases[1], plain)
@@ -124,7 +144,7 @@
         links[block * 8 : block * 8 + 8, :] = links_in[block * 8 : block * 8 + 8, :] * scale
     weight = jnp.zeros((8, LANES), F32)
     for j in range(8):
-        on = jnp.where(time_rank[0] % DILUTE == dilution[j], step_size, 0.0)
+        on = jnp.where(time_rank[0] % DILUTE == bits[4 + j], step_size, 0.0)
         weight = jnp.where(row == j, on, weight)
     for half in range(2):
         vector = []
@@ -136,9 +156,12 @@
                 source[plane] = value
                 pair.append(value)
             vector.append(tuple(pair))
-        for mu, out in ((3, behind_time), (2, behind_space)):
+        for mu, rank, inner, outer in (
+            (3, time_rank, t_inner, t_outer),
+            (2, space_rank, z_inner, z_outer),
+        ):
             moved = link_times(links, mu, half, vector, True)
-            store_spin(out, 0, half, moved)
+            store_sends(inner, outer, is_even(rank), 0, half, moved, vector)
 
 
 def shift_x(value, forward):
@@ -266,17 +289,32 @@
     return load
 
 
-def step_body(kind, local, links, at, bt, az, bz, solution, sat, sbt, saz, sbz):
-    received = ((3, kind(at), kind(bt)), (2, kind(az), kind(bz)))
+def arrivals(kind, time_rank, space_rank, t_inner, t_outer, z_inner, z_outer):
+    received = []
+    for mu, rank, inner, outer in (
+        (3, time_rank, t_inner, t_outer),
+        (2, space_rank, z_inner, z_outer),
+    ):
+        even = is_even(rank)
+        received.append((mu, kind(Pick(even, inner, outer)), kind(Pick(even, outer, inner))))
+    return received
+
+
+def step_body(kind, time_rank, space_rank, local, links, ti, to, zi, zo, solution, *sends):
+    received = arrivals(kind, time_rank, space_rank, ti, to, zi, zo)
     for comp in range(2):
         for half in range(2):
             top, bottom = hops(local, links, received, comp, half)
             store_spin(solution, comp, half, top)
             store_spin(solution, 2 + comp, half, bottom)
-            for mu, ahead, behind in ((3, sat, sbt), (2, saz, sbz)):
-                store_spin(ahead, comp, half, half_spin(mu, comp, -1, top, bottom))
+            for mu, rank, inner, outer in (
+                (3, time_rank, *sends[:2]),
+                (2, space_rank, *sends[2:]),
+            ):
+                ahead = half_spin(mu, comp, -1, top, bottom)
                 plus = half_spin(mu, comp, 1, top, bottom)
-                store_spin(behind, comp, half, link_times(links, mu, half, plus, True))
+                behind = link_times(links, mu, half, plus, True)
+                store_sends(inner, outer, is_even(rank), comp, half, behind, ahead)
 
 
 def step_first_kernel(*refs):
@@ -303,11 +341,8 @@
                     out[2 * c + p, 128 + start : 128 + start + count, lanes] = low
 
 
-def last_kernel(local, links, at, bt, az, bz, modes, out, rows):
-    received = (
-        (3, from_halves(at), from_halves(bt)),
-        (2, from_halves(az), from_halves(bz)),
-    )
+def last_kernel(time_rank, space_rank, local, links, ti, to, zi, zo, modes, out, rows):
+    received = arrivals(from_halves, time_rank, space_rank, ti, to, zi, zo)
     for comp in range(2):
         for half in range(2):
             pair = hops(local, links, received, comp, half)
@@ -332,8 +367,10 @@
         out[pl.ds(spin, 8, stride=4), :] = total[8 * spin : 8 * spin + 8, : out.shape[1]]
 
 
-def sum_kernel(parts, out):
-    out[...] = jnp.sum(parts[...], axis=0, keepdims=True)
+def sum_kernel(parts, out, copies):
+    total = jnp.sum(parts[...], axis=0, keepdims=True)
+    out[...] = total
+    copies[...] = jnp.broadcast_to(total, copies.shape)
 
 
 def correlate_kernel(row, rows, partner, out):
@@ -374,16 +411,17 @@
     return jax.ShapeDtypeStruct((count, 8, LANES), F32)
 
 
-def exchange(ahead_time, behind_time, ahead_space, behind_space):
-    def ring(axis, step):
+def exchange(t_inner, t_outer, z_inner, z_outer):
+    def swap(axis, shift):
         size = lax.axis_size(axis)
-        return [(i, (i + step) % size) for i in range(size)]
-
-    az = lax.ppermute(ahead_space, "space", ring("space", -1))
-    bz = lax.ppermute(behind_space, "space", ring("space", 1))
-    at = lax.ppermute(ahead_time, "tm", ring("tm", -1))
-    bt = lax.ppermute(behind_time, "tm", ring("tm", 1))
-    return at, bt, az, bz
+        pairs = [((i + shift) % size, (i + 1 + shift) % size) for i in range(0, size, 2)]
+        return pairs + [(j, i) for i, j in pairs]
+
+    zi = lax.ppermute(z_inner, "space", swap("space", 0))
+    zo = lax.ppermute(z_outer, "space", swap("space", 1))
+    ti = lax.ppermute(t_inner, "tm", swap("tm", 0))
+    to = lax.ppermute(t_outer, "tm", swap("tm", 1))
+    return ti, to, zi, zo
 
 
 def partial_rows(noise_field, gauge_links, clover, eigvecs, dilution, boundary):
@@ -396,21 +434,22 @@
     space_rank = lax.axis_index("space").astype(jnp.int32).reshape(1)
     last_time, last_space = lax.axis_size("tm") - 1, lax.axis_size("space") - 1
 
-    def prepare(tr, sr, *refs):
-        prepare_kernel(tr, sr, last_time, last_space, *refs)
-
-    links, source, behind_time, behind_space = call(
+    ranks = (time_rank, space_rank)
+
+    def prepare(*refs):
+        prepare_kernel(last_time, last_space, *refs)
+
+    links, source, *sends = call(
         prepare,
-        [jax.ShapeDtypeStruct(links_in.shape, F32), vectors(12), vectors(12), vectors(12)],
+        [jax.ShapeDtypeStruct(links_in.shape, F32)] + [vectors(12)] * 5,
         10**6,
-        (time_rank, space_rank, boundary, dilution),
+        (*ranks, jnp.concatenate([boundary, dilution])),
         noise,
         links_in,
     )
-    sends = (source, behind_time, source, behind_space)
     solution = None
     for iteration in range(ITERS):
-        at, bt, az, bz = exchange(*sends)
+        arrived = exchange(*sends)
         if iteration == 0:
             local = call(local_first_kernel, vectors(48), 5 * 10**6, (), links, clover, source)
             modes = call(
@@ -428,16 +467,16 @@
                 body,
                 [vectors(48)] + [vectors(24)] * 4,
                 3 * 10**6,
-                (),
-                local, links, at, bt, az, bz,
+                ranks,
+                local, links, *arrived,
             )
         else:
             partial_sums = call(
                 last_kernel,
                 jax.ShapeDtypeStruct((32, 2 * count), F32),
                 10**7,
-                (),
-                local, links, at, bt, az, bz, modes,
+                ranks,
+                local, links, *arrived, modes,
                 scratch=[pltpu.VMEM((6, 32, 256), F32)],
             )
     return partial_sums
@@ -449,9 +488,15 @@
         noise_field, gauge_links, clover, eigvecs, dilution, boundary
     )
     parts = lax.all_to_all(partial_sums, "space", 0, 0, tiled=True)
-    row = call(sum_kernel, jax.ShapeDtypeStruct((1, 2 * count), F32), 10**4, (), parts)
     times = lax.axis_size("tm")
-    rows = lax.all_to_all(jnp.broadcast_to(row, (times, 2 * count)), "tm", 0, 0, tiled=True)
+    row, copies = call(
+        sum_kernel,
+        [jax.ShapeDtypeStruct((n, 2 * count), F32) for n in (1, times)],
+        10**4,
+        (),
+        parts,
+    )
+    rows = lax.all_to_all(copies, "tm", 0, 0, tiled=True)
     both = jnp.concatenate([partner, partner + count]).reshape(1, 2 * count)
     correlator = call(
         correlate_kernel, jax.ShapeDtypeStruct((1, times), F32), 10**5, (), row, rows, both

time: 130 us -> 124 us (0.954)
  starting transfers between devices: 87.5 us -> 81.8 us
  local copies, waits for them, and re-layouts: 4.29 us -> 2.35 us
    all_to_all x1, starting transfers between devices: 9.57 us -> 5.71 us  [shards(): parts = lax.all_to_all(partial_sums, 'space', 0, 0, tiled=True)]
    ppermute x16, starting transfers between devices: 73 us -> 70 us  [the longest x4 28.1 us: exchange(): to = lax.ppermute(t_outer, 'tm', swap('tm', 1))]
    unnamed x16 -> x12, local copies, waits for them, and re-layouts: 3.69 us -> 2.35 us
where the time goes in v2:
time: 124 us; the launch traced here: 123 us
  starting transfers between devices  81.8 us (66%)
  waiting for transfers between devices  31.4 us (25%)
  Pallas kernels  5.71 us (5%)
  local copies, waits for them, and re-layouts  2.35 us (2%)
    ppermute x4, starting transfers between devices, exchange(): to = lax.ppermute(t_outer, 'tm', swap('tm', 1))  28.1 us
    ppermute x4, starting transfers between devices, exchange(): zi = lax.ppermute(z_inner, 'space', swap('space', 0))  20.2 us
    ppermute x4, starting transfers between devices, exchange(): ti = lax.ppermute(t_inner, 'tm', swap('tm', 0))  12.9 us
    all_to_all x1, waiting for transfers between devices, shards(): rows = lax.all_to_all(copies, 'tm', 0, 0, tiled=True)  11 us
    ppermute x4, starting transfers between devices, exchange(): zo = lax.ppermute(z_outer, 'space', swap('space', 1))  8.86 us
    ppermute x4, waiting for transfers between devices, exchange(): zo = lax.ppermute(z_outer, 'space', swap('space', 1))  8.74 us
    all_to_all x1, waiting for transfers between devices, shards(): parts = lax.all_to_all(partial_sums, 'space', 0, 0, tiled=True)  7.96 us
    all_to_all x1, starting transfers between devices, shards(): rows = lax.all_to_all(copies, 'tm', 0, 0, tiled=True)  6.09 us
  transfers between devices with their start and end apart: 18, of which 6 were waited for; matrix products, arithmetic and copies ran while one was open for 0% of the time, Pallas kernels for 2%

profile of v2, /device:TPU:1, one launch (start us, length us, event | category | flops | bytes accessed | tf_op | source)
XLA Modules:
  0.0 123.1 jit_solution(12905826330920514809)
XLA Ops:
  0.7 0.8 pad_add_fusion.refs_2_
  1.4 0.9 copy-done.2
  2.3 0.8 copy-done.3
  3.1 0.6 shard_map.86
  3.7 5.5 %collective-permute-start = (f32[12,8,128]{2,1,0:T(8,128)S(1)}, f32[12,8,128]{2,1,0:T(8,128)S(1)}, u32[]{:S(2)}, u32[]{:S(2)}) collective-permute-start(f32[12,8,128]{2,1,0:T(8,128)S(1)} %get-tuple-element.27), channel_id=1, source_target_pairs={{0,32},{64,96},{128,160},{192,224},{256,288},{320,352},{384,416},{... | collective-permute-start | bytes 147464 | tf_op jit(solution)/shard_map/ppermute | solution.py:422
  9.2 14.2 %collective-permute-start.1 = (f32[12,8,128]{2,1,0:T(8,128)S(1)}, f32[12,8,128]{2,1,0:T(8,128)S(1)}, u32[]{:S(2)}, u32[]{:S(2)}) collective-permute-start(f32[12,8,128]{2,1,0:T(8,128)S(1)} %get-tuple-element.28), channel_id=1, source_target_pairs={{32,64},{96,128},{160,192},{224,256},{288,320},{352,384},{416,448}... | collective-permute-start | bytes 147464 | tf_op jit(solution)/shard_map/ppermute | solution.py:423
  23.5 3.1 %collective-permute-start.2 = (f32[12,8,128]{2,1,0:T(8,128)S(1)}, f32[12,8,128]{2,1,0:T(8,128)S(1)}, u32[]{:S(2)}, u32[]{:S(2)}) collective-permute-start(f32[12,8,128]{2,1,0:T(8,128)S(1)} %get-tuple-element.29), channel_id=1, source_target_pairs={{0,1},{2,3},{4,5},{6,7},{8,9},{10,11},{12,13},{14,15},{16,17},{18,... | collective-permute-start | bytes 147464 | tf_op jit(solution)/shard_map/ppermute | solution.py:420
  26.6 3.1 %collective-permute-start.3 = (f32[12,8,128]{2,1,0:T(8,128)S(1)}, f32[12,8,128]{2,1,0:T(8,128)S(1)}, u32[]{:S(2)}, u32[]{:S(2)}) collective-permute-start(f32[12,8,128]{2,1,0:T(8,128)S(1)} %get-tuple-element.30), channel_id=1, source_target_pairs={{1,2},{3,4},{5,6},{7,8},{9,10},{11,12},{13,14},{15,16},{17,18},{19... | collective-permute-start | bytes 147464 | tf_op jit(solution)/shard_map/ppermute | solution.py:421
  29.7 0.4 shard_map.87.refs_2_
  30.2 0.0 collective-permute-done.1.refs_5_
  30.2 0.0 collective-permute-done.2.refs_6_
  30.2 1.8 %collective-permute-done.3.refs_7_ = f32[12,8,128]{2,1,0:T(8,128)S(1)} collective-permute-done((f32[12,8,128]{2,1,0:T(8,128)S(1)}, f32[12,8,128]{2,1,0:T(8,128)S(1)}, u32[]{:S(2)}, u32[]{:S(2)}) %collective-permute-start.3) | collective-permute-done | bytes 49184 | tf_op jit(solution)/shard_map/ppermute | solution.py:421
  32.0 0.3 shard_map.88
  32.3 1.9 %collective-permute-start.4 = (f32[24,8,128]{2,1,0:T(8,128)S(1)}, f32[24,8,128]{2,1,0:T(8,128)S(1)}, u32[]{:S(2)}, u32[]{:S(2)}) collective-permute-start(f32[24,8,128]{2,1,0:T(8,128)S(1)} %get-tuple-element.32), channel_id=1, source_target_pairs={{0,32},{64,96},{128,160},{192,224},{256,288},{320,352},{384,416},{... | collective-permute-start | bytes 294920 | tf_op jit(solution)/shard_map/ppermute | solution.py:422
  34.2 4.9 %collective-permute-start.5 = (f32[24,8,128]{2,1,0:T(8,128)S(1)}, f32[24,8,128]{2,1,0:T(8,128)S(1)}, u32[]{:S(2)}, u32[]{:S(2)}) collective-permute-start(f32[24,8,128]{2,1,0:T(8,128)S(1)} %get-tuple-element.33), channel_id=1, source_target_pairs={{32,64},{96,128},{160,192},{224,256},{288,320},{352,384},{416,448}... | collective-permute-start | bytes 294920 | tf_op jit(solution)/shard_map/ppermute | solution.py:423
  39.1 5.2 %collective-permute-start.6 = (f32[24,8,128]{2,1,0:T(8,128)S(1)}, f32[24,8,128]{2,1,0:T(8,128)S(1)}, u32[]{:S(2)}, u32[]{:S(2)}) collective-permute-start(f32[24,8,128]{2,1,0:T(8,128)S(1)} %get-tuple-element.34), channel_id=1, source_target_pairs={{0,1},{2,3},{4,5},{6,7},{8,9},{10,11},{12,13},{14,15},{16,17},{18,... | collective-permute-start | bytes 294920 | tf_op jit(solution)/shard_map/ppermute | solution.py:420
  44.3 1.9 %collective-permute-start.7 = (f32[24,8,128]{2,1,0:T(8,128)S(1)}, f32[24,8,128]{2,1,0:T(8,128)S(1)}, u32[]{:S(2)}, u32[]{:S(2)}) collective-permute-start(f32[24,8,128]{2,1,0:T(8,128)S(1)} %get-tuple-element.35), channel_id=1, source_target_pairs={{1,2},{3,4},{5,6},{7,8},{9,10},{11,12},{13,14},{15,16},{17,18},{19... | collective-permute-start | bytes 294920 | tf_op jit(solution)/shard_map/ppermute | solution.py:421
  46.3 0.4 shard_map.89.refs_2_
  46.7 0.0 collective-permute-done.6.refs_6_
  46.7 3.5 %collective-permute-done.7.refs_7_ = f32[24,8,128]{2,1,0:T(8,128)S(1)} collective-permute-done((f32[24,8,128]{2,1,0:T(8,128)S(1)}, f32[24,8,128]{2,1,0:T(8,128)S(1)}, u32[]{:S(2)}, u32[]{:S(2)}) %collective-permute-start.7) | collective-permute-done | bytes 98336 | tf_op jit(solution)/shard_map/ppermute | solution.py:421
  50.3 0.2 shard_map.90
  50.5 4.0 %collective-permute-start.10 = (f32[24,8,128]{2,1,0:T(8,128)S(1)}, f32[24,8,128]{2,1,0:T(8,128)S(1)}, u32[]{:S(2)}, u32[]{:S(2)}) collective-permute-start(f32[24,8,128]{2,1,0:T(8,128)S(1)} %get-tuple-element.39), channel_id=1, source_target_pairs={{0,1},{2,3},{4,5},{6,7},{8,9},{10,11},{12,13},{14,15},{16,17},{18,... | collective-permute-start | bytes 294920 | tf_op jit(solution)/shard_map/ppermute | solution.py:420
  54.5 1.9 %collective-permute-start.11 = (f32[24,8,128]{2,1,0:T(8,128)S(1)}, f32[24,8,128]{2,1,0:T(8,128)S(1)}, u32[]{:S(2)}, u32[]{:S(2)}) collective-permute-start(f32[24,8,128]{2,1,0:T(8,128)S(1)} %get-tuple-element.40), channel_id=1, source_target_pairs={{1,2},{3,4},{5,6},{7,8},{9,10},{11,12},{13,14},{15,16},{17,18},{19... | collective-permute-start | bytes 294920 | tf_op jit(solution)/shard_map/ppermute | solution.py:421
  56.5 2.0 %collective-permute-start.8 = (f32[24,8,128]{2,1,0:T(8,128)S(1)}, f32[24,8,128]{2,1,0:T(8,128)S(1)}, u32[]{:S(2)}, u32[]{:S(2)}) collective-permute-start(f32[24,8,128]{2,1,0:T(8,128)S(1)} %get-tuple-element.37), channel_id=1, source_target_pairs={{0,32},{64,96},{128,160},{192,224},{256,288},{320,352},{384,416},{... | collective-permute-start | bytes 294920 | tf_op jit(solution)/shard_map/ppermute | solution.py:422
  58.5 4.9 %collective-permute-start.9 = (f32[24,8,128]{2,1,0:T(8,128)S(1)}, f32[24,8,128]{2,1,0:T(8,128)S(1)}, u32[]{:S(2)}, u32[]{:S(2)}) collective-permute-start(f32[24,8,128]{2,1,0:T(8,128)S(1)} %get-tuple-element.38), channel_id=1, source_target_pairs={{32,64},{96,128},{160,192},{224,256},{288,320},{352,384},{416,448}... | collective-permute-start | bytes 294920 | tf_op jit(solution)/shard_map/ppermute | solution.py:423
  63.4 0.4 shard_map.91.refs_2_
  63.8 0.0 copy-start.1
  63.9 0.0 collective-permute-done.10.refs_6_
  63.9 0.0 collective-permute-done.11.refs_7_
  63.9 3.6 %collective-permute-done.9.refs_5_ = f32[24,8,128]{2,1,0:T(8,128)S(1)} collective-permute-done((f32[24,8,128]{2,1,0:T(8,128)S(1)}, f32[24,8,128]{2,1,0:T(8,128)S(1)}, u32[]{:S(2)}, u32[]{:S(2)}) %collective-permute-start.9) | collective-permute-done | bytes 98336 | tf_op jit(solution)/shard_map/ppermute | solution.py:423
  67.5 0.2 shard_map.92
  67.8 3.5 %collective-permute-start.12 = (f32[24,8,128]{2,1,0:T(8,128)S(1)}, f32[24,8,128]{2,1,0:T(8,128)S(1)}, u32[]{:S(2)}, u32[]{:S(2)}) collective-permute-start(f32[24,8,128]{2,1,0:T(8,128)S(1)} %get-tuple-element.42), channel_id=1, source_target_pairs={{0,32},{64,96},{128,160},{192,224},{256,288},{320,352},{384,416},{... | collective-permute-start | bytes 294920 | tf_op jit(solution)/shard_map/ppermute | solution.py:422
  71.3 4.1 %collective-permute-start.13 = (f32[24,8,128]{2,1,0:T(8,128)S(1)}, f32[24,8,128]{2,1,0:T(8,128)S(1)}, u32[]{:S(2)}, u32[]{:S(2)}) collective-permute-start(f32[24,8,128]{2,1,0:T(8,128)S(1)} %get-tuple-element.43), channel_id=1, source_target_pairs={{32,64},{96,128},{160,192},{224,256},{288,320},{352,384},{416,448}... | collective-permute-start | bytes 294920 | tf_op jit(solution)/shard_map/ppermute | solution.py:423
  75.4 7.7 %collective-permute-start.14 = (f32[24,8,128]{2,1,0:T(8,128)S(1)}, f32[24,8,128]{2,1,0:T(8,128)S(1)}, u32[]{:S(2)}, u32[]{:S(2)}) collective-permute-start(f32[24,8,128]{2,1,0:T(8,128)S(1)} %get-tuple-element.44), channel_id=1, source_target_pairs={{0,1},{2,3},{4,5},{6,7},{8,9},{10,11},{12,13},{14,15},{16,17},{18,... | collective-permute-start | bytes 294920 | tf_op jit(solution)/shard_map/ppermute | solution.py:420
  83.1 1.9 %collective-permute-start.15 = (f32[24,8,128]{2,1,0:T(8,128)S(1)}, f32[24,8,128]{2,1,0:T(8,128)S(1)}, u32[]{:S(2)}, u32[]{:S(2)}) collective-permute-start(f32[24,8,128]{2,1,0:T(8,128)S(1)} %get-tuple-element.45), channel_id=1, source_target_pairs={{1,2},{3,4},{5,6},{7,8},{9,10},{11,12},{13,14},{15,16},{17,18},{19... | collective-permute-start | bytes 294920 | tf_op jit(solution)/shard_map/ppermute | solution.py:421
  85.1 0.1 shard_map.94.modes
  85.2 0.4 shard_map.93.local
  85.7 0.0 collective-permute-done.13.to
  85.7 3.4 %collective-permute-done.15.zo = f32[24,8,128]{2,1,0:T(8,128)S(1)} collective-permute-done((f32[24,8,128]{2,1,0:T(8,128)S(1)}, f32[24,8,128]{2,1,0:T(8,128)S(1)}, u32[]{:S(2)}, u32[]{:S(2)}) %collective-permute-start.15) | collective-permute-done | bytes 98336 | tf_op jit(solution)/shard_map/ppermute | solution.py:421
  89.1 1.0 shard_map.95
  90.1 5.7 %all-to-all-start = ((f32[32,1,96]{2,1,0:T(1,128)}), f32[32,1,96]{2,1,0:T(1,128)S(1)}, u32[]{:S(2)}, u32[]{:S(2)}) async-start(f32[32,1,96]{2,1,0:T(1,128)} %bitcast.7), calls=%async_computation | async-start | bytes 32768 | tf_op jit(solution)/shard_map/all_to_all | solution.py:490
  95.8 8.0 %all-to-all-done = f32[32,1,96]{2,1,0:T(1,128)S(1)} async-done(((f32[32,1,96]{2,1,0:T(1,128)}), f32[32,1,96]{2,1,0:T(1,128)S(1)}, u32[]{:S(2)}, u32[]{:S(2)}) %all-to-all-start) | async-done | bytes 12320 | tf_op jit(solution)/shard_map/all_to_all | solution.py:490
  103.8 0.6 shard_map.96
  104.4 6.1 %all-to-all-start.1 = ((f32[24,1,96]{2,1,0:T(1,128)}), f32[24,1,96]{2,1,0:T(1,128)S(1)}, u32[]{:S(2)}, u32[]{:S(2)}) async-start(f32[24,1,96]{2,1,0:T(1,128)} %bitcast.11), calls=%async_computation.1 | async-start | bytes 24576 | tf_op jit(solution)/shard_map/all_to_all | solution.py:499
  110.5 0.1 add_bitcast_fusion.partner
  110.6 11.0 %all-to-all-done.1 = f32[24,1,96]{2,1,0:T(1,128)S(1)} async-done(((f32[24,1,96]{2,1,0:T(1,128)}), f32[24,1,96]{2,1,0:T(1,128)S(1)}, u32[]{:S(2)}, u32[]{:S(2)}) %all-to-all-start.1) | async-done | bytes 9248 | tf_op jit(solution)/shard_map/all_to_all | solution.py:499
  121.6 0.7 copy-done.4
  122.3 0.9 shard_map.97
  (15 shorter events, 0.0 us)
Async XLA Ops:
  0.6 29.1 %copy-start = (f32[2,6,1,1,12,256]{5,3,4,2,1,0:T(1,128)S(1)}, f32[2,6,1,1,12,256]{5,3,4,2,1,0:T(1,128)}, u32[]{:S(2)}) copy-start(f32[2,6,1,1,12,256]{5,3,4,2,1,0:T(1,128)} %param.9) | copy-start | bytes 442372
  1.4 0.9 copy-start.2
  2.3 0.8 copy-start.3
  3.7 26.4 %collective-permute-start = (f32[12,8,128]{2,1,0:T(8,128)S(1)}, f32[12,8,128]{2,1,0:T(8,128)S(1)}, u32[]{:S(2)}, u32[]{:S(2)}) collective-permute-start(f32[12,8,128]{2,1,0:T(8,128)S(1)} %get-tuple-element.27), channel_id=1, source_target_pairs={{0,32},{64,96},{128,160},{192,224},{256,288},{320,352},{384,416},{... | collective-permute-start | bytes 147464 | tf_op jit(solution)/shard_map/ppermute | solution.py:422
  9.2 21.0 %collective-permute-start.1 = (f32[12,8,128]{2,1,0:T(8,128)S(1)}, f32[12,8,128]{2,1,0:T(8,128)S(1)}, u32[]{:S(2)}, u32[]{:S(2)}) collective-permute-start(f32[12,8,128]{2,1,0:T(8,128)S(1)} %get-tuple-element.28), channel_id=1, source_target_pairs={{32,64},{96,128},{160,192},{224,256},{288,320},{352,384},{416,448}... | collective-permute-start | bytes 147464 | tf_op jit(solution)/shard_map/ppermute | solution.py:423
  23.5 6.7 %collective-permute-start.2 = (f32[12,8,128]{2,1,0:T(8,128)S(1)}, f32[12,8,128]{2,1,0:T(8,128)S(1)}, u32[]{:S(2)}, u32[]{:S(2)}) collective-permute-start(f32[12,8,128]{2,1,0:T(8,128)S(1)} %get-tuple-element.29), channel_id=1, source_target_pairs={{0,1},{2,3},{4,5},{6,7},{8,9},{10,11},{12,13},{14,15},{16,17},{18,... | collective-permute-start | bytes 147464 | tf_op jit(solution)/shard_map/ppermute | solution.py:420
  26.6 5.4 %collective-permute-start.3 = (f32[12,8,128]{2,1,0:T(8,128)S(1)}, f32[12,8,128]{2,1,0:T(8,128)S(1)}, u32[]{:S(2)}, u32[]{:S(2)}) collective-permute-start(f32[12,8,128]{2,1,0:T(8,128)S(1)} %get-tuple-element.30), channel_id=1, source_target_pairs={{1,2},{3,4},{5,6},{7,8},{9,10},{11,12},{13,14},{15,16},{17,18},{19... | collective-permute-start | bytes 147464 | tf_op jit(solution)/shard_map/ppermute | solution.py:421
  32.3 14.4 %collective-permute-start.4 = (f32[24,8,128]{2,1,0:T(8,128)S(1)}, f32[24,8,128]{2,1,0:T(8,128)S(1)}, u32[]{:S(2)}, u32[]{:S(2)}) collective-permute-start(f32[24,8,128]{2,1,0:T(8,128)S(1)} %get-tuple-element.32), channel_id=1, source_target_pairs={{0,32},{64,96},{128,160},{192,224},{256,288},{320,352},{384,416},{... | collective-permute-start | bytes 294920 | tf_op jit(solution)/shard_map/ppermute | solution.py:422
  34.2 12.5 %collective-permute-start.5 = (f32[24,8,128]{2,1,0:T(8,128)S(1)}, f32[24,8,128]{2,1,0:T(8,128)S(1)}, u32[]{:S(2)}, u32[]{:S(2)}) collective-permute-start(f32[24,8,128]{2,1,0:T(8,128)S(1)} %get-tuple-element.33), channel_id=1, source_target_pairs={{32,64},{96,128},{160,192},{224,256},{288,320},{352,384},{416,448}... | collective-permute-start | bytes 294920 | tf_op jit(solution)/shard_map/ppermute | solution.py:423
  39.1 7.6 %collective-permute-start.6 = (f32[24,8,128]{2,1,0:T(8,128)S(1)}, f32[24,8,128]{2,1,0:T(8,128)S(1)}, u32[]{:S(2)}, u32[]{:S(2)}) collective-permute-start(f32[24,8,128]{2,1,0:T(8,128)S(1)} %get-tuple-element.34), channel_id=1, source_target_pairs={{0,1},{2,3},{4,5},{6,7},{8,9},{10,11},{12,13},{14,15},{16,17},{18,... | collective-permute-start | bytes 294920 | tf_op jit(solution)/shard_map/ppermute | solution.py:420
  44.3 5.9 %collective-permute-start.7 = (f32[24,8,128]{2,1,0:T(8,128)S(1)}, f32[24,8,128]{2,1,0:T(8,128)S(1)}, u32[]{:S(2)}, u32[]{:S(2)}) collective-permute-start(f32[24,8,128]{2,1,0:T(8,128)S(1)} %get-tuple-element.35), channel_id=1, source_target_pairs={{1,2},{3,4},{5,6},{7,8},{9,10},{11,12},{13,14},{15,16},{17,18},{19... | collective-permute-start | bytes 294920 | tf_op jit(solution)/shard_map/ppermute | solution.py:421
  50.5 13.3 %collective-permute-start.10 = (f32[24,8,128]{2,1,0:T(8,128)S(1)}, f32[24,8,128]{2,1,0:T(8,128)S(1)}, u32[]{:S(2)}, u32[]{:S(2)}) collective-permute-start(f32[24,8,128]{2,1,0:T(8,128)S(1)} %get-tuple-element.39), channel_id=1, source_target_pairs={{0,1},{2,3},{4,5},{6,7},{8,9},{10,11},{12,13},{14,15},{16,17},{18,... | collective-permute-start | bytes 294920 | tf_op jit(solution)/shard_map/ppermute | solution.py:420
  54.5 9.3 %collective-permute-start.11 = (f32[24,8,128]{2,1,0:T(8,128)S(1)}, f32[24,8,128]{2,1,0:T(8,128)S(1)}, u32[]{:S(2)}, u32[]{:S(2)}) collective-permute-start(f32[24,8,128]{2,1,0:T(8,128)S(1)} %get-tuple-element.40), channel_id=1, source_target_pairs={{1,2},{3,4},{5,6},{7,8},{9,10},{11,12},{13,14},{15,16},{17,18},{19... | collective-permute-start | bytes 294920 | tf_op jit(solution)/shard_map/ppermute | solution.py:421
  56.5 7.4 %collective-permute-start.8 = (f32[24,8,128]{2,1,0:T(8,128)S(1)}, f32[24,8,128]{2,1,0:T(8,128)S(1)}, u32[]{:S(2)}, u32[]{:S(2)}) collective-permute-start(f32[24,8,128]{2,1,0:T(8,128)S(1)} %get-tuple-element.37), channel_id=1, source_target_pairs={{0,32},{64,96},{128,160},{192,224},{256,288},{320,352},{384,416},{... | collective-permute-start | bytes 294920 | tf_op jit(solution)/shard_map/ppermute | solution.py:422
  58.5 9.1 %collective-permute-start.9 = (f32[24,8,128]{2,1,0:T(8,128)S(1)}, f32[24,8,128]{2,1,0:T(8,128)S(1)}, u32[]{:S(2)}, u32[]{:S(2)}) collective-permute-start(f32[24,8,128]{2,1,0:T(8,128)S(1)} %get-tuple-element.38), channel_id=1, source_target_pairs={{32,64},{96,128},{160,192},{224,256},{288,320},{352,384},{416,448}... | collective-permute-start | bytes 294920 | tf_op jit(solution)/shard_map/ppermute | solution.py:423
  63.8 21.2 %copy-start.1 = (f32[48,1,1,6,256]{4,2,3,1,0:T(1,128)S(1)}, f32[48,1,1,6,256]{4,2,3,1,0:T(1,128)}, u32[]{:S(2)}) copy-start(f32[48,1,1,6,256]{4,2,3,1,0:T(1,128)} %param.10) | copy-start | bytes 884740
  67.8 17.9 %collective-permute-start.12 = (f32[24,8,128]{2,1,0:T(8,128)S(1)}, f32[24,8,128]{2,1,0:T(8,128)S(1)}, u32[]{:S(2)}, u32[]{:S(2)}) collective-permute-start(f32[24,8,128]{2,1,0:T(8,128)S(1)} %get-tuple-element.42), channel_id=1, source_target_pairs={{0,32},{64,96},{128,160},{192,224},{256,288},{320,352},{384,416},{... | collective-permute-start | bytes 294920 | tf_op jit(solution)/shard_map/ppermute | solution.py:422
  71.3 14.4 %collective-permute-start.13 = (f32[24,8,128]{2,1,0:T(8,128)S(1)}, f32[24,8,128]{2,1,0:T(8,128)S(1)}, u32[]{:S(2)}, u32[]{:S(2)}) collective-permute-start(f32[24,8,128]{2,1,0:T(8,128)S(1)} %get-tuple-element.43), channel_id=1, source_target_pairs={{32,64},{96,128},{160,192},{224,256},{288,320},{352,384},{416,448}... | collective-permute-start | bytes 294920 | tf_op jit(solution)/shard_map/ppermute | solution.py:423
  75.4 10.3 %collective-permute-start.14 = (f32[24,8,128]{2,1,0:T(8,128)S(1)}, f32[24,8,128]{2,1,0:T(8,128)S(1)}, u32[]{:S(2)}, u32[]{:S(2)}) collective-permute-start(f32[24,8,128]{2,1,0:T(8,128)S(1)} %get-tuple-element.44), channel_id=1, source_target_pairs={{0,1},{2,3},{4,5},{6,7},{8,9},{10,11},{12,13},{14,15},{16,17},{18,... | collective-permute-start | bytes 294920 | tf_op jit(solution)/shard_map/ppermute | solution.py:420
  83.1 5.9 %collective-permute-start.15 = (f32[24,8,128]{2,1,0:T(8,128)S(1)}, f32[24,8,128]{2,1,0:T(8,128)S(1)}, u32[]{:S(2)}, u32[]{:S(2)}) collective-permute-start(f32[24,8,128]{2,1,0:T(8,128)S(1)} %get-tuple-element.45), channel_id=1, source_target_pairs={{1,2},{3,4},{5,6},{7,8},{9,10},{11,12},{13,14},{15,16},{17,18},{19... | collective-permute-start | bytes 294920 | tf_op jit(solution)/shard_map/ppermute | solution.py:421
  90.1 5.7 %copy-start.5 = (s32[48]{0:T(128)S(1)}, s32[48]{0:T(128)}, u32[]{:S(2)}) copy-start(s32[48]{0:T(128)} %param.11) | copy-start | bytes 580
  90.1 13.7 %all-to-all-start = ((f32[32,1,96]{2,1,0:T(1,128)}), f32[32,1,96]{2,1,0:T(1,128)S(1)}, u32[]{:S(2)}, u32[]{:S(2)}) async-start(f32[32,1,96]{2,1,0:T(1,128)} %bitcast.7), calls=%async_computation | async-start | bytes 32768 | tf_op jit(solution)/shard_map/all_to_all | solution.py:490
  104.4 17.2 %all-to-all-start.1 = ((f32[24,1,96]{2,1,0:T(1,128)}), f32[24,1,96]{2,1,0:T(1,128)S(1)}, u32[]{:S(2)}, u32[]{:S(2)}) async-start(f32[24,1,96]{2,1,0:T(1,128)} %bitcast.11), calls=%async_computation.1 | async-start | bytes 24576 | tf_op jit(solution)/shard_map/all_to_all | solution.py:499
  121.6 0.7 copy-start.4

commit v3 on v2

--- a/solution.py
+++ b/solution.py
@@ -33,7 +33,14 @@
 
 
 def row8(ref, row):
+    if isinstance(ref, PackedLinks):
+        return jnp.where(ref.first, row8(ref.here, row + ref.shift), row8(ref.there, row + ref.shift))
     return ref[pl.ds(row, 8, stride=0), :]
+
+
+class PackedLinks:
+    def __init__(self, first, here, there, shift):
+        self.first, self.here, self.there, self.shift = first, here, there, shift
 
 
 def link_times(links, mu, half, vector, adjoint):
@@ -125,16 +132,27 @@
             outer[spinor_at(comp, c, p, half)] = jnp.where(even, down, up)
 
 
-def prepare_kernel(last_time, last_space, time_rank, space_rank, bits, noise, links_in,
-                   links, source, t_inner, t_outer, z_inner, z_outer):
+def source_weight(bits, time):
+    row = source_rows((8, LANES))
+    weight = jnp.zeros((8, LANES), F32)
+    for j in range(8):
+        on = jnp.where(time % DILUTE == bits[4 + j], step_size, 0.0)
+        weight = jnp.where(row == j, on, weight)
+    return weight
+
+
+def hop_factor(bits, mu, crosses):
+    phase = (1 - 2 * bits[mu]).astype(F32) * (0.5 * step_size)
+    return jnp.where(crosses, phase, 0.5 * step_size)
+
+
+def prepare_kernel(sizes, time_rank, space_rank, bits, noise, links_in, links, source):
     lane = lax.broadcasted_iota(jnp.int32, (8, LANES), 1)
     row = lax.broadcasted_iota(jnp.int32, (8, LANES), 0)
-    phases = [(1 - 2 * bits[mu]).astype(F32) * (0.5 * step_size) for mu in range(4)]
-    plain = 0.5 * step_size
-    at_x = jnp.where(lane % SIDE == SIDE - 1, phases[0], plain)
-    at_y = jnp.where((lane >= LANES - SIDE) & (row % 2 == 1), phases[1], plain)
-    at_z = jnp.full((8, LANES), jnp.where(space_rank[0] == last_space, phases[2], plain))
-    at_t = jnp.full((8, LANES), jnp.where(time_rank[0] == last_time, phases[3], plain))
+    at_x = hop_factor(bits, 0, lane % SIDE == SIDE - 1)
+    at_y = hop_factor(bits, 1, (lane >= LANES - SIDE) & (row % 2 == 1))
+    at_z = jnp.full((8, LANES), hop_factor(bits, 2, space_rank[0] == sizes[1] - 1))
+    at_t = jnp.full((8, LANES), hop_factor(bits, 3, time_rank[0] == sizes[0] - 1))
     scales = (at_x, at_y, at_z, at_t)
     for block in range(18):
         first, last = (block * 8) // 36, (block * 8 + 7) // 36
@@ -142,26 +160,9 @@
         if last != first:
             scale = jnp.where(row + block * 8 >= last * 36, scales[last], scale)
         links[block * 8 : block * 8 + 8, :] = links_in[block * 8 : block * 8 + 8, :] * scale
-    weight = jnp.zeros((8, LANES), F32)
-    for j in range(8):
-        on = jnp.where(time_rank[0] % DILUTE == bits[4 + j], step_size, 0.0)
-        weight = jnp.where(row == j, on, weight)
-    for half in range(2):
-        vector = []
-        for c in range(3):
-            pair = []
-            for p in range(2):
-                plane = (c * 2 + p) * 2 + half
-                value = noise[pl.ds(plane, 8, stride=12), :] * weight
-                source[plane] = value
-                pair.append(value)
-            vector.append(tuple(pair))
-        for mu, rank, inner, outer in (
-            (3, time_rank, t_inner, t_outer),
-            (2, space_rank, z_inner, z_outer),
-        ):
-            moved = link_times(links, mu, half, vector, True)
-            store_sends(inner, outer, is_even(rank), 0, half, moved, vector)
+    weight = source_weight(bits, time_rank[0])
+    for plane in range(12):
+        source[plane] = noise[pl.ds(plane, 8, stride=12), :] * weight
 
 
 def shift_x(value, forward):
@@ -300,8 +301,7 @@
     return received
 
 
-def step_body(kind, time_rank, space_rank, local, links, ti, to, zi, zo, solution, *sends):
-    received = arrivals(kind, time_rank, space_rank, ti, to, zi, zo)
+def step_body(received, time_rank, space_rank, local, links, solution, *sends):
     for comp in range(2):
         for half in range(2):
             top, bottom = hops(local, links, received, comp, half)
@@ -317,12 +317,38 @@
                 store_sends(inner, outer, is_even(rank), comp, half, behind, ahead)
 
 
-def step_first_kernel(*refs):
-    step_body(from_source, *refs)
-
-
-def step_kernel(*refs):
-    step_body(from_halves, *refs)
+def step_first_kernel(sizes, time_rank, space_rank, bits, local, links, ti, to, zi, zo,
+                      solution, sti, sto, szi, szo, at, bt, az, bz):
+    time, space = time_rank[0], space_rank[0]
+    own = source_weight(bits, time)
+    later = source_weight(bits, lax.rem(time + 1, sizes[0]))
+    earlier = source_weight(bits, lax.rem(time + sizes[0] - 1, sizes[0]))
+    for mu, rank, inner, outer, ahead, behind, up, down, crosses in (
+        (3, time_rank, ti, to, at, bt, later, earlier, time == 0),
+        (2, space_rank, zi, zo, az, bz, own, own, space == 0),
+    ):
+        even = is_even(rank)
+        down = down * hop_factor(bits, mu, crosses)
+        next_links = PackedLinks(even, outer, inner, 24)
+        for half in range(2):
+            vector = []
+            for c in range(3):
+                pair = []
+                for p in range(2):
+                    plane = (c * 2 + p) * 2 + half
+                    rows = pl.ds(plane, 8, stride=12)
+                    here, there = inner[rows, :], outer[rows, :]
+                    ahead[plane] = jnp.where(even, here, there) * up
+                    pair.append(jnp.where(even, there, here) * down)
+                vector.append(tuple(pair))
+            store_spin(behind, 0, half, link_times(next_links, mu, half, vector, True))
+    received = ((3, from_source(at), from_source(bt)), (2, from_source(az), from_source(bz)))
+    step_body(received, time_rank, space_rank, local, links, solution, sti, sto, szi, szo)
+
+
+def step_kernel(time_rank, space_rank, local, links, ti, to, zi, zo, *outs):
+    received = arrivals(from_halves, time_rank, space_rank, ti, to, zi, zo)
+    step_body(received, time_rank, space_rank, local, links, *outs)
 
 
 def modes_kernel(modes, out):
@@ -373,13 +399,13 @@
     copies[...] = jnp.broadcast_to(total, copies.shape)
 
 
-def correlate_kernel(row, rows, partner, out):
-    size = row.shape[1]
+def correlate_kernel(time_rank, rows, partner, out):
+    size = rows.shape[1]
     onehot = (
         partner[...] == lax.broadcasted_iota(jnp.int32, (size, size), 0)
     ).astype(F32)
     contract = (((1,), (1,)), ((), ()))
-    own = jnp.broadcast_to(row[...], (8, size))
+    own = jnp.broadcast_to(rows[pl.ds(time_rank[0], 1), :], (8, size))
     weighted = lax.dot_general(
         own, onehot, contract, precision=lax.Precision.HIGHEST, preferred_element_type=F32
     )
@@ -424,33 +450,40 @@
     return ti, to, zi, zo
 
 
+def mesh_ranks():
+    return tuple(lax.axis_index(name).astype(jnp.int32).reshape(1) for name in ("tm", "space"))
+
+
 def partial_rows(noise_field, gauge_links, clover, eigvecs, dilution, boundary):
     count = eigvecs.shape[0]
     noise = noise_field.reshape(-1, LANES)
     links_in = gauge_links.reshape(-1, LANES)
     clover = clover.reshape(-1, LANES)
     modes_in = eigvecs.reshape(-1, LANES)
-    time_rank = lax.axis_index("tm").astype(jnp.int32).reshape(1)
-    space_rank = lax.axis_index("space").astype(jnp.int32).reshape(1)
-    last_time, last_space = lax.axis_size("tm") - 1, lax.axis_size("space") - 1
-
-    ranks = (time_rank, space_rank)
+    ranks = mesh_ranks()
+    sizes = (lax.axis_size("tm"), lax.axis_size("space"))
+    bits = jnp.concatenate([boundary, dilution])
 
     def prepare(*refs):
-        prepare_kernel(last_time, last_space, *refs)
-
-    links, source, *sends = call(
-        prepare,
-        [jax.ShapeDtypeStruct(links_in.shape, F32)] + [vectors(12)] * 5,
-        10**6,
-        (*ranks, jnp.concatenate([boundary, dilution])),
-        noise,
-        links_in,
-    )
+        prepare_kernel(sizes, *refs)
+
+    def step_first(*refs):
+        step_first_kernel(sizes, *refs)
+
+    packed = jnp.concatenate([noise, links_in[links_in.shape[0] // 2 :]])
+    sends = (packed,) * 4
     solution = None
     for iteration in range(ITERS):
         arrived = exchange(*sends)
         if iteration == 0:
+            links, source = call(
+                prepare,
+                [jax.ShapeDtypeStruct(links_in.shape, F32), vectors(12)],
+                10**6,
+                (*ranks, bits),
+                noise,
+                links_in,
+            )
             local = call(local_first_kernel, vectors(48), 5 * 10**6, (), links, clover, source)
             modes = call(
                 modes_kernel,
@@ -462,13 +495,14 @@
         else:
             local = call(local_kernel, vectors(48), 5 * 10**6, (), solution, links, clover, source)
         if iteration < ITERS - 1:
-            body = step_first_kernel if iteration == 0 else step_kernel
+            first = iteration == 0
             solution, *sends = call(
-                body,
+                step_first if first else step_kernel,
                 [vectors(48)] + [vectors(24)] * 4,
                 3 * 10**6,
-                ranks,
+                (*ranks, bits) if first else ranks,
                 local, links, *arrived,
+                scratch=[pltpu.VMEM((12, 8, LANES), F32)] * 4 if first else (),
             )
         else:
             partial_sums = call(
@@ -488,7 +522,7 @@
         noise_field, gauge_links, clover, eigvecs, dilution, boundary
     )
     parts = lax.all_to_all(partial_sums, "space", 0, 0, tiled=True)
-    times = lax.axis_size("tm")
+    times, ranks = lax.axis_size("tm"), mesh_ranks()[:1]
     row, copies = call(
         sum_kernel,
         [jax.ShapeDtypeStruct((n, 2 * count), F32) for n in (1, times)],
@@ -499,7 +533,7 @@
     rows = lax.all_to_all(copies, "tm", 0, 0, tiled=True)
     both = jnp.concatenate([partner, partner + count]).reshape(1, 2 * count)
     correlator = call(
-        correlate_kernel, jax.ShapeDtypeStruct((1, times), F32), 10**5, (), row, rows, both
+        correlate_kernel, jax.ShapeDtypeStruct((1, times), F32), 10**5, ranks, rows, both
     )
     return row.reshape(1, 1, 2 * count), correlator.reshape(1, 1, times)
 

time: 124 us -> 122 us (0.984)
  local copies, waits for them, and re-layouts: 2.35 us -> 0.82 us
    unnamed x12 -> x14, local copies, waits for them, and re-layouts: 2.35 us -> 0.03 us
where the time goes in v3:
time: 122 us; the launch traced here: 121 us
  starting transfers between devices  82 us (67%)
  waiting for transfers between devices  31.1 us (25%)
  Pallas kernels  6.29 us (5%)
    ppermute x4, starting transfers between devices, exchange(): to = lax.ppermute(t_outer, 'tm', swap('tm', 1))  28.1 us
    ppermute x4, starting transfers between devices, exchange(): zi = lax.ppermute(z_inner, 'space', swap('space', 0))  20.2 us
    ppermute x4, starting transfers between devices, exchange(): ti = lax.ppermute(t_inner, 'tm', swap('tm', 0))  13 us
    all_to_all x1, waiting for transfers between devices, shards(): rows = lax.all_to_all(copies, 'tm', 0, 0, tiled=True)  11.1 us
    ppermute x4, starting transfers between devices, exchange(): zo = lax.ppermute(z_outer, 'space', swap('space', 1))  8.86 us
    ppermute x4, waiting for transfers between devices, exchange(): zo = lax.ppermute(z_outer, 'space', swap('space', 1))  8.43 us
    all_to_all x1, waiting for transfers between devices, shards(): parts = lax.all_to_all(partial_sums, 'space', 0, 0, tiled=True)  7.96 us
    pallas_call x12, Pallas kernels, call(): pl.pallas_call(kernel, out_shape=outs, in_specs=[smem] * len(scalars) + [...  6.29 us
  transfers between devices with their start and end apart: 18, of which 6 were waited for; matrix products, arithmetic and copies ran while one was open for 0% of the time, Pallas kernels for 2%

profile of v3, /device:TPU:1, one launch (start us, length us, event | category | flops | bytes accessed | tf_op | source)
XLA Modules:
  0.0 121.4 jit_solution(16718809468198184460)
XLA Ops:
  0.6 0.8 slice.6
  1.4 0.0 copy-start
  1.5 5.6 %collective-permute-start = (f32[168,128]{1,0:T(8,128)S(1)}, f32[168,128]{1,0:T(8,128)S(1)}, u32[]{:S(2)}, u32[]{:S(2)}) collective-permute-start(f32[168,128]{1,0:T(8,128)S(1)} %pad_maximum_fusion), channel_id=1, source_target_pairs={{0,32},{64,96},{128,160},{192,224},{256,288},{320,352},{384,416},{... | collective-permute-start | bytes 258056 | tf_op jit(solution)/shard_map/ppermute | solution.py:448
  7.1 14.2 %collective-permute-start.1 = (f32[168,128]{1,0:T(8,128)S(1)}, f32[168,128]{1,0:T(8,128)S(1)}, u32[]{:S(2)}, u32[]{:S(2)}) collective-permute-start(f32[168,128]{1,0:T(8,128)S(1)} %pad_maximum_fusion), channel_id=1, source_target_pairs={{32,64},{96,128},{160,192},{224,256},{288,320},{352,384},{416,448}... | collective-permute-start | bytes 258056 | tf_op jit(solution)/shard_map/ppermute | solution.py:449
  21.3 3.1 %collective-permute-start.2 = (f32[168,128]{1,0:T(8,128)S(1)}, f32[168,128]{1,0:T(8,128)S(1)}, u32[]{:S(2)}, u32[]{:S(2)}) collective-permute-start(f32[168,128]{1,0:T(8,128)S(1)} %pad_maximum_fusion), channel_id=1, source_target_pairs={{0,1},{2,3},{4,5},{6,7},{8,9},{10,11},{12,13},{14,15},{16,17},{18,... | collective-permute-start | bytes 258056 | tf_op jit(solution)/shard_map/ppermute | solution.py:446
  24.5 3.1 %collective-permute-start.3 = (f32[168,128]{1,0:T(8,128)S(1)}, f32[168,128]{1,0:T(8,128)S(1)}, u32[]{:S(2)}, u32[]{:S(2)}) collective-permute-start(f32[168,128]{1,0:T(8,128)S(1)} %pad_maximum_fusion), channel_id=1, source_target_pairs={{1,2},{3,4},{5,6},{7,8},{9,10},{11,12},{13,14},{15,16},{17,18},{19... | collective-permute-start | bytes 258056 | tf_op jit(solution)/shard_map/ppermute | solution.py:447
  27.6 0.1 pad_add_fusion.refs_2_
  27.7 0.6 shard_map.86
  28.3 0.4 shard_map.87.refs_3_
  28.7 0.0 collective-permute-done.1.refs_6_
  28.8 0.0 collective-permute-done.2.refs_7_
  28.8 1.5 %collective-permute-done.3.refs_8_ = f32[168,128]{1,0:T(8,128)S(1)} collective-permute-done((f32[168,128]{1,0:T(8,128)S(1)}, f32[168,128]{1,0:T(8,128)S(1)}, u32[]{:S(2)}, u32[]{:S(2)}) %collective-permute-start.3) | collective-permute-done | bytes 86048 | tf_op jit(solution)/shard_map/ppermute | solution.py:447
  30.3 0.9 shard_map.88
  31.2 1.9 %collective-permute-start.4 = (f32[24,8,128]{2,1,0:T(8,128)S(1)}, f32[24,8,128]{2,1,0:T(8,128)S(1)}, u32[]{:S(2)}, u32[]{:S(2)}) collective-permute-start(f32[24,8,128]{2,1,0:T(8,128)S(1)} %get-tuple-element.24), channel_id=1, source_target_pairs={{0,32},{64,96},{128,160},{192,224},{256,288},{320,352},{384,416},{... | collective-permute-start | bytes 294920 | tf_op jit(solution)/shard_map/ppermute | solution.py:448
  33.1 4.9 %collective-permute-start.5 = (f32[24,8,128]{2,1,0:T(8,128)S(1)}, f32[24,8,128]{2,1,0:T(8,128)S(1)}, u32[]{:S(2)}, u32[]{:S(2)}) collective-permute-start(f32[24,8,128]{2,1,0:T(8,128)S(1)} %get-tuple-element.25), channel_id=1, source_target_pairs={{32,64},{96,128},{160,192},{224,256},{288,320},{352,384},{416,448}... | collective-permute-start | bytes 294920 | tf_op jit(solution)/shard_map/ppermute | solution.py:449
  38.0 5.2 %collective-permute-start.6 = (f32[24,8,128]{2,1,0:T(8,128)S(1)}, f32[24,8,128]{2,1,0:T(8,128)S(1)}, u32[]{:S(2)}, u32[]{:S(2)}) collective-permute-start(f32[24,8,128]{2,1,0:T(8,128)S(1)} %get-tuple-element.26), channel_id=1, source_target_pairs={{0,1},{2,3},{4,5},{6,7},{8,9},{10,11},{12,13},{14,15},{16,17},{18,... | collective-permute-start | bytes 294920 | tf_op jit(solution)/shard_map/ppermute | solution.py:446
  43.2 1.9 %collective-permute-start.7 = (f32[24,8,128]{2,1,0:T(8,128)S(1)}, f32[24,8,128]{2,1,0:T(8,128)S(1)}, u32[]{:S(2)}, u32[]{:S(2)}) collective-permute-start(f32[24,8,128]{2,1,0:T(8,128)S(1)} %get-tuple-element.27), channel_id=1, source_target_pairs={{1,2},{3,4},{5,6},{7,8},{9,10},{11,12},{13,14},{15,16},{17,18},{19... | collective-permute-start | bytes 294920 | tf_op jit(solution)/shard_map/ppermute | solution.py:447
  45.1 0.5 shard_map.89.local
  45.6 0.0 collective-permute-done.5.to
  45.6 0.0 collective-permute-done.6.zi
  45.6 3.5 %collective-permute-done.7.zo = f32[24,8,128]{2,1,0:T(8,128)S(1)} collective-permute-done((f32[24,8,128]{2,1,0:T(8,128)S(1)}, f32[24,8,128]{2,1,0:T(8,128)S(1)}, u32[]{:S(2)}, u32[]{:S(2)}) %collective-permute-start.7) | collective-permute-done | bytes 98336 | tf_op jit(solution)/shard_map/ppermute | solution.py:447
  49.1 0.2 shard_map.90
  49.4 4.0 %collective-permute-start.10 = (f32[24,8,128]{2,1,0:T(8,128)S(1)}, f32[24,8,128]{2,1,0:T(8,128)S(1)}, u32[]{:S(2)}, u32[]{:S(2)}) collective-permute-start(f32[24,8,128]{2,1,0:T(8,128)S(1)} %get-tuple-element.31), channel_id=1, source_target_pairs={{0,1},{2,3},{4,5},{6,7},{8,9},{10,11},{12,13},{14,15},{16,17},{18,... | collective-permute-start | bytes 294920 | tf_op jit(solution)/shard_map/ppermute | solution.py:446
  53.4 1.9 %collective-permute-start.11 = (f32[24,8,128]{2,1,0:T(8,128)S(1)}, f32[24,8,128]{2,1,0:T(8,128)S(1)}, u32[]{:S(2)}, u32[]{:S(2)}) collective-permute-start(f32[24,8,128]{2,1,0:T(8,128)S(1)} %get-tuple-element.32), channel_id=1, source_target_pairs={{1,2},{3,4},{5,6},{7,8},{9,10},{11,12},{13,14},{15,16},{17,18},{19... | collective-permute-start | bytes 294920 | tf_op jit(solution)/shard_map/ppermute | solution.py:447
  55.3 2.0 %collective-permute-start.8 = (f32[24,8,128]{2,1,0:T(8,128)S(1)}, f32[24,8,128]{2,1,0:T(8,128)S(1)}, u32[]{:S(2)}, u32[]{:S(2)}) collective-permute-start(f32[24,8,128]{2,1,0:T(8,128)S(1)} %get-tuple-element.29), channel_id=1, source_target_pairs={{0,32},{64,96},{128,160},{192,224},{256,288},{320,352},{384,416},{... | collective-permute-start | bytes 294920 | tf_op jit(solution)/shard_map/ppermute | solution.py:448
  57.3 4.9 %collective-permute-start.9 = (f32[24,8,128]{2,1,0:T(8,128)S(1)}, f32[24,8,128]{2,1,0:T(8,128)S(1)}, u32[]{:S(2)}, u32[]{:S(2)}) collective-permute-start(f32[24,8,128]{2,1,0:T(8,128)S(1)} %get-tuple-element.30), channel_id=1, source_target_pairs={{32,64},{96,128},{160,192},{224,256},{288,320},{352,384},{416,448}... | collective-permute-start | bytes 294920 | tf_op jit(solution)/shard_map/ppermute | solution.py:449
  62.3 0.4 shard_map.91.local
  62.7 0.0 copy-start.1
  62.7 0.0 collective-permute-done.10.zi
  62.7 0.0 collective-permute-done.11.zo
  62.8 3.6 %collective-permute-done.9.to = f32[24,8,128]{2,1,0:T(8,128)S(1)} collective-permute-done((f32[24,8,128]{2,1,0:T(8,128)S(1)}, f32[24,8,128]{2,1,0:T(8,128)S(1)}, u32[]{:S(2)}, u32[]{:S(2)}) %collective-permute-start.9) | collective-permute-done | bytes 98336 | tf_op jit(solution)/shard_map/ppermute | solution.py:449
  66.4 0.2 shard_map.92
  66.6 3.5 %collective-permute-start.12 = (f32[24,8,128]{2,1,0:T(8,128)S(1)}, f32[24,8,128]{2,1,0:T(8,128)S(1)}, u32[]{:S(2)}, u32[]{:S(2)}) collective-permute-start(f32[24,8,128]{2,1,0:T(8,128)S(1)} %get-tuple-element.34), channel_id=1, source_target_pairs={{0,32},{64,96},{128,160},{192,224},{256,288},{320,352},{384,416},{... | collective-permute-start | bytes 294920 | tf_op jit(solution)/shard_map/ppermute | solution.py:448
  70.2 4.1 %collective-permute-start.13 = (f32[24,8,128]{2,1,0:T(8,128)S(1)}, f32[24,8,128]{2,1,0:T(8,128)S(1)}, u32[]{:S(2)}, u32[]{:S(2)}) collective-permute-start(f32[24,8,128]{2,1,0:T(8,128)S(1)} %get-tuple-element.35), channel_id=1, source_target_pairs={{32,64},{96,128},{160,192},{224,256},{288,320},{352,384},{416,448}... | collective-permute-start | bytes 294920 | tf_op jit(solution)/shard_map/ppermute | solution.py:449
  74.2 7.7 %collective-permute-start.14 = (f32[24,8,128]{2,1,0:T(8,128)S(1)}, f32[24,8,128]{2,1,0:T(8,128)S(1)}, u32[]{:S(2)}, u32[]{:S(2)}) collective-permute-start(f32[24,8,128]{2,1,0:T(8,128)S(1)} %get-tuple-element.36), channel_id=1, source_target_pairs={{0,1},{2,3},{4,5},{6,7},{8,9},{10,11},{12,13},{14,15},{16,17},{18,... | collective-permute-start | bytes 294920 | tf_op jit(solution)/shard_map/ppermute | solution.py:446
  82.0 1.9 %collective-permute-start.15 = (f32[24,8,128]{2,1,0:T(8,128)S(1)}, f32[24,8,128]{2,1,0:T(8,128)S(1)}, u32[]{:S(2)}, u32[]{:S(2)}) collective-permute-start(f32[24,8,128]{2,1,0:T(8,128)S(1)} %get-tuple-element.37), channel_id=1, source_target_pairs={{1,2},{3,4},{5,6},{7,8},{9,10},{11,12},{13,14},{15,16},{17,18},{19... | collective-permute-start | bytes 294920 | tf_op jit(solution)/shard_map/ppermute | solution.py:447
  83.9 0.1 shard_map.94.modes
  84.1 0.4 shard_map.93.local
  84.5 0.0 collective-permute-done.13.to
  84.5 3.4 %collective-permute-done.15.zo = f32[24,8,128]{2,1,0:T(8,128)S(1)} collective-permute-done((f32[24,8,128]{2,1,0:T(8,128)S(1)}, f32[24,8,128]{2,1,0:T(8,128)S(1)}, u32[]{:S(2)}, u32[]{:S(2)}) %collective-permute-start.15) | collective-permute-done | bytes 98336 | tf_op jit(solution)/shard_map/ppermute | solution.py:447
  87.9 1.0 shard_map.95
  88.9 5.8 %all-to-all-start = ((f32[32,1,96]{2,1,0:T(1,128)}), f32[32,1,96]{2,1,0:T(1,128)S(1)}, u32[]{:S(2)}, u32[]{:S(2)}) async-start(f32[32,1,96]{2,1,0:T(1,128)} %bitcast.8), calls=%async_computation | async-start | bytes 32768 | tf_op jit(solution)/shard_map/all_to_all | solution.py:524
  94.7 8.0 %all-to-all-done = f32[32,1,96]{2,1,0:T(1,128)S(1)} async-done(((f32[32,1,96]{2,1,0:T(1,128)}), f32[32,1,96]{2,1,0:T(1,128)S(1)}, u32[]{:S(2)}, u32[]{:S(2)}) %all-to-all-start) | async-done | bytes 12320 | tf_op jit(solution)/shard_map/all_to_all | solution.py:524
  102.7 0.6 shard_map.96
  103.3 6.1 %all-to-all-start.1 = ((f32[24,1,96]{2,1,0:T(1,128)}), f32[24,1,96]{2,1,0:T(1,128)S(1)}, u32[]{:S(2)}, u32[]{:S(2)}) async-start(f32[24,1,96]{2,1,0:T(1,128)} %bitcast.12), calls=%async_computation.1 | async-start | bytes 24576 | tf_op jit(solution)/shard_map/all_to_all | solution.py:533
  109.4 0.1 add_bitcast_fusion.partner
  109.5 11.1 %all-to-all-done.1 = f32[24,1,96]{2,1,0:T(1,128)S(1)} async-done(((f32[24,1,96]{2,1,0:T(1,128)}), f32[24,1,96]{2,1,0:T(1,128)S(1)}, u32[]{:S(2)}, u32[]{:S(2)}) %all-to-all-start.1) | async-done | bytes 9248 | tf_op jit(solution)/shard_map/all_to_all | solution.py:533
  120.5 0.9 shard_map.97
  (19 shorter events, 0.0 us)
Async XLA Ops:
  0.6 0.8 copy-start.2
  1.4 26.2 %copy-start.4 = (s32[8]{0:T(128)S(1)}, s32[8]{0:T(128)}, u32[]{:S(2)}) copy-start(s32[8]{0:T(128)} %param.12) | copy-start | bytes 100
  1.4 26.2 %copy-start.5 = (s32[4]{0:T(128)S(1)}, s32[4]{0:T(128)}, u32[]{:S(2)}) copy-start(s32[4]{0:T(128)} %param.13) | copy-start | bytes 52
  1.4 26.3 %copy-start.3 = (f32[4,3,1,1,6,256]{5,3,4,2,1,0:T(1,128)S(1)}, f32[4,3,1,1,6,256]{5,3,4,2,1,0:T(1,128)}, u32[]{:S(2)}) copy-start(f32[4,3,1,1,6,256]{5,3,4,2,1,0:T(1,128)} %param.8) | copy-start | bytes 221188
  1.4 26.8 %copy-start = (f32[2,6,1,1,12,256]{5,3,4,2,1,0:T(1,128)S(1)}, f32[2,6,1,1,12,256]{5,3,4,2,1,0:T(1,128)}, u32[]{:S(2)}) copy-start(f32[2,6,1,1,12,256]{5,3,4,2,1,0:T(1,128)} %param.9) | copy-start | bytes 442372
  1.5 27.3 %collective-permute-start = (f32[168,128]{1,0:T(8,128)S(1)}, f32[168,128]{1,0:T(8,128)S(1)}, u32[]{:S(2)}, u32[]{:S(2)}) collective-permute-start(f32[168,128]{1,0:T(8,128)S(1)} %pad_maximum_fusion), channel_id=1, source_target_pairs={{0,32},{64,96},{128,160},{192,224},{256,288},{320,352},{384,416},{... | collective-permute-start | bytes 258056 | tf_op jit(solution)/shard_map/ppermute | solution.py:448
  7.1 21.7 %collective-permute-start.1 = (f32[168,128]{1,0:T(8,128)S(1)}, f32[168,128]{1,0:T(8,128)S(1)}, u32[]{:S(2)}, u32[]{:S(2)}) collective-permute-start(f32[168,128]{1,0:T(8,128)S(1)} %pad_maximum_fusion), channel_id=1, source_target_pairs={{32,64},{96,128},{160,192},{224,256},{288,320},{352,384},{416,448}... | collective-permute-start | bytes 258056 | tf_op jit(solution)/shard_map/ppermute | solution.py:449
  21.3 7.4 %collective-permute-start.2 = (f32[168,128]{1,0:T(8,128)S(1)}, f32[168,128]{1,0:T(8,128)S(1)}, u32[]{:S(2)}, u32[]{:S(2)}) collective-permute-start(f32[168,128]{1,0:T(8,128)S(1)} %pad_maximum_fusion), channel_id=1, source_target_pairs={{0,1},{2,3},{4,5},{6,7},{8,9},{10,11},{12,13},{14,15},{16,17},{18,... | collective-permute-start | bytes 258056 | tf_op jit(solution)/shard_map/ppermute | solution.py:446
  24.5 5.8 %collective-permute-start.3 = (f32[168,128]{1,0:T(8,128)S(1)}, f32[168,128]{1,0:T(8,128)S(1)}, u32[]{:S(2)}, u32[]{:S(2)}) collective-permute-start(f32[168,128]{1,0:T(8,128)S(1)} %pad_maximum_fusion), channel_id=1, source_target_pairs={{1,2},{3,4},{5,6},{7,8},{9,10},{11,12},{13,14},{15,16},{17,18},{19... | collective-permute-start | bytes 258056 | tf_op jit(solution)/shard_map/ppermute | solution.py:447
  31.2 14.4 %collective-permute-start.4 = (f32[24,8,128]{2,1,0:T(8,128)S(1)}, f32[24,8,128]{2,1,0:T(8,128)S(1)}, u32[]{:S(2)}, u32[]{:S(2)}) collective-permute-start(f32[24,8,128]{2,1,0:T(8,128)S(1)} %get-tuple-element.24), channel_id=1, source_target_pairs={{0,32},{64,96},{128,160},{192,224},{256,288},{320,352},{384,416},{... | collective-permute-start | bytes 294920 | tf_op jit(solution)/shard_map/ppermute | solution.py:448
  33.1 12.5 %collective-permute-start.5 = (f32[24,8,128]{2,1,0:T(8,128)S(1)}, f32[24,8,128]{2,1,0:T(8,128)S(1)}, u32[]{:S(2)}, u32[]{:S(2)}) collective-permute-start(f32[24,8,128]{2,1,0:T(8,128)S(1)} %get-tuple-element.25), channel_id=1, source_target_pairs={{32,64},{96,128},{160,192},{224,256},{288,320},{352,384},{416,448}... | collective-permute-start | bytes 294920 | tf_op jit(solution)/shard_map/ppermute | solution.py:449
  38.0 7.7 %collective-permute-start.6 = (f32[24,8,128]{2,1,0:T(8,128)S(1)}, f32[24,8,128]{2,1,0:T(8,128)S(1)}, u32[]{:S(2)}, u32[]{:S(2)}) collective-permute-start(f32[24,8,128]{2,1,0:T(8,128)S(1)} %get-tuple-element.26), channel_id=1, source_target_pairs={{0,1},{2,3},{4,5},{6,7},{8,9},{10,11},{12,13},{14,15},{16,17},{18,... | collective-permute-start | bytes 294920 | tf_op jit(solution)/shard_map/ppermute | solution.py:446
  43.2 5.9 %collective-permute-start.7 = (f32[24,8,128]{2,1,0:T(8,128)S(1)}, f32[24,8,128]{2,1,0:T(8,128)S(1)}, u32[]{:S(2)}, u32[]{:S(2)}) collective-permute-start(f32[24,8,128]{2,1,0:T(8,128)S(1)} %get-tuple-element.27), channel_id=1, source_target_pairs={{1,2},{3,4},{5,6},{7,8},{9,10},{11,12},{13,14},{15,16},{17,18},{19... | collective-permute-start | bytes 294920 | tf_op jit(solution)/shard_map/ppermute | solution.py:447
  49.4 13.3 %collective-permute-start.10 = (f32[24,8,128]{2,1,0:T(8,128)S(1)}, f32[24,8,128]{2,1,0:T(8,128)S(1)}, u32[]{:S(2)}, u32[]{:S(2)}) collective-permute-start(f32[24,8,128]{2,1,0:T(8,128)S(1)} %get-tuple-element.31), channel_id=1, source_target_pairs={{0,1},{2,3},{4,5},{6,7},{8,9},{10,11},{12,13},{14,15},{16,17},{18,... | collective-permute-start | bytes 294920 | tf_op jit(solution)/shard_map/ppermute | solution.py:446
  53.4 9.3 %collective-permute-start.11 = (f32[24,8,128]{2,1,0:T(8,128)S(1)}, f32[24,8,128]{2,1,0:T(8,128)S(1)}, u32[]{:S(2)}, u32[]{:S(2)}) collective-permute-start(f32[24,8,128]{2,1,0:T(8,128)S(1)} %get-tuple-element.32), channel_id=1, source_target_pairs={{1,2},{3,4},{5,6},{7,8},{9,10},{11,12},{13,14},{15,16},{17,18},{19... | collective-permute-start | bytes 294920 | tf_op jit(solution)/shard_map/ppermute | solution.py:447
  55.3 7.4 %collective-permute-start.8 = (f32[24,8,128]{2,1,0:T(8,128)S(1)}, f32[24,8,128]{2,1,0:T(8,128)S(1)}, u32[]{:S(2)}, u32[]{:S(2)}) collective-permute-start(f32[24,8,128]{2,1,0:T(8,128)S(1)} %get-tuple-element.29), channel_id=1, source_target_pairs={{0,32},{64,96},{128,160},{192,224},{256,288},{320,352},{384,416},{... | collective-permute-start | bytes 294920 | tf_op jit(solution)/shard_map/ppermute | solution.py:448
  57.3 9.1 %collective-permute-start.9 = (f32[24,8,128]{2,1,0:T(8,128)S(1)}, f32[24,8,128]{2,1,0:T(8,128)S(1)}, u32[]{:S(2)}, u32[]{:S(2)}) collective-permute-start(f32[24,8,128]{2,1,0:T(8,128)S(1)} %get-tuple-element.30), channel_id=1, source_target_pairs={{32,64},{96,128},{160,192},{224,256},{288,320},{352,384},{416,448}... | collective-permute-start | bytes 294920 | tf_op jit(solution)/shard_map/ppermute | solution.py:449
  62.7 21.2 %copy-start.1 = (f32[48,1,1,6,256]{4,2,3,1,0:T(1,128)S(1)}, f32[48,1,1,6,256]{4,2,3,1,0:T(1,128)}, u32[]{:S(2)}) copy-start(f32[48,1,1,6,256]{4,2,3,1,0:T(1,128)} %param.10) | copy-start | bytes 884740
  66.6 17.9 %collective-permute-start.12 = (f32[24,8,128]{2,1,0:T(8,128)S(1)}, f32[24,8,128]{2,1,0:T(8,128)S(1)}, u32[]{:S(2)}, u32[]{:S(2)}) collective-permute-start(f32[24,8,128]{2,1,0:T(8,128)S(1)} %get-tuple-element.34), channel_id=1, source_target_pairs={{0,32},{64,96},{128,160},{192,224},{256,288},{320,352},{384,416},{... | collective-permute-start | bytes 294920 | tf_op jit(solution)/shard_map/ppermute | solution.py:448
  70.2 14.4 %collective-permute-start.13 = (f32[24,8,128]{2,1,0:T(8,128)S(1)}, f32[24,8,128]{2,1,0:T(8,128)S(1)}, u32[]{:S(2)}, u32[]{:S(2)}) collective-permute-start(f32[24,8,128]{2,1,0:T(8,128)S(1)} %get-tuple-element.35), channel_id=1, source_target_pairs={{32,64},{96,128},{160,192},{224,256},{288,320},{352,384},{416,448}... | collective-permute-start | bytes 294920 | tf_op jit(solution)/shard_map/ppermute | solution.py:449
  74.2 10.3 %collective-permute-start.14 = (f32[24,8,128]{2,1,0:T(8,128)S(1)}, f32[24,8,128]{2,1,0:T(8,128)S(1)}, u32[]{:S(2)}, u32[]{:S(2)}) collective-permute-start(f32[24,8,128]{2,1,0:T(8,128)S(1)} %get-tuple-element.36), channel_id=1, source_target_pairs={{0,1},{2,3},{4,5},{6,7},{8,9},{10,11},{12,13},{14,15},{16,17},{18,... | collective-permute-start | bytes 294920 | tf_op jit(solution)/shard_map/ppermute | solution.py:446
  82.0 5.9 %collective-permute-start.15 = (f32[24,8,128]{2,1,0:T(8,128)S(1)}, f32[24,8,128]{2,1,0:T(8,128)S(1)}, u32[]{:S(2)}, u32[]{:S(2)}) collective-permute-start(f32[24,8,128]{2,1,0:T(8,128)S(1)} %get-tuple-element.37), channel_id=1, source_target_pairs={{1,2},{3,4},{5,6},{7,8},{9,10},{11,12},{13,14},{15,16},{17,18},{19... | collective-permute-start | bytes 294920 | tf_op jit(solution)/shard_map/ppermute | solution.py:447
  88.9 5.8 %copy-start.6 = (s32[48]{0:T(128)S(1)}, s32[48]{0:T(128)}, u32[]{:S(2)}) copy-start(s32[48]{0:T(128)} %param.11) | copy-start | bytes 580
  88.9 13.7 %all-to-all-start = ((f32[32,1,96]{2,1,0:T(1,128)}), f32[32,1,96]{2,1,0:T(1,128)S(1)}, u32[]{:S(2)}, u32[]{:S(2)}) async-start(f32[32,1,96]{2,1,0:T(1,128)} %bitcast.8), calls=%async_computation | async-start | bytes 32768 | tf_op jit(solution)/shard_map/all_to_all | solution.py:524
  103.3 17.2 %all-to-all-start.1 = ((f32[24,1,96]{2,1,0:T(1,128)}), f32[24,1,96]{2,1,0:T(1,128)S(1)}, u32[]{:S(2)}, u32[]{:S(2)}) async-start(f32[24,1,96]{2,1,0:T(1,128)} %bitcast.12), calls=%async_computation.1 | async-start | bytes 24576 | tf_op jit(solution)/shard_map/all_to_all | solution.py:533

commit v4 on v3

--- a/solution.py
+++ b/solution.py
@@ -34,13 +34,13 @@
 
 def row8(ref, row):
     if isinstance(ref, PackedLinks):
-        return jnp.where(ref.first, row8(ref.here, row + ref.shift), row8(ref.there, row + ref.shift))
+        return jnp.where(ref.first, *(row8(side, row + base + 24) for side, base in ref.sides))
     return ref[pl.ds(row, 8, stride=0), :]
 
 
 class PackedLinks:
-    def __init__(self, first, here, there, shift):
-        self.first, self.here, self.there, self.shift = first, here, there, shift
+    def __init__(self, first, *sides):
+        self.first, self.sides = first, sides
 
 
 def link_times(links, mu, half, vector, adjoint):
@@ -113,11 +113,19 @@
 
 
 class Pick:
-    def __init__(self, first, here, there):
-        self.first, self.here, self.there = first, here, there
+    def __init__(self, first, *sides):
+        self.first, self.sides = first, sides
 
     def __getitem__(self, index):
-        return jnp.where(self.first, self.here[index], self.there[index])
+        return jnp.where(self.first, *(ref[base + index] for ref, base in self.sides))
+
+
+def neighbours(time_rank, space_rank, ti, to, zi, zo):
+    half = zi.shape[0] // 2
+    return (
+        (3, is_even(time_rank), ((ti, 0), (to, 0)), ((to, 0), (ti, 0))),
+        (2, is_even(space_rank), ((zi, half), (zo, 0)), ((zo, 0), (zi, 0))),
+    )
 
 
 def is_even(rank):
@@ -290,15 +298,11 @@
     return load
 
 
-def arrivals(kind, time_rank, space_rank, t_inner, t_outer, z_inner, z_outer):
-    received = []
-    for mu, rank, inner, outer in (
-        (3, time_rank, t_inner, t_outer),
-        (2, space_rank, z_inner, z_outer),
-    ):
-        even = is_even(rank)
-        received.append((mu, kind(Pick(even, inner, outer)), kind(Pick(even, outer, inner))))
-    return received
+def arrivals(*refs):
+    return [
+        (mu, from_halves(Pick(even, *after)), from_halves(Pick(even, *before)))
+        for mu, even, after, before in neighbours(*refs)
+    ]
 
 
 def step_body(received, time_rank, space_rank, local, links, solution, *sends):
@@ -323,31 +327,33 @@
     own = source_weight(bits, time)
     later = source_weight(bits, lax.rem(time + 1, sizes[0]))
     earlier = source_weight(bits, lax.rem(time + sizes[0] - 1, sizes[0]))
-    for mu, rank, inner, outer, ahead, behind, up, down, crosses in (
-        (3, time_rank, ti, to, at, bt, later, earlier, time == 0),
-        (2, space_rank, zi, zo, az, bz, own, own, space == 0),
+    blocks = neighbours(time_rank, space_rank, ti, to, zi, zo)
+    for (mu, even, after, before), ahead, behind, up, down, crosses in (
+        (blocks[0], at, bt, later, earlier, time == 0),
+        (blocks[1], az, bz, own, own, space == 0),
     ):
-        even = is_even(rank)
         down = down * hop_factor(bits, mu, crosses)
-        next_links = PackedLinks(even, outer, inner, 24)
         for half in range(2):
             vector = []
             for c in range(3):
                 pair = []
                 for p in range(2):
                     plane = (c * 2 + p) * 2 + half
-                    rows = pl.ds(plane, 8, stride=12)
-                    here, there = inner[rows, :], outer[rows, :]
-                    ahead[plane] = jnp.where(even, here, there) * up
-                    pair.append(jnp.where(even, there, here) * down)
+                    next_block, last_block = (
+                        jnp.where(even, *(ref[pl.ds(base + plane, 8, stride=12), :] for ref, base in sides))
+                        for sides in (after, before)
+                    )
+                    ahead[plane] = next_block * up
+                    pair.append(last_block * down)
                 vector.append(tuple(pair))
-            store_spin(behind, 0, half, link_times(next_links, mu, half, vector, True))
+            moved = link_times(PackedLinks(even, *before), mu, half, vector, True)
+            store_spin(behind, 0, half, moved)
     received = ((3, from_source(at), from_source(bt)), (2, from_source(az), from_source(bz)))
     step_body(received, time_rank, space_rank, local, links, solution, sti, sto, szi, szo)
 
 
 def step_kernel(time_rank, space_rank, local, links, ti, to, zi, zo, *outs):
-    received = arrivals(from_halves, time_rank, space_rank, ti, to, zi, zo)
+    received = arrivals(time_rank, space_rank, ti, to, zi, zo)
     step_body(received, time_rank, space_rank, local, links, *outs)
 
 
@@ -368,7 +374,7 @@
 
 
 def last_kernel(time_rank, space_rank, local, links, ti, to, zi, zo, modes, out, rows):
-    received = arrivals(from_halves, time_rank, space_rank, ti, to, zi, zo)
+    received = arrivals(time_rank, space_rank, ti, to, zi, zo)
     for comp in range(2):
         for half in range(2):
             pair = hops(local, links, received, comp, half)
@@ -443,7 +449,8 @@
         pairs = [((i + shift) % size, (i + 1 + shift) % size) for i in range(0, size, 2)]
         return pairs + [(j, i) for i, j in pairs]
 
-    zi = lax.ppermute(z_inner, "space", swap("space", 0))
+    pairs = [[i, i + 1] for i in range(0, lax.axis_size("space"), 2)]
+    zi = lax.all_gather(z_inner, "space", axis_index_groups=pairs, tiled=True)
     zo = lax.ppermute(z_outer, "space", swap("space", 1))
     ti = lax.ppermute(t_inner, "tm", swap("tm", 0))
     to = lax.ppermute(t_outer, "tm", swap("tm", 1))
@@ -521,6 +528,8 @@
     partial_sums = partial_rows(
         noise_field, gauge_links, clover, eigvecs, dilution, boundary
     )
+    both = jnp.concatenate([partner, partner + count]).reshape(1, 2 * count)
+    both, partial_sums = lax.optimization_barrier((both, partial_sums))
     parts = lax.all_to_all(partial_sums, "space", 0, 0, tiled=True)
     times, ranks = lax.axis_size("tm"), mesh_ranks()[:1]
     row, copies = call(
@@ -531,7 +540,6 @@
         parts,
     )
     rows = lax.all_to_all(copies, "tm", 0, 0, tiled=True)
-    both = jnp.concatenate([partner, partner + count]).reshape(1, 2 * count)
     correlator = call(
         correlate_kernel, jax.ShapeDtypeStruct((1, times), F32), 10**5, ranks, rows, both
     )

time: 122 us -> 110 us (0.902)
  blocking collectives: 0 us -> 50.6 us
  waiting for transfers between devices: 31.1 us -> 0.03 us
  starting transfers between devices: 82 us -> 51.4 us
    all_to_all x0 -> x2, blocking collectives: none -> 30.1 us  [the longest x1 17.9 us: shards(): rows = lax.all_to_all(copies, 'tm', 0, 0, tiled=True)]
    all_gather x0 -> x4, blocking collectives: none -> 20.5 us  [exchange(): zi = lax.all_gather(z_inner, 'space', axis_index_groups=pairs, tiled=True)]
    ppermute x4 -> x0, starting transfers between devices: 20.2 us -> none  [exchange(): zi = lax.ppermute(z_inner, 'space', swap('space', 0))]
    all_to_all x2 -> x0, waiting for transfers between devices: 19 us -> none  [the longest x1 11.1 us: shards(): rows = lax.all_to_all(copies, 'tm', 0, 0, tiled=True)]
    all_to_all x2 -> x0, starting transfers between devices: 11.8 us -> none  [the longest x1 6.09 us: shards(): rows = lax.all_to_all(copies, 'tm', 0, 0, tiled=True)]
    ppermute x4, waiting for transfers between devices: 8.43 us -> 0.01 us  [exchange(): zo = lax.ppermute(z_outer, 'space', swap('space', 1))]
    ppermute x4, waiting for transfers between devices: 3.66 us -> 0.01 us  [exchange(): to = lax.ppermute(t_outer, 'tm', swap('tm', 1))]
    ppermute x4, starting transfers between devices: 8.86 us -> 10.3 us  [exchange(): zo = lax.ppermute(z_outer, 'space', swap('space', 1))]
  transfers between devices with their start and end apart: 18 -> 12, of which waited for: 6 -> 0; matrix products, arithmetic and copies ran while one was open for 0% -> 0% of each run, Pallas kernels for 2% -> 2%
where the time goes in v4:
time: 110 us; the launch traced here: 109 us
  starting transfers between devices  51.4 us (47%)
  blocking collectives  50.6 us (46%)
  Pallas kernels  5.61 us (5%)
    ppermute x4, starting transfers between devices, exchange(): to = lax.ppermute(t_outer, 'tm', swap('tm', 1))  28 us
    all_gather x4, blocking collectives, exchange(): zi = lax.all_gather(z_inner, 'space', axis_index_groups=pairs, tiled=True)  20.5 us
    all_to_all x1, blocking collectives, shards(): rows = lax.all_to_all(copies, 'tm', 0, 0, tiled=True)  17.9 us
    ppermute x4, starting transfers between devices, exchange(): ti = lax.ppermute(t_inner, 'tm', swap('tm', 0))  13.1 us
    all_to_all x1, blocking collectives, shards(): parts = lax.all_to_all(partial_sums, 'space', 0, 0, tiled=True)  12.2 us
    ppermute x4, starting transfers between devices, exchange(): zo = lax.ppermute(z_outer, 'space', swap('space', 1))  10.3 us
    pallas_call x12, Pallas kernels, call(): pl.pallas_call(kernel, out_shape=outs, in_specs=[smem] * len(scalars) + [...  5.61 us
  transfers between devices with their start and end apart: 12, of which 0 were waited for; matrix products, arithmetic and copies ran while one was open for 0% of the time, Pallas kernels for 2%

profile of v4, /device:TPU:1, one launch (start us, length us, event | category | flops | bytes accessed | tf_op | source)
XLA Modules:
  0.0 109.5 jit_solution(8852493694621449882)
XLA Ops:
  0.6 0.8 slice.6
  1.4 0.0 copy-start
  1.5 5.6 %collective-permute-start = (f32[168,128]{1,0:T(8,128)S(1)}, f32[168,128]{1,0:T(8,128)S(1)}, u32[]{:S(2)}, u32[]{:S(2)}) collective-permute-start(f32[168,128]{1,0:T(8,128)S(1)} %pad_maximum_fusion), channel_id=1, source_target_pairs={{0,32},{64,96},{128,160},{192,224},{256,288},{320,352},{384,416},{... | collective-permute-start | bytes 258056 | tf_op jit(solution)/shard_map/ppermute | solution.py:455
  7.1 14.2 %collective-permute-start.1 = (f32[168,128]{1,0:T(8,128)S(1)}, f32[168,128]{1,0:T(8,128)S(1)}, u32[]{:S(2)}, u32[]{:S(2)}) collective-permute-start(f32[168,128]{1,0:T(8,128)S(1)} %pad_maximum_fusion), channel_id=1, source_target_pairs={{32,64},{96,128},{160,192},{224,256},{288,320},{352,384},{416,448}... | collective-permute-start | bytes 258056 | tf_op jit(solution)/shard_map/ppermute | solution.py:456
  21.3 4.3 %collective-permute-start.2 = (f32[168,128]{1,0:T(8,128)S(1)}, f32[168,128]{1,0:T(8,128)S(1)}, u32[]{:S(2)}, u32[]{:S(2)}) collective-permute-start(f32[168,128]{1,0:T(8,128)S(1)} %pad_maximum_fusion), channel_id=1, source_target_pairs={{1,2},{3,4},{5,6},{7,8},{9,10},{11,12},{13,14},{15,16},{17,18},{19... | collective-permute-start | bytes 258056 | tf_op jit(solution)/shard_map/ppermute | solution.py:454
  25.7 0.0 copy-done.4
  25.7 0.1 pad_add_fusion.refs_2_
  25.8 0.6 shard_map.86
  26.4 0.4 shard_map.87.refs_3_
  26.8 3.7 %all_gather.12.refs_7_ = f32[336,128]{1,0:T(8,128)S(1)} all-gather(f32[168,128]{1,0:T(8,128)S(1)} %pad_maximum_fusion), channel_id=1, replica_groups={{0,1},{2,3},{4,5},{6,7},{8,9},{10,11},{12,13},{14,15},{16,17},{18,19},{..., dimensions={0}, use_global_device_ids=true | all-gather | bytes 258048 | tf_op jit(solution)/shard_map/all_gather | solution.py:453
  30.5 0.0 collective-permute-done.refs_5_
  30.5 0.0 collective-permute-done.1.refs_6_
  30.5 0.0 collective-permute-done.2.refs_8_
  30.5 0.9 shard_map.88
  31.3 1.9 %collective-permute-start.3 = (f32[24,8,128]{2,1,0:T(8,128)S(1)}, f32[24,8,128]{2,1,0:T(8,128)S(1)}, u32[]{:S(2)}, u32[]{:S(2)}) collective-permute-start(f32[24,8,128]{2,1,0:T(8,128)S(1)} %get-tuple-element.26), channel_id=1, source_target_pairs={{0,32},{64,96},{128,160},{192,224},{256,288},{320,352},{384,416},{... | collective-permute-start | bytes 294920 | tf_op jit(solution)/shard_map/ppermute | solution.py:455
  33.3 4.9 %collective-permute-start.4 = (f32[24,8,128]{2,1,0:T(8,128)S(1)}, f32[24,8,128]{2,1,0:T(8,128)S(1)}, u32[]{:S(2)}, u32[]{:S(2)}) collective-permute-start(f32[24,8,128]{2,1,0:T(8,128)S(1)} %get-tuple-element.27), channel_id=1, source_target_pairs={{32,64},{96,128},{160,192},{224,256},{288,320},{352,384},{416,448}... | collective-permute-start | bytes 294920 | tf_op jit(solution)/shard_map/ppermute | solution.py:456
  38.1 2.1 %collective-permute-start.5 = (f32[24,8,128]{2,1,0:T(8,128)S(1)}, f32[24,8,128]{2,1,0:T(8,128)S(1)}, u32[]{:S(2)}, u32[]{:S(2)}) collective-permute-start(f32[24,8,128]{2,1,0:T(8,128)S(1)} %get-tuple-element.29), channel_id=1, source_target_pairs={{1,2},{3,4},{5,6},{7,8},{9,10},{11,12},{13,14},{15,16},{17,18},{19... | collective-permute-start | bytes 294920 | tf_op jit(solution)/shard_map/ppermute | solution.py:454
  40.3 0.5 shard_map.89.local
  40.7 4.7 %all_gather.13.zi = f32[48,8,128]{2,1,0:T(8,128)S(1)} all-gather(f32[24,8,128]{2,1,0:T(8,128)S(1)} %get-tuple-element.28), channel_id=1, replica_groups={{0,1},{2,3},{4,5},{6,7},{8,9},{10,11},{12,13},{14,15},{16,17},{18,19},{..., dimensions={0}, use_global_device_ids=true | all-gather | bytes 294912 | tf_op jit(solution)/shard_map/all_gather | solution.py:453
  45.4 0.0 collective-permute-done.3.ti
  45.4 0.0 collective-permute-done.4.to
  45.4 0.0 collective-permute-done.5.zo
  45.4 0.2 shard_map.90
  45.6 2.5 %collective-permute-start.6 = (f32[24,8,128]{2,1,0:T(8,128)S(1)}, f32[24,8,128]{2,1,0:T(8,128)S(1)}, u32[]{:S(2)}, u32[]{:S(2)}) collective-permute-start(f32[24,8,128]{2,1,0:T(8,128)S(1)} %get-tuple-element.31), channel_id=1, source_target_pairs={{0,32},{64,96},{128,160},{192,224},{256,288},{320,352},{384,416},{... | collective-permute-start | bytes 294920 | tf_op jit(solution)/shard_map/ppermute | solution.py:455
  48.2 0.0 copy-start.6
  48.2 4.2 %collective-permute-start.7 = (f32[24,8,128]{2,1,0:T(8,128)S(1)}, f32[24,8,128]{2,1,0:T(8,128)S(1)}, u32[]{:S(2)}, u32[]{:S(2)}) collective-permute-start(f32[24,8,128]{2,1,0:T(8,128)S(1)} %get-tuple-element.32), channel_id=1, source_target_pairs={{32,64},{96,128},{160,192},{224,256},{288,320},{352,384},{416,448}... | collective-permute-start | bytes 294920 | tf_op jit(solution)/shard_map/ppermute | solution.py:456
  52.5 1.9 %collective-permute-start.8 = (f32[24,8,128]{2,1,0:T(8,128)S(1)}, f32[24,8,128]{2,1,0:T(8,128)S(1)}, u32[]{:S(2)}, u32[]{:S(2)}) collective-permute-start(f32[24,8,128]{2,1,0:T(8,128)S(1)} %get-tuple-element.34), channel_id=1, source_target_pairs={{1,2},{3,4},{5,6},{7,8},{9,10},{11,12},{13,14},{15,16},{17,18},{19... | collective-permute-start | bytes 294920 | tf_op jit(solution)/shard_map/ppermute | solution.py:454
  54.4 0.4 shard_map.91.local
  54.8 5.6 %all_gather.14.zi = f32[48,8,128]{2,1,0:T(8,128)S(1)} all-gather(f32[24,8,128]{2,1,0:T(8,128)S(1)} %get-tuple-element.33), channel_id=1, replica_groups={{0,1},{2,3},{4,5},{6,7},{8,9},{10,11},{12,13},{14,15},{16,17},{18,19},{..., dimensions={0}, use_global_device_ids=true | all-gather | bytes 294912 | tf_op jit(solution)/shard_map/all_gather | solution.py:453
  60.5 0.0 collective-permute-done.6.ti
  60.5 0.0 collective-permute-done.7.to
  60.5 0.0 collective-permute-done.8.zo
  60.5 0.2 shard_map.92
  60.7 4.7 %collective-permute-start.10 = (f32[24,8,128]{2,1,0:T(8,128)S(1)}, f32[24,8,128]{2,1,0:T(8,128)S(1)}, u32[]{:S(2)}, u32[]{:S(2)}) collective-permute-start(f32[24,8,128]{2,1,0:T(8,128)S(1)} %get-tuple-element.37), channel_id=1, source_target_pairs={{32,64},{96,128},{160,192},{224,256},{288,320},{352,384},{416,448}... | collective-permute-start | bytes 294920 | tf_op jit(solution)/shard_map/ppermute | solution.py:456
  65.4 1.9 %collective-permute-start.11 = (f32[24,8,128]{2,1,0:T(8,128)S(1)}, f32[24,8,128]{2,1,0:T(8,128)S(1)}, u32[]{:S(2)}, u32[]{:S(2)}) collective-permute-start(f32[24,8,128]{2,1,0:T(8,128)S(1)} %get-tuple-element.39), channel_id=1, source_target_pairs={{1,2},{3,4},{5,6},{7,8},{9,10},{11,12},{13,14},{15,16},{17,18},{19... | collective-permute-start | bytes 294920 | tf_op jit(solution)/shard_map/ppermute | solution.py:454
  67.3 3.0 %collective-permute-start.9 = (f32[24,8,128]{2,1,0:T(8,128)S(1)}, f32[24,8,128]{2,1,0:T(8,128)S(1)}, u32[]{:S(2)}, u32[]{:S(2)}) collective-permute-start(f32[24,8,128]{2,1,0:T(8,128)S(1)} %get-tuple-element.36), channel_id=1, source_target_pairs={{0,32},{64,96},{128,160},{192,224},{256,288},{320,352},{384,416},{... | collective-permute-start | bytes 294920 | tf_op jit(solution)/shard_map/ppermute | solution.py:455
  70.4 0.1 add_bitcast_fusion.partner
  70.5 0.1 shard_map.94.modes
  70.6 0.4 shard_map.93.local
  71.0 6.5 %all_gather.15.zi = f32[48,8,128]{2,1,0:T(8,128)S(1)} all-gather(f32[24,8,128]{2,1,0:T(8,128)S(1)} %get-tuple-element.38), channel_id=1, replica_groups={{0,1},{2,3},{4,5},{6,7},{8,9},{10,11},{12,13},{14,15},{16,17},{18,19},{..., dimensions={0}, use_global_device_ids=true | all-gather | bytes 294912 | tf_op jit(solution)/shard_map/all_gather | solution.py:453
  77.5 0.0 collective-permute-done.10.to
  77.6 0.0 collective-permute-done.11.zo
  77.6 0.0 collective-permute-done.9.ti
  77.6 0.4 shard_map.95
  78.0 12.2 %all_to_all.22 = f32[32,1,96]{2,1,0:T(1,128)S(1)} all-to-all(f32[32,1,96]{2,1,0:T(1,128)S(1)} %bitcast.27), channel_id=1, replica_groups=mesh['tm'=24,'space'=32] {'space'}, dimensions={0} | all-to-all | bytes 24576 | tf_op jit(solution)/shard_map/all_to_all | solution.py:533
  90.2 0.5 shard_map.96
  90.7 17.9 %all_to_all.23 = f32[24,1,96]{2,1,0:T(1,128)S(1)} all-to-all(f32[24,1,96]{2,1,0:T(1,128)S(1)} %bitcast.30), channel_id=1, replica_groups=mesh['tm'=24,'space'=32] {'tm'}, dimensions={0} | all-to-all | bytes 18432 | tf_op jit(solution)/shard_map/all_to_all | solution.py:542
  108.6 0.9 shard_map.97
  (13 shorter events, 0.0 us)
Async XLA Ops:
  0.6 0.8 copy-start.2
  1.4 24.3 %copy-start.4 = (s32[8]{0:T(128)S(1)}, s32[8]{0:T(128)}, u32[]{:S(2)}) copy-start(s32[8]{0:T(128)} %param.12) | copy-start | bytes 100
  1.4 24.3 %copy-start.5 = (s32[4]{0:T(128)S(1)}, s32[4]{0:T(128)}, u32[]{:S(2)}) copy-start(s32[4]{0:T(128)} %param.13) | copy-start | bytes 52
  1.4 24.3 %copy-start.3 = (f32[4,3,1,1,6,256]{5,3,4,2,1,0:T(1,128)S(1)}, f32[4,3,1,1,6,256]{5,3,4,2,1,0:T(1,128)}, u32[]{:S(2)}) copy-start(f32[4,3,1,1,6,256]{5,3,4,2,1,0:T(1,128)} %param.8) | copy-start | bytes 221188
  1.4 24.9 %copy-start = (f32[2,6,1,1,12,256]{5,3,4,2,1,0:T(1,128)S(1)}, f32[2,6,1,1,12,256]{5,3,4,2,1,0:T(1,128)}, u32[]{:S(2)}) copy-start(f32[2,6,1,1,12,256]{5,3,4,2,1,0:T(1,128)} %param.9) | copy-start | bytes 442372
  1.5 29.0 %collective-permute-start = (f32[168,128]{1,0:T(8,128)S(1)}, f32[168,128]{1,0:T(8,128)S(1)}, u32[]{:S(2)}, u32[]{:S(2)}) collective-permute-start(f32[168,128]{1,0:T(8,128)S(1)} %pad_maximum_fusion), channel_id=1, source_target_pairs={{0,32},{64,96},{128,160},{192,224},{256,288},{320,352},{384,416},{... | collective-permute-start | bytes 258056 | tf_op jit(solution)/shard_map/ppermute | solution.py:455
  7.1 23.4 %collective-permute-start.1 = (f32[168,128]{1,0:T(8,128)S(1)}, f32[168,128]{1,0:T(8,128)S(1)}, u32[]{:S(2)}, u32[]{:S(2)}) collective-permute-start(f32[168,128]{1,0:T(8,128)S(1)} %pad_maximum_fusion), channel_id=1, source_target_pairs={{32,64},{96,128},{160,192},{224,256},{288,320},{352,384},{416,448}... | collective-permute-start | bytes 258056 | tf_op jit(solution)/shard_map/ppermute | solution.py:456
  21.3 9.1 %collective-permute-start.2 = (f32[168,128]{1,0:T(8,128)S(1)}, f32[168,128]{1,0:T(8,128)S(1)}, u32[]{:S(2)}, u32[]{:S(2)}) collective-permute-start(f32[168,128]{1,0:T(8,128)S(1)} %pad_maximum_fusion), channel_id=1, source_target_pairs={{1,2},{3,4},{5,6},{7,8},{9,10},{11,12},{13,14},{15,16},{17,18},{19... | collective-permute-start | bytes 258056 | tf_op jit(solution)/shard_map/ppermute | solution.py:454
  31.3 14.1 %collective-permute-start.3 = (f32[24,8,128]{2,1,0:T(8,128)S(1)}, f32[24,8,128]{2,1,0:T(8,128)S(1)}, u32[]{:S(2)}, u32[]{:S(2)}) collective-permute-start(f32[24,8,128]{2,1,0:T(8,128)S(1)} %get-tuple-element.26), channel_id=1, source_target_pairs={{0,32},{64,96},{128,160},{192,224},{256,288},{320,352},{384,416},{... | collective-permute-start | bytes 294920 | tf_op jit(solution)/shard_map/ppermute | solution.py:455
  33.3 12.1 %collective-permute-start.4 = (f32[24,8,128]{2,1,0:T(8,128)S(1)}, f32[24,8,128]{2,1,0:T(8,128)S(1)}, u32[]{:S(2)}, u32[]{:S(2)}) collective-permute-start(f32[24,8,128]{2,1,0:T(8,128)S(1)} %get-tuple-element.27), channel_id=1, source_target_pairs={{32,64},{96,128},{160,192},{224,256},{288,320},{352,384},{416,448}... | collective-permute-start | bytes 294920 | tf_op jit(solution)/shard_map/ppermute | solution.py:456
  38.1 7.3 %collective-permute-start.5 = (f32[24,8,128]{2,1,0:T(8,128)S(1)}, f32[24,8,128]{2,1,0:T(8,128)S(1)}, u32[]{:S(2)}, u32[]{:S(2)}) collective-permute-start(f32[24,8,128]{2,1,0:T(8,128)S(1)} %get-tuple-element.29), channel_id=1, source_target_pairs={{1,2},{3,4},{5,6},{7,8},{9,10},{11,12},{13,14},{15,16},{17,18},{19... | collective-permute-start | bytes 294920 | tf_op jit(solution)/shard_map/ppermute | solution.py:454
  45.6 14.8 %collective-permute-start.6 = (f32[24,8,128]{2,1,0:T(8,128)S(1)}, f32[24,8,128]{2,1,0:T(8,128)S(1)}, u32[]{:S(2)}, u32[]{:S(2)}) collective-permute-start(f32[24,8,128]{2,1,0:T(8,128)S(1)} %get-tuple-element.31), channel_id=1, source_target_pairs={{0,32},{64,96},{128,160},{192,224},{256,288},{320,352},{384,416},{... | collective-permute-start | bytes 294920 | tf_op jit(solution)/shard_map/ppermute | solution.py:455
  48.2 6.2 %copy-start.6 = (s32[48]{0:T(128)S(1)}, s32[48]{0:T(128)}, u32[]{:S(2)}) copy-start(s32[48]{0:T(128)} %param.11) | copy-start | bytes 580
  48.2 12.3 %collective-permute-start.7 = (f32[24,8,128]{2,1,0:T(8,128)S(1)}, f32[24,8,128]{2,1,0:T(8,128)S(1)}, u32[]{:S(2)}, u32[]{:S(2)}) collective-permute-start(f32[24,8,128]{2,1,0:T(8,128)S(1)} %get-tuple-element.32), channel_id=1, source_target_pairs={{32,64},{96,128},{160,192},{224,256},{288,320},{352,384},{416,448}... | collective-permute-start | bytes 294920 | tf_op jit(solution)/shard_map/ppermute | solution.py:456
  52.5 8.0 %collective-permute-start.8 = (f32[24,8,128]{2,1,0:T(8,128)S(1)}, f32[24,8,128]{2,1,0:T(8,128)S(1)}, u32[]{:S(2)}, u32[]{:S(2)}) collective-permute-start(f32[24,8,128]{2,1,0:T(8,128)S(1)} %get-tuple-element.34), channel_id=1, source_target_pairs={{1,2},{3,4},{5,6},{7,8},{9,10},{11,12},{13,14},{15,16},{17,18},{19... | collective-permute-start | bytes 294920 | tf_op jit(solution)/shard_map/ppermute | solution.py:454
  60.5 10.0 %copy-start.1 = (f32[48,1,1,6,256]{4,2,3,1,0:T(1,128)S(1)}, f32[48,1,1,6,256]{4,2,3,1,0:T(1,128)}, u32[]{:S(2)}) copy-start(f32[48,1,1,6,256]{4,2,3,1,0:T(1,128)} %param.10) | copy-start | bytes 884740
  60.7 16.8 %collective-permute-start.10 = (f32[24,8,128]{2,1,0:T(8,128)S(1)}, f32[24,8,128]{2,1,0:T(8,128)S(1)}, u32[]{:S(2)}, u32[]{:S(2)}) collective-permute-start(f32[24,8,128]{2,1,0:T(8,128)S(1)} %get-tuple-element.37), channel_id=1, source_target_pairs={{32,64},{96,128},{160,192},{224,256},{288,320},{352,384},{416,448}... | collective-permute-start | bytes 294920 | tf_op jit(solution)/shard_map/ppermute | solution.py:456
  65.4 12.2 %collective-permute-start.11 = (f32[24,8,128]{2,1,0:T(8,128)S(1)}, f32[24,8,128]{2,1,0:T(8,128)S(1)}, u32[]{:S(2)}, u32[]{:S(2)}) collective-permute-start(f32[24,8,128]{2,1,0:T(8,128)S(1)} %get-tuple-element.39), channel_id=1, source_target_pairs={{1,2},{3,4},{5,6},{7,8},{9,10},{11,12},{13,14},{15,16},{17,18},{19... | collective-permute-start | bytes 294920 | tf_op jit(solution)/shard_map/ppermute | solution.py:454
  67.3 10.2 %collective-permute-start.9 = (f32[24,8,128]{2,1,0:T(8,128)S(1)}, f32[24,8,128]{2,1,0:T(8,128)S(1)}, u32[]{:S(2)}, u32[]{:S(2)}) collective-permute-start(f32[24,8,128]{2,1,0:T(8,128)S(1)} %get-tuple-element.36), channel_id=1, source_target_pairs={{0,32},{64,96},{128,160},{192,224},{256,288},{320,352},{384,416},{... | collective-permute-start | bytes 294920 | tf_op jit(solution)/shard_map/ppermute | solution.py:455

commit v5 on v4

--- a/solution.py
+++ b/solution.py
@@ -154,7 +154,7 @@
     return jnp.where(crosses, phase, 0.5 * step_size)
 
 
-def prepare_kernel(sizes, time_rank, space_rank, bits, noise, links_in, links, source):
+def prepare_kernel(sizes, time_rank, space_rank, bits, packed, links, source):
     lane = lax.broadcasted_iota(jnp.int32, (8, LANES), 1)
     row = lax.broadcasted_iota(jnp.int32, (8, LANES), 0)
     at_x = hop_factor(bits, 0, lane % SIDE == SIDE - 1)
@@ -167,10 +167,11 @@
         scale = scales[first]
         if last != first:
             scale = jnp.where(row + block * 8 >= last * 36, scales[last], scale)
-        links[block * 8 : block * 8 + 8, :] = links_in[block * 8 : block * 8 + 8, :] * scale
+        from_row = 8 * block + (168 if block < 9 else 24)
+        links[block * 8 : block * 8 + 8, :] = packed[from_row : from_row + 8, :] * scale
     weight = source_weight(bits, time_rank[0])
     for plane in range(12):
-        source[plane] = noise[pl.ds(plane, 8, stride=12), :] * weight
+        source[plane] = packed[pl.ds(plane, 8, stride=12), :] * weight
 
 
 def shift_x(value, forward):
@@ -399,19 +400,22 @@
         out[pl.ds(spin, 8, stride=4), :] = total[8 * spin : 8 * spin + 8, : out.shape[1]]
 
 
-def sum_kernel(parts, out, copies):
+def sum_kernel(parts, copies):
     total = jnp.sum(parts[...], axis=0, keepdims=True)
-    out[...] = total
     copies[...] = jnp.broadcast_to(total, copies.shape)
 
 
-def correlate_kernel(time_rank, rows, partner, out):
+def correlate_kernel(place, gathered, partner, row, out, rows):
     size = rows.shape[1]
+    for time in range(rows.shape[0]):
+        rows[time : time + 1, :] = gathered[swapped(time) : swapped(time) + 1, :]
+    mine = rows[pl.ds(place[0], 1), :]
+    row[...] = mine
     onehot = (
         partner[...] == lax.broadcasted_iota(jnp.int32, (size, size), 0)
     ).astype(F32)
     contract = (((1,), (1,)), ((), ()))
-    own = jnp.broadcast_to(rows[pl.ds(time_rank[0], 1), :], (8, size))
+    own = jnp.broadcast_to(mine, (8, size))
     weighted = lax.dot_general(
         own, onehot, contract, precision=lax.Precision.HIGHEST, preferred_element_type=F32
     )
@@ -443,17 +447,24 @@
     return jax.ShapeDtypeStruct((count, 8, LANES), F32)
 
 
+def swapped(index):
+    return index ^ ((index // 2) % 2)
+
+
+def swap(axis, shift, place=lambda index: index):
+    size = lax.axis_size(axis)
+    pairs = [(place((i + shift) % size), place((i + 1 + shift) % size)) for i in range(0, size, 2)]
+    return pairs + [(j, i) for i, j in pairs]
+
+
 def exchange(t_inner, t_outer, z_inner, z_outer):
-    def swap(axis, shift):
-        size = lax.axis_size(axis)
-        pairs = [((i + shift) % size, (i + 1 + shift) % size) for i in range(0, size, 2)]
-        return pairs + [(j, i) for i, j in pairs]
-
     pairs = [[i, i + 1] for i in range(0, lax.axis_size("space"), 2)]
     zi = lax.all_gather(z_inner, "space", axis_index_groups=pairs, tiled=True)
     zo = lax.ppermute(z_outer, "space", swap("space", 1))
+    to = lax.ppermute(t_outer, "tm", swap("tm", 1, swapped))
+    if t_inner is None:
+        return to, zi, zo
     ti = lax.ppermute(t_inner, "tm", swap("tm", 0))
-    to = lax.ppermute(t_outer, "tm", swap("tm", 1))
     return ti, to, zi, zo
 
 
@@ -467,7 +478,9 @@
     links_in = gauge_links.reshape(-1, LANES)
     clover = clover.reshape(-1, LANES)
     modes_in = eigvecs.reshape(-1, LANES)
-    ranks = mesh_ranks()
+    place, space_rank = mesh_ranks()
+    moved = (place[0] // 2) % 2 == 1
+    ranks = (swapped(place), space_rank)
     sizes = (lax.axis_size("tm"), lax.axis_size("space"))
     bits = jnp.concatenate([boundary, dilution])
 
@@ -477,28 +490,37 @@
     def step_first(*refs):
         step_first_kernel(sizes, *refs)
 
-    packed = jnp.concatenate([noise, links_in[links_in.shape[0] // 2 :]])
-    sends = (packed,) * 4
+    cut = links_in.shape[0] // 2
+    packed = jnp.concatenate([noise, links_in[cut:], links_in[:cut]])
+    other = lax.ppermute(packed, "tm", swap("tm", 0))
+    other_clover = lax.ppermute(clover, "tm", swap("tm", 0))
+    block, pair = jnp.where(moved, other, packed), jnp.where(moved, packed, other)
+    clover = jnp.where(moved, other_clover, clover)
+    block_sent = block[: packed.shape[0] - cut]
     solution = None
     for iteration in range(ITERS):
-        arrived = exchange(*sends)
+        if iteration == 0:
+            arrived = (pair, *exchange(None, block_sent, block_sent, block_sent))
+        else:
+            arrived = exchange(*sends)
+        if iteration == 1:
+            other_modes = lax.ppermute(modes_in, "tm", swap("tm", 0))
+            modes = call(
+                modes_kernel,
+                jax.ShapeDtypeStruct((6, 256, 256), jnp.bfloat16),
+                10**6,
+                (),
+                jnp.where(moved, other_modes, modes_in),
+            )
         if iteration == 0:
             links, source = call(
                 prepare,
                 [jax.ShapeDtypeStruct(links_in.shape, F32), vectors(12)],
                 10**6,
                 (*ranks, bits),
-                noise,
-                links_in,
+                block,
             )
             local = call(local_first_kernel, vectors(48), 5 * 10**6, (), links, clover, source)
-            modes = call(
-                modes_kernel,
-                jax.ShapeDtypeStruct((6, 256, 256), jnp.bfloat16),
-                10**6,
-                (),
-                modes_in,
-            )
         else:
             local = call(local_kernel, vectors(48), 5 * 10**6, (), solution, links, clover, source)
         if iteration < ITERS - 1:
@@ -531,17 +553,19 @@
     both = jnp.concatenate([partner, partner + count]).reshape(1, 2 * count)
     both, partial_sums = lax.optimization_barrier((both, partial_sums))
     parts = lax.all_to_all(partial_sums, "space", 0, 0, tiled=True)
-    times, ranks = lax.axis_size("tm"), mesh_ranks()[:1]
-    row, copies = call(
-        sum_kernel,
-        [jax.ShapeDtypeStruct((n, 2 * count), F32) for n in (1, times)],
-        10**4,
-        (),
-        parts,
-    )
-    rows = lax.all_to_all(copies, "tm", 0, 0, tiled=True)
-    correlator = call(
-        correlate_kernel, jax.ShapeDtypeStruct((1, times), F32), 10**5, ranks, rows, both
+    times = lax.axis_size("tm")
+    copies = call(
+        sum_kernel, jax.ShapeDtypeStruct((times, 2 * count), F32), 10**4, (), parts
+    )
+    gathered = lax.all_to_all(copies, "tm", 0, 0, tiled=True)
+    row, correlator = call(
+        correlate_kernel,
+        [jax.ShapeDtypeStruct((1, n), F32) for n in (2 * count, times)],
+        10**5,
+        mesh_ranks()[:1],
+        gathered,
+        both,
+        scratch=[pltpu.VMEM((times, 2 * count), F32)],
     )
     return row.reshape(1, 1, 2 * count), correlator.reshape(1, 1, times)
 

time: 110 us -> 115 us (1.045)
  starting transfers between devices: 51.4 us -> 56.5 us
    ppermute x4 -> x7, starting transfers between devices: 28 us -> 36 us  [the longest x4 23.8 us: exchange(): to = lax.ppermute(t_outer, 'tm', swap('tm', 1, swapped))]
    all_gather x4, blocking collectives: 20.5 us -> 16.1 us  [exchange(): zi = lax.all_gather(z_inner, 'space', axis_index_groups=pairs, tiled=True)]
    ppermute x4 -> x3, starting transfers between devices: 13.1 us -> 9.46 us  [exchange(): ti = lax.ppermute(t_inner, 'tm', swap('tm', 0))]
    all_to_all x1, blocking collectives: 12.2 us -> 14.7 us  [shards(): parts = lax.all_to_all(partial_sums, 'space', 0, 0, tiled=True)]
    all_to_all x1, blocking collectives: 17.9 us -> 19.3 us  [shards(): gathered = lax.all_to_all(copies, 'tm', 0, 0, tiled=True)]
  transfers between devices with their start and end apart: 12 -> 14, of which waited for: 0 -> 0; matrix products, arithmetic and copies ran while one was open for 0% -> 0% of each run, Pallas kernels for 2% -> 3%
where the time goes in v5:
time: 115 us
  starting transfers between devices  56.5 us (49%)
  blocking collectives  50.2 us (44%)
  Pallas kernels  5.09 us (4%)
  local copies, waits for them, and re-layouts  1.53 us (1%)
    ppermute x4, starting transfers between devices, exchange(): to = lax.ppermute(t_outer, 'tm', swap('tm', 1, swapped))  23.8 us
    all_to_all x1, blocking collectives, shards(): gathered = lax.all_to_all(copies, 'tm', 0, 0, tiled=True)  19.3 us
    all_gather x4, blocking collectives, exchange(): zi = lax.all_gather(z_inner, 'space', axis_index_groups=pairs, tiled=True)  16.1 us
    all_to_all x1, blocking collectives, shards(): parts = lax.all_to_all(partial_sums, 'space', 0, 0, tiled=True)  14.7 us
    ppermute x4, starting transfers between devices, exchange(): zo = lax.ppermute(z_outer, 'space', swap('space', 1))  11 us
    ppermute x3, starting transfers between devices, exchange(): ti = lax.ppermute(t_inner, 'tm', swap('tm', 0))  9.46 us
    ppermute x1, starting transfers between devices, partial_rows(): other = lax.ppermute(packed, 'tm', swap('tm', 0))  5.47 us
    pallas_call x12, Pallas kernels, call(): pl.pallas_call(kernel, out_shape=outs, in_specs=[smem] * len(scalars) + [...  5.09 us
  transfers between devices with their start and end apart: 14, of which 0 were waited for; matrix products, arithmetic and copies ran while one was open for 0% of the time, Pallas kernels for 3%

profile of v5, /device:TPU:1, one launch (start us, length us, event | category | flops | bytes accessed | tf_op | source)
XLA Modules:
  0.0 114.6 jit_solution(15173684972685687887)
XLA Ops:
  0.6 0.8 fusion
  1.5 5.5 %collective-permute-start = (f32[240,128]{1,0:T(8,128)S(1)}, f32[240,128]{1,0:T(8,128)S(1)}, u32[]{:S(2)}, u32[]{:S(2)}) collective-permute-start(f32[240,128]{1,0:T(8,128)S(1)} %pad_maximum_fusion), channel_id=1, source_target_pairs={{0,32},{64,96},{128,160},{192,224},{256,288},{320,352},{384,416},{... | collective-permute-start | bytes 368648 | tf_op jit(solution)/shard_map/ppermute | solution.py:495
  7.0 1.9 %collective-permute-start.1 = (f32[288,128]{1,0:T(8,128)}, f32[288,128]{1,0:T(8,128)S(1)}, u32[]{:S(2)}, u32[]{:S(2)}) collective-permute-start(f32[288,128]{1,0:T(8,128)} %bitcast.31), channel_id=1, source_target_pairs={{0,32},{64,96},{128,160},{192,224},{256,288},{320,352},{384,416},{... | collective-permute-start | bytes 442376 | tf_op jit(solution)/shard_map/ppermute | solution.py:496
  8.9 4.9 %collective-permute-start.13 = (f32[576,128]{1,0:T(8,128)S(1)}, f32[576,128]{1,0:T(8,128)S(1)}, u32[]{:S(2)}, u32[]{:S(2)}) collective-permute-start(f32[576,128]{1,0:T(8,128)S(1)} %bitcast.27), channel_id=1, source_target_pairs={{0,32},{64,96},{128,160},{192,224},{256,288},{320,352},{384,416},{... | collective-permute-start | bytes 884744 | tf_op jit(solution)/shard_map/ppermute | solution.py:507
  13.9 0.0 copy-start.3
  13.9 0.0 copy-start.4
  13.9 0.6 copy-done.3
  14.5 0.0 copy-done.4
  14.5 0.1 pad_add_fusion.refs_2_
  14.6 0.0 collective-permute-done
  14.7 14.3 %collective-permute-start.2 = (f32[168,128]{1,0:T(8,128)S(1)}, f32[168,128]{1,0:T(8,128)S(1)}, u32[]{:S(2)}, u32[]{:S(2)}) collective-permute-start(f32[168,128]{1,0:T(8,128)S(1)} %slice.20), channel_id=1, source_target_pairs={{32,96},{64,128},{160,224},{192,256},{288,352},{320,384},{416,480}... | collective-permute-start | bytes 258056 | tf_op jit(solution)/shard_map/ppermute | solution.py:464
  29.0 4.9 %collective-permute-start.3 = (f32[168,128]{1,0:T(8,128)S(1)}, f32[168,128]{1,0:T(8,128)S(1)}, u32[]{:S(2)}, u32[]{:S(2)}) collective-permute-start(f32[168,128]{1,0:T(8,128)S(1)} %slice.20), channel_id=1, source_target_pairs={{1,2},{3,4},{5,6},{7,8},{9,10},{11,12},{13,14},{15,16},{17,18},{19... | collective-permute-start | bytes 258056 | tf_op jit(solution)/shard_map/ppermute | solution.py:463
  33.9 0.6 shard_map.86
  34.4 0.0 copy-start.2
  34.5 2.3 %all_gather.12.refs_7_ = f32[336,128]{1,0:T(8,128)S(1)} all-gather(f32[168,128]{1,0:T(8,128)S(1)} %slice.20), channel_id=1, replica_groups={{0,1},{2,3},{4,5},{6,7},{8,9},{10,11},{12,13},{14,15},{16,17},{18,19},{..., dimensions={0}, use_global_device_ids=true | all-gather | bytes 258048 | tf_op jit(solution)/shard_map/all_gather | solution.py:462
  36.8 0.0 collective-permute-done.1
  36.8 0.4 shard_map.87.refs_3_
  37.3 0.9 shard_map.88
  38.2 1.9 %collective-permute-start.4 = (f32[24,8,128]{2,1,0:T(8,128)S(1)}, f32[24,8,128]{2,1,0:T(8,128)S(1)}, u32[]{:S(2)}, u32[]{:S(2)}) collective-permute-start(f32[24,8,128]{2,1,0:T(8,128)S(1)} %get-tuple-element.26), channel_id=1, source_target_pairs={{0,32},{64,96},{128,160},{192,224},{256,288},{320,352},{384,416},{... | collective-permute-start | bytes 294920 | tf_op jit(solution)/shard_map/ppermute | solution.py:467
  40.1 0.0 copy-start.5
  40.1 3.9 %collective-permute-start.5 = (f32[24,8,128]{2,1,0:T(8,128)S(1)}, f32[24,8,128]{2,1,0:T(8,128)S(1)}, u32[]{:S(2)}, u32[]{:S(2)}) collective-permute-start(f32[24,8,128]{2,1,0:T(8,128)S(1)} %get-tuple-element.27), channel_id=1, source_target_pairs={{32,96},{64,128},{160,224},{192,256},{288,352},{320,384},{416,480}... | collective-permute-start | bytes 294920 | tf_op jit(solution)/shard_map/ppermute | solution.py:464
  44.0 2.0 %collective-permute-start.6 = (f32[24,8,128]{2,1,0:T(8,128)S(1)}, f32[24,8,128]{2,1,0:T(8,128)S(1)}, u32[]{:S(2)}, u32[]{:S(2)}) collective-permute-start(f32[24,8,128]{2,1,0:T(8,128)S(1)} %get-tuple-element.29), channel_id=1, source_target_pairs={{1,2},{3,4},{5,6},{7,8},{9,10},{11,12},{13,14},{15,16},{17,18},{19... | collective-permute-start | bytes 294920 | tf_op jit(solution)/shard_map/ppermute | solution.py:463
  46.0 0.5 shard_map.89.local
  46.5 4.1 %all_gather.13.zi = f32[48,8,128]{2,1,0:T(8,128)S(1)} all-gather(f32[24,8,128]{2,1,0:T(8,128)S(1)} %get-tuple-element.28), channel_id=1, replica_groups={{0,1},{2,3},{4,5},{6,7},{8,9},{10,11},{12,13},{14,15},{16,17},{18,19},{..., dimensions={0}, use_global_device_ids=true | all-gather | bytes 294912 | tf_op jit(solution)/shard_map/all_gather | solution.py:462
  50.6 0.0 collective-permute-done.4.ti
  50.6 0.2 shard_map.90
  50.9 4.1 %collective-permute-start.7 = (f32[24,8,128]{2,1,0:T(8,128)S(1)}, f32[24,8,128]{2,1,0:T(8,128)S(1)}, u32[]{:S(2)}, u32[]{:S(2)}) collective-permute-start(f32[24,8,128]{2,1,0:T(8,128)S(1)} %get-tuple-element.31), channel_id=1, source_target_pairs={{0,32},{64,96},{128,160},{192,224},{256,288},{320,352},{384,416},{... | collective-permute-start | bytes 294920 | tf_op jit(solution)/shard_map/ppermute | solution.py:467
  55.0 2.4 %collective-permute-start.8 = (f32[24,8,128]{2,1,0:T(8,128)S(1)}, f32[24,8,128]{2,1,0:T(8,128)S(1)}, u32[]{:S(2)}, u32[]{:S(2)}) collective-permute-start(f32[24,8,128]{2,1,0:T(8,128)S(1)} %get-tuple-element.32), channel_id=1, source_target_pairs={{32,96},{64,128},{160,224},{192,256},{288,352},{320,384},{416,480}... | collective-permute-start | bytes 294920 | tf_op jit(solution)/shard_map/ppermute | solution.py:464
  57.4 2.2 %collective-permute-start.9 = (f32[24,8,128]{2,1,0:T(8,128)S(1)}, f32[24,8,128]{2,1,0:T(8,128)S(1)}, u32[]{:S(2)}, u32[]{:S(2)}) collective-permute-start(f32[24,8,128]{2,1,0:T(8,128)S(1)} %get-tuple-element.34), channel_id=1, source_target_pairs={{1,2},{3,4},{5,6},{7,8},{9,10},{11,12},{13,14},{15,16},{17,18},{19... | collective-permute-start | bytes 294920 | tf_op jit(solution)/shard_map/ppermute | solution.py:463
  59.6 0.1 add_bitcast_fusion.partner
  59.7 0.4 shard_map.91.local
  60.1 4.7 %all_gather.14.zi = f32[48,8,128]{2,1,0:T(8,128)S(1)} all-gather(f32[24,8,128]{2,1,0:T(8,128)S(1)} %get-tuple-element.33), channel_id=1, replica_groups={{0,1},{2,3},{4,5},{6,7},{8,9},{10,11},{12,13},{14,15},{16,17},{18,19},{..., dimensions={0}, use_global_device_ids=true | all-gather | bytes 294912 | tf_op jit(solution)/shard_map/all_gather | solution.py:462
  64.9 0.0 collective-permute-done.7.ti
  64.9 0.0 collective-permute-done.8.to
  64.9 0.0 collective-permute-done.9.zo
  64.9 0.2 shard_map.92
  65.1 3.4 %collective-permute-start.10 = (f32[24,8,128]{2,1,0:T(8,128)S(1)}, f32[24,8,128]{2,1,0:T(8,128)S(1)}, u32[]{:S(2)}, u32[]{:S(2)}) collective-permute-start(f32[24,8,128]{2,1,0:T(8,128)S(1)} %get-tuple-element.36), channel_id=1, source_target_pairs={{0,32},{64,96},{128,160},{192,224},{256,288},{320,352},{384,416},{... | collective-permute-start | bytes 294920 | tf_op jit(solution)/shard_map/ppermute | solution.py:467
  68.6 3.1 %collective-permute-start.11 = (f32[24,8,128]{2,1,0:T(8,128)S(1)}, f32[24,8,128]{2,1,0:T(8,128)S(1)}, u32[]{:S(2)}, u32[]{:S(2)}) collective-permute-start(f32[24,8,128]{2,1,0:T(8,128)S(1)} %get-tuple-element.37), channel_id=1, source_target_pairs={{32,96},{64,128},{160,224},{192,256},{288,352},{320,384},{416,480}... | collective-permute-start | bytes 294920 | tf_op jit(solution)/shard_map/ppermute | solution.py:464
  71.7 1.9 %collective-permute-start.12 = (f32[24,8,128]{2,1,0:T(8,128)S(1)}, f32[24,8,128]{2,1,0:T(8,128)S(1)}, u32[]{:S(2)}, u32[]{:S(2)}) collective-permute-start(f32[24,8,128]{2,1,0:T(8,128)S(1)} %get-tuple-element.39), channel_id=1, source_target_pairs={{1,2},{3,4},{5,6},{7,8},{9,10},{11,12},{13,14},{15,16},{17,18},{19... | collective-permute-start | bytes 294920 | tf_op jit(solution)/shard_map/ppermute | solution.py:463
  73.7 0.1 shard_map.94.modes
  73.8 0.4 shard_map.93.local
  74.3 5.0 %all_gather.15.zi = f32[48,8,128]{2,1,0:T(8,128)S(1)} all-gather(f32[24,8,128]{2,1,0:T(8,128)S(1)} %get-tuple-element.38), channel_id=1, replica_groups={{0,1},{2,3},{4,5},{6,7},{8,9},{10,11},{12,13},{14,15},{16,17},{18,19},{..., dimensions={0}, use_global_device_ids=true | all-gather | bytes 294912 | tf_op jit(solution)/shard_map/all_gather | solution.py:462
  79.3 0.0 collective-permute-done.11.to
  79.3 0.0 collective-permute-done.12.zo
  79.3 0.4 shard_map.95
  79.7 14.7 %all_to_all.22 = f32[32,1,96]{2,1,0:T(1,128)S(1)} all-to-all(f32[32,1,96]{2,1,0:T(1,128)S(1)} %bitcast.19), channel_id=1, replica_groups=mesh['tm'=24,'space'=32] {'space'}, dimensions={0} | all-to-all | bytes 24576 | tf_op jit(solution)/shard_map/all_to_all | solution.py:555
  94.4 19.3 %all_to_all.23 = f32[24,1,96]{2,1,0:T(1,128)S(1)} all-to-all(f32[24,1,96]{2,1,0:T(1,128)S(1)} %bitcast.21), channel_id=1, replica_groups=mesh['tm'=24,'space'=32] {'tm'}, dimensions={0} | all-to-all | bytes 18432 | tf_op jit(solution)/shard_map/all_to_all | solution.py:560
  113.7 0.9 shard_map.97
  (19 shorter events, 0.1 us)
Async XLA Ops:
  0.6 0.9 copy-start.1
  0.6 8.3 %copy-start = (f32[48,1,1,6,256]{4,2,3,1,0:T(1,128)S(1)}, f32[48,1,1,6,256]{4,2,3,1,0:T(1,128)}, u32[]{:S(2)}) copy-start(f32[48,1,1,6,256]{4,2,3,1,0:T(1,128)} %param.10) | copy-start | bytes 884740
  1.5 13.1 %collective-permute-start = (f32[240,128]{1,0:T(8,128)S(1)}, f32[240,128]{1,0:T(8,128)S(1)}, u32[]{:S(2)}, u32[]{:S(2)}) collective-permute-start(f32[240,128]{1,0:T(8,128)S(1)} %pad_maximum_fusion), channel_id=1, source_target_pairs={{0,32},{64,96},{128,160},{192,224},{256,288},{320,352},{384,416},{... | collective-permute-start | bytes 368648 | tf_op jit(solution)/shard_map/ppermute | solution.py:495
  7.0 29.8 %collective-permute-start.1 = (f32[288,128]{1,0:T(8,128)}, f32[288,128]{1,0:T(8,128)S(1)}, u32[]{:S(2)}, u32[]{:S(2)}) collective-permute-start(f32[288,128]{1,0:T(8,128)} %bitcast.31), channel_id=1, source_target_pairs={{0,32},{64,96},{128,160},{192,224},{256,288},{320,352},{384,416},{... | collective-permute-start | bytes 442376 | tf_op jit(solution)/shard_map/ppermute | solution.py:496
  8.9 64.7 %collective-permute-start.13 = (f32[576,128]{1,0:T(8,128)S(1)}, f32[576,128]{1,0:T(8,128)S(1)}, u32[]{:S(2)}, u32[]{:S(2)}) collective-permute-start(f32[576,128]{1,0:T(8,128)S(1)} %bitcast.27), channel_id=1, source_target_pairs={{0,32},{64,96},{128,160},{192,224},{256,288},{320,352},{384,416},{... | collective-permute-start | bytes 884744 | tf_op jit(solution)/shard_map/ppermute | solution.py:507
  13.9 0.7 copy-start.3
  13.9 0.7 copy-start.4
  14.7 22.6 %collective-permute-start.2 = (f32[168,128]{1,0:T(8,128)S(1)}, f32[168,128]{1,0:T(8,128)S(1)}, u32[]{:S(2)}, u32[]{:S(2)}) collective-permute-start(f32[168,128]{1,0:T(8,128)S(1)} %slice.20), channel_id=1, source_target_pairs={{32,96},{64,128},{160,224},{192,256},{288,352},{320,384},{416,480}... | collective-permute-start | bytes 258056 | tf_op jit(solution)/shard_map/ppermute | solution.py:464
  29.0 8.3 %collective-permute-start.3 = (f32[168,128]{1,0:T(8,128)S(1)}, f32[168,128]{1,0:T(8,128)S(1)}, u32[]{:S(2)}, u32[]{:S(2)}) collective-permute-start(f32[168,128]{1,0:T(8,128)S(1)} %slice.20), channel_id=1, source_target_pairs={{1,2},{3,4},{5,6},{7,8},{9,10},{11,12},{13,14},{15,16},{17,18},{19... | collective-permute-start | bytes 258056 | tf_op jit(solution)/shard_map/ppermute | solution.py:463
  34.4 2.4 %copy-start.2 = (f32[2,6,1,1,12,256]{5,3,4,2,1,0:T(1,128)S(1)}, f32[2,6,1,1,12,256]{5,3,4,2,1,0:T(1,128)}, u32[]{:S(2)}) copy-start(f32[2,6,1,1,12,256]{5,3,4,2,1,0:T(1,128)} %param.9) | copy-start | bytes 442372
  38.2 12.4 %collective-permute-start.4 = (f32[24,8,128]{2,1,0:T(8,128)S(1)}, f32[24,8,128]{2,1,0:T(8,128)S(1)}, u32[]{:S(2)}, u32[]{:S(2)}) collective-permute-start(f32[24,8,128]{2,1,0:T(8,128)S(1)} %get-tuple-element.26), channel_id=1, source_target_pairs={{0,32},{64,96},{128,160},{192,224},{256,288},{320,352},{384,416},{... | collective-permute-start | bytes 294920 | tf_op jit(solution)/shard_map/ppermute | solution.py:467
  40.1 6.0 %copy-start.5 = (s32[48]{0:T(128)S(1)}, s32[48]{0:T(128)}, u32[]{:S(2)}) copy-start(s32[48]{0:T(128)} %param.11) | copy-start | bytes 580
  40.1 10.5 %collective-permute-start.5 = (f32[24,8,128]{2,1,0:T(8,128)S(1)}, f32[24,8,128]{2,1,0:T(8,128)S(1)}, u32[]{:S(2)}, u32[]{:S(2)}) collective-permute-start(f32[24,8,128]{2,1,0:T(8,128)S(1)} %get-tuple-element.27), channel_id=1, source_target_pairs={{32,96},{64,128},{160,224},{192,256},{288,352},{320,384},{416,480}... | collective-permute-start | bytes 294920 | tf_op jit(solution)/shard_map/ppermute | solution.py:464
  44.0 6.6 %collective-permute-start.6 = (f32[24,8,128]{2,1,0:T(8,128)S(1)}, f32[24,8,128]{2,1,0:T(8,128)S(1)}, u32[]{:S(2)}, u32[]{:S(2)}) collective-permute-start(f32[24,8,128]{2,1,0:T(8,128)S(1)} %get-tuple-element.29), channel_id=1, source_target_pairs={{1,2},{3,4},{5,6},{7,8},{9,10},{11,12},{13,14},{15,16},{17,18},{19... | collective-permute-start | bytes 294920 | tf_op jit(solution)/shard_map/ppermute | solution.py:463
  50.9 14.0 %collective-permute-start.7 = (f32[24,8,128]{2,1,0:T(8,128)S(1)}, f32[24,8,128]{2,1,0:T(8,128)S(1)}, u32[]{:S(2)}, u32[]{:S(2)}) collective-permute-start(f32[24,8,128]{2,1,0:T(8,128)S(1)} %get-tuple-element.31), channel_id=1, source_target_pairs={{0,32},{64,96},{128,160},{192,224},{256,288},{320,352},{384,416},{... | collective-permute-start | bytes 294920 | tf_op jit(solution)/shard_map/ppermute | solution.py:467
  55.0 9.9 %collective-permute-start.8 = (f32[24,8,128]{2,1,0:T(8,128)S(1)}, f32[24,8,128]{2,1,0:T(8,128)S(1)}, u32[]{:S(2)}, u32[]{:S(2)}) collective-permute-start(f32[24,8,128]{2,1,0:T(8,128)S(1)} %get-tuple-element.32), channel_id=1, source_target_pairs={{32,96},{64,128},{160,224},{192,256},{288,352},{320,384},{416,480}... | collective-permute-start | bytes 294920 | tf_op jit(solution)/shard_map/ppermute | solution.py:464
  57.4 7.5 %collective-permute-start.9 = (f32[24,8,128]{2,1,0:T(8,128)S(1)}, f32[24,8,128]{2,1,0:T(8,128)S(1)}, u32[]{:S(2)}, u32[]{:S(2)}) collective-permute-start(f32[24,8,128]{2,1,0:T(8,128)S(1)} %get-tuple-element.34), channel_id=1, source_target_pairs={{1,2},{3,4},{5,6},{7,8},{9,10},{11,12},{13,14},{15,16},{17,18},{19... | collective-permute-start | bytes 294920 | tf_op jit(solution)/shard_map/ppermute | solution.py:463
  65.1 14.1 %collective-permute-start.10 = (f32[24,8,128]{2,1,0:T(8,128)S(1)}, f32[24,8,128]{2,1,0:T(8,128)S(1)}, u32[]{:S(2)}, u32[]{:S(2)}) collective-permute-start(f32[24,8,128]{2,1,0:T(8,128)S(1)} %get-tuple-element.36), channel_id=1, source_target_pairs={{0,32},{64,96},{128,160},{192,224},{256,288},{320,352},{384,416},{... | collective-permute-start | bytes 294920 | tf_op jit(solution)/shard_map/ppermute | solution.py:467
  68.6 10.7 %collective-permute-start.11 = (f32[24,8,128]{2,1,0:T(8,128)S(1)}, f32[24,8,128]{2,1,0:T(8,128)S(1)}, u32[]{:S(2)}, u32[]{:S(2)}) collective-permute-start(f32[24,8,128]{2,1,0:T(8,128)S(1)} %get-tuple-element.37), channel_id=1, source_target_pairs={{32,96},{64,128},{160,224},{192,256},{288,352},{320,384},{416,480}... | collective-permute-start | bytes 294920 | tf_op jit(solution)/shard_map/ppermute | solution.py:464
  71.7 7.6 %collective-permute-start.12 = (f32[24,8,128]{2,1,0:T(8,128)S(1)}, f32[24,8,128]{2,1,0:T(8,128)S(1)}, u32[]{:S(2)}, u32[]{:S(2)}) collective-permute-start(f32[24,8,128]{2,1,0:T(8,128)S(1)} %get-tuple-element.39), channel_id=1, source_target_pairs={{1,2},{3,4},{5,6},{7,8},{9,10},{11,12},{13,14},{15,16},{17,18},{19... | collective-permute-start | bytes 294920 | tf_op jit(solution)/shard_map/ppermute | solution.py:463

commit v6 on v5

--- a/solution.py
+++ b/solution.py
@@ -306,7 +306,9 @@
     ]
 
 
-def step_body(received, time_rank, space_rank, local, links, solution, *sends):
+def step_body(received, time_rank, space_rank, local, links, carried, solution, *sends):
+    if carried is not None:
+        sends[0][24:] = carried[...]
     for comp in range(2):
         for half in range(2):
             top, bottom = hops(local, links, received, comp, half)
@@ -323,7 +325,7 @@
 
 
 def step_first_kernel(sizes, time_rank, space_rank, bits, local, links, ti, to, zi, zo,
-                      solution, sti, sto, szi, szo, at, bt, az, bz):
+                      carried, solution, sti, sto, szi, szo, at, bt, az, bz):
     time, space = time_rank[0], space_rank[0]
     own = source_weight(bits, time)
     later = source_weight(bits, lax.rem(time + 1, sizes[0]))
@@ -350,12 +352,17 @@
             moved = link_times(PackedLinks(even, *before), mu, half, vector, True)
             store_spin(behind, 0, half, moved)
     received = ((3, from_source(at), from_source(bt)), (2, from_source(az), from_source(bz)))
-    step_body(received, time_rank, space_rank, local, links, solution, sti, sto, szi, szo)
+    step_body(received, time_rank, space_rank, local, links, carried, solution, sti, sto, szi, szo)
+
+
+def step_carry_kernel(time_rank, space_rank, local, links, ti, to, zi, zo, *refs):
+    received = arrivals(time_rank, space_rank, ti, to, zi, zo)
+    step_body(received, time_rank, space_rank, local, links, *refs)
 
 
 def step_kernel(time_rank, space_rank, local, links, ti, to, zi, zo, *outs):
     received = arrivals(time_rank, space_rank, ti, to, zi, zo)
-    step_body(received, time_rank, space_rank, local, links, *outs)
+    step_body(received, time_rank, space_rank, local, links, None, *outs)
 
 
 def modes_kernel(modes, out):
@@ -497,20 +504,22 @@
     block, pair = jnp.where(moved, other, packed), jnp.where(moved, packed, other)
     clover = jnp.where(moved, other_clover, clover)
     block_sent = block[: packed.shape[0] - cut]
-    solution = None
+    solution, other_modes = None, []
+    modes_halves = modes_in.reshape(2, -1, 8, LANES)
     for iteration in range(ITERS):
         if iteration == 0:
             arrived = (pair, *exchange(None, block_sent, block_sent, block_sent))
         else:
             arrived = exchange(*sends)
-        if iteration == 1:
-            other_modes = lax.ppermute(modes_in, "tm", swap("tm", 0))
+        if iteration in (1, 2):
+            other_modes.append(arrived[0][24:])
+        if iteration == 2:
             modes = call(
                 modes_kernel,
                 jax.ShapeDtypeStruct((6, 256, 256), jnp.bfloat16),
                 10**6,
                 (),
-                jnp.where(moved, other_modes, modes_in),
+                jnp.where(moved, jnp.concatenate(other_modes).reshape(modes_in.shape), modes_in),
             )
         if iteration == 0:
             links, source = call(
@@ -525,12 +534,15 @@
             local = call(local_kernel, vectors(48), 5 * 10**6, (), solution, links, clover, source)
         if iteration < ITERS - 1:
             first = iteration == 0
+            carried = (modes_halves[iteration],) if iteration < 2 else ()
+            body = (step_first, step_carry_kernel, step_kernel)[iteration]
+            inner = 24 + sum(half.shape[0] for half in carried)
             solution, *sends = call(
-                step_first if first else step_kernel,
-                [vectors(48)] + [vectors(24)] * 4,
+                body,
+                [vectors(48), vectors(inner)] + [vectors(24)] * 3,
                 3 * 10**6,
                 (*ranks, bits) if first else ranks,
-                local, links, *arrived,
+                local, links, *arrived, *carried,
                 scratch=[pltpu.VMEM((12, 8, LANES), F32)] * 4 if first else (),
             )
         else:

time: 115 us -> 110 us (0.957)
  starting transfers between devices: 56.5 us -> 51.6 us
    ppermute x1 -> x0, starting transfers between devices: 4.87 us -> none  [partial_rows(): other_modes = lax.ppermute(modes_in, 'tm', swap('tm', 0))]
    all_to_all x1, blocking collectives: 19.3 us -> 17.5 us  [shards(): gathered = lax.all_to_all(copies, 'tm', 0, 0, tiled=True)]
    ppermute x3, starting transfers between devices: 9.46 us -> 7.84 us  [exchange(): ti = lax.ppermute(t_inner, 'tm', swap('tm', 0))]
    all_gather x4, blocking collectives: 16.1 us -> 17.6 us  [exchange(): zi = lax.all_gather(z_inner, 'space', axis_index_groups=pairs, tiled=True)]
  transfers between devices with their start and end apart: 14 -> 13, of which waited for: 0 -> 1; matrix products, arithmetic and copies ran while one was open for 0% -> 0% of each run, Pallas kernels for 3% -> 2%
where the time goes in v6:
time: 110 us
  starting transfers between devices  51.6 us (47%)
  blocking collectives  49.6 us (45%)
  Pallas kernels  5.16 us (5%)
  local copies, waits for them, and re-layouts  1.75 us (2%)
    ppermute x4, starting transfers between devices, exchange(): to = lax.ppermute(t_outer, 'tm', swap('tm', 1, swapped))  24.4 us
    all_gather x4, blocking collectives, exchange(): zi = lax.all_gather(z_inner, 'space', axis_index_groups=pairs, tiled=True)  17.6 us
    all_to_all x1, blocking collectives, shards(): gathered = lax.all_to_all(copies, 'tm', 0, 0, tiled=True)  17.5 us
    all_to_all x1, blocking collectives, shards(): parts = lax.all_to_all(partial_sums, 'space', 0, 0, tiled=True)  14.5 us
    ppermute x4, starting transfers between devices, exchange(): zo = lax.ppermute(z_outer, 'space', swap('space', 1))  12 us
    ppermute x3, starting transfers between devices, exchange(): ti = lax.ppermute(t_inner, 'tm', swap('tm', 0))  7.84 us
    ppermute x1, starting transfers between devices, partial_rows(): other = lax.ppermute(packed, 'tm', swap('tm', 0))  5.47 us
    pallas_call x12, Pallas kernels, call(): pl.pallas_call(kernel, out_shape=outs, in_specs=[smem] * len(scalars) + [...  5.16 us
  transfers between devices with their start and end apart: 13, of which 1 were waited for; matrix products, arithmetic and copies ran while one was open for 0% of the time, Pallas kernels for 2%

profile of v6, /device:TPU:1, one launch (start us, length us, event | category | flops | bytes accessed | tf_op | source)
XLA Modules:
  0.0 109.7 jit_solution(6802264272985839556)
XLA Ops:
  0.6 0.8 fusion.2
  1.5 5.5 %collective-permute-start = (f32[240,128]{1,0:T(8,128)S(1)}, f32[240,128]{1,0:T(8,128)S(1)}, u32[]{:S(2)}, u32[]{:S(2)}) collective-permute-start(f32[240,128]{1,0:T(8,128)S(1)} %pad_maximum_fusion), channel_id=1, source_target_pairs={{0,32},{64,96},{128,160},{192,224},{256,288},{320,352},{384,416},{... | collective-permute-start | bytes 368648 | tf_op jit(solution)/shard_map/ppermute | solution.py:502
  7.0 1.9 %collective-permute-start.1 = (f32[288,128]{1,0:T(8,128)}, f32[288,128]{1,0:T(8,128)S(1)}, u32[]{:S(2)}, u32[]{:S(2)}) collective-permute-start(f32[288,128]{1,0:T(8,128)} %bitcast.38), channel_id=1, source_target_pairs={{0,32},{64,96},{128,160},{192,224},{256,288},{320,352},{384,416},{... | collective-permute-start | bytes 442376 | tf_op jit(solution)/shard_map/ppermute | solution.py:503
  8.9 0.2 fusion.1
  9.2 0.0 copy-start.4
  9.2 0.0 copy-start.5
  9.2 0.6 copy-done.4
  9.9 0.0 copy-done.5
  9.9 0.1 pad_add_fusion.refs_2_
  10.0 0.0 collective-permute-done
  10.0 4.6 %collective-permute-start.3 = (f32[168,128]{1,0:T(8,128)S(1)}, f32[168,128]{1,0:T(8,128)S(1)}, u32[]{:S(2)}, u32[]{:S(2)}) collective-permute-start(f32[168,128]{1,0:T(8,128)S(1)} %slice.38), channel_id=1, source_target_pairs={{1,2},{3,4},{5,6},{7,8},{9,10},{11,12},{13,14},{15,16},{17,18},{19... | collective-permute-start | bytes 258056 | tf_op jit(solution)/shard_map/ppermute | solution.py:470
  14.6 14.3 %collective-permute-start.2 = (f32[168,128]{1,0:T(8,128)S(1)}, f32[168,128]{1,0:T(8,128)S(1)}, u32[]{:S(2)}, u32[]{:S(2)}) collective-permute-start(f32[168,128]{1,0:T(8,128)S(1)} %slice.38), channel_id=1, source_target_pairs={{32,96},{64,128},{160,224},{192,256},{288,352},{320,384},{416,480}... | collective-permute-start | bytes 258056 | tf_op jit(solution)/shard_map/ppermute | solution.py:471
  28.9 0.6 shard_map.86
  29.5 0.0 copy-start.3
  29.5 4.0 %all_gather.12.refs_7_ = f32[336,128]{1,0:T(8,128)S(1)} all-gather(f32[168,128]{1,0:T(8,128)S(1)} %slice.38), channel_id=1, replica_groups={{0,1},{2,3},{4,5},{6,7},{8,9},{10,11},{12,13},{14,15},{16,17},{18,19},{..., dimensions={0}, use_global_device_ids=true | all-gather | bytes 258048 | tf_op jit(solution)/shard_map/all_gather | solution.py:469
  33.5 0.0 collective-permute-done.1
  33.6 0.4 shard_map.87.refs_3_
  34.0 0.0 collective-permute-done.3.refs_8_
  34.0 0.0 collective-permute-done.2.refs_6_
  34.0 0.9 shard_map.88
  34.9 1.9 %collective-permute-start.4 = (f32[60,8,128]{2,1,0:T(8,128)S(1)}, f32[60,8,128]{2,1,0:T(8,128)S(1)}, u32[]{:S(2)}, u32[]{:S(2)}) collective-permute-start(f32[60,8,128]{2,1,0:T(8,128)S(1)} %get-tuple-element.26), channel_id=1, source_target_pairs={{0,32},{64,96},{128,160},{192,224},{256,288},{320,352},{384,416},{... | collective-permute-start | bytes 737288 | tf_op jit(solution)/shard_map/ppermute | solution.py:474
  36.8 4.6 %collective-permute-start.5 = (f32[24,8,128]{2,1,0:T(8,128)S(1)}, f32[24,8,128]{2,1,0:T(8,128)S(1)}, u32[]{:S(2)}, u32[]{:S(2)}) collective-permute-start(f32[24,8,128]{2,1,0:T(8,128)S(1)} %get-tuple-element.27), channel_id=1, source_target_pairs={{32,96},{64,128},{160,224},{192,256},{288,352},{320,384},{416,480}... | collective-permute-start | bytes 294920 | tf_op jit(solution)/shard_map/ppermute | solution.py:471
  41.5 2.4 %collective-permute-start.6 = (f32[24,8,128]{2,1,0:T(8,128)S(1)}, f32[24,8,128]{2,1,0:T(8,128)S(1)}, u32[]{:S(2)}, u32[]{:S(2)}) collective-permute-start(f32[24,8,128]{2,1,0:T(8,128)S(1)} %get-tuple-element.29), channel_id=1, source_target_pairs={{1,2},{3,4},{5,6},{7,8},{9,10},{11,12},{13,14},{15,16},{17,18},{19... | collective-permute-start | bytes 294920 | tf_op jit(solution)/shard_map/ppermute | solution.py:470
  43.9 0.5 shard_map.89.local
  44.3 2.8 %all_gather.13.zi = f32[48,8,128]{2,1,0:T(8,128)S(1)} all-gather(f32[24,8,128]{2,1,0:T(8,128)S(1)} %get-tuple-element.28), channel_id=1, replica_groups={{0,1},{2,3},{4,5},{6,7},{8,9},{10,11},{12,13},{14,15},{16,17},{18,19},{..., dimensions={0}, use_global_device_ids=true | all-gather | bytes 294912 | tf_op jit(solution)/shard_map/all_gather | solution.py:469
  47.1 0.0 collective-permute-done.5.to
  47.1 0.3 collective-permute-done.6.zo
  47.4 0.2 shard_map.90
  47.6 0.0 copy-start.6
  47.7 2.3 %collective-permute-start.7 = (f32[60,8,128]{2,1,0:T(8,128)S(1)}, f32[60,8,128]{2,1,0:T(8,128)S(1)}, u32[]{:S(2)}, u32[]{:S(2)}) collective-permute-start(f32[60,8,128]{2,1,0:T(8,128)S(1)} %get-tuple-element.31), channel_id=1, source_target_pairs={{0,32},{64,96},{128,160},{192,224},{256,288},{320,352},{384,416},{... | collective-permute-start | bytes 737288 | tf_op jit(solution)/shard_map/ppermute | solution.py:474
  50.0 3.0 %collective-permute-start.8 = (f32[24,8,128]{2,1,0:T(8,128)S(1)}, f32[24,8,128]{2,1,0:T(8,128)S(1)}, u32[]{:S(2)}, u32[]{:S(2)}) collective-permute-start(f32[24,8,128]{2,1,0:T(8,128)S(1)} %get-tuple-element.32), channel_id=1, source_target_pairs={{32,96},{64,128},{160,224},{192,256},{288,352},{320,384},{416,480}... | collective-permute-start | bytes 294920 | tf_op jit(solution)/shard_map/ppermute | solution.py:471
  53.0 2.9 %collective-permute-start.9 = (f32[24,8,128]{2,1,0:T(8,128)S(1)}, f32[24,8,128]{2,1,0:T(8,128)S(1)}, u32[]{:S(2)}, u32[]{:S(2)}) collective-permute-start(f32[24,8,128]{2,1,0:T(8,128)S(1)} %get-tuple-element.34), channel_id=1, source_target_pairs={{1,2},{3,4},{5,6},{7,8},{9,10},{11,12},{13,14},{15,16},{17,18},{19... | collective-permute-start | bytes 294920 | tf_op jit(solution)/shard_map/ppermute | solution.py:470
  55.9 0.1 add_bitcast_fusion.partner
  55.9 0.5 shard_map.91.local
  56.4 5.0 %all_gather.14.zi = f32[48,8,128]{2,1,0:T(8,128)S(1)} all-gather(f32[24,8,128]{2,1,0:T(8,128)S(1)} %get-tuple-element.33), channel_id=1, replica_groups={{0,1},{2,3},{4,5},{6,7},{8,9},{10,11},{12,13},{14,15},{16,17},{18,19},{..., dimensions={0}, use_global_device_ids=true | all-gather | bytes 294912 | tf_op jit(solution)/shard_map/all_gather | solution.py:469
  61.4 0.2 shard_map.92
  61.6 3.6 %collective-permute-start.10 = (f32[24,8,128]{2,1,0:T(8,128)S(1)}, f32[24,8,128]{2,1,0:T(8,128)S(1)}, u32[]{:S(2)}, u32[]{:S(2)}) collective-permute-start(f32[24,8,128]{2,1,0:T(8,128)S(1)} %get-tuple-element.36), channel_id=1, source_target_pairs={{0,32},{64,96},{128,160},{192,224},{256,288},{320,352},{384,416},{... | collective-permute-start | bytes 294920 | tf_op jit(solution)/shard_map/ppermute | solution.py:474
  65.3 2.4 %collective-permute-start.11 = (f32[24,8,128]{2,1,0:T(8,128)S(1)}, f32[24,8,128]{2,1,0:T(8,128)S(1)}, u32[]{:S(2)}, u32[]{:S(2)}) collective-permute-start(f32[24,8,128]{2,1,0:T(8,128)S(1)} %get-tuple-element.37), channel_id=1, source_target_pairs={{32,96},{64,128},{160,224},{192,256},{288,352},{320,384},{416,480}... | collective-permute-start | bytes 294920 | tf_op jit(solution)/shard_map/ppermute | solution.py:471
  67.7 0.0 slice-start
  67.7 2.1 %collective-permute-start.12 = (f32[24,8,128]{2,1,0:T(8,128)S(1)}, f32[24,8,128]{2,1,0:T(8,128)S(1)}, u32[]{:S(2)}, u32[]{:S(2)}) collective-permute-start(f32[24,8,128]{2,1,0:T(8,128)S(1)} %get-tuple-element.39), channel_id=1, source_target_pairs={{1,2},{3,4},{5,6},{7,8},{9,10},{11,12},{13,14},{15,16},{17,18},{19... | collective-permute-start | bytes 294920 | tf_op jit(solution)/shard_map/ppermute | solution.py:470
  69.9 0.1 shard_map.94.modes
  70.1 0.5 shard_map.93.local
  70.5 5.8 %all_gather.15.zi = f32[48,8,128]{2,1,0:T(8,128)S(1)} all-gather(f32[24,8,128]{2,1,0:T(8,128)S(1)} %get-tuple-element.38), channel_id=1, replica_groups={{0,1},{2,3},{4,5},{6,7},{8,9},{10,11},{12,13},{14,15},{16,17},{18,19},{..., dimensions={0}, use_global_device_ids=true | all-gather | bytes 294912 | tf_op jit(solution)/shard_map/all_gather | solution.py:469
  76.4 0.0 collective-permute-done.10.ti
  76.4 0.4 shard_map.95
  76.8 14.5 %all_to_all.22 = f32[32,1,96]{2,1,0:T(1,128)S(1)} all-to-all(f32[32,1,96]{2,1,0:T(1,128)S(1)} %bitcast.27), channel_id=1, replica_groups=mesh['tm'=24,'space'=32] {'space'}, dimensions={0} | all-to-all | bytes 24576 | tf_op jit(solution)/shard_map/all_to_all | solution.py:567
  91.2 17.5 %all_to_all.23 = f32[24,1,96]{2,1,0:T(1,128)S(1)} all-to-all(f32[24,1,96]{2,1,0:T(1,128)S(1)} %bitcast.29), channel_id=1, replica_groups=mesh['tm'=24,'space'=32] {'tm'}, dimensions={0} | all-to-all | bytes 18432 | tf_op jit(solution)/shard_map/all_to_all | solution.py:572
  108.8 0.9 shard_map.97
  (23 shorter events, 0.2 us)
Async XLA Ops:
  0.6 0.9 copy-start.2
  0.6 8.3 %copy-start.1 = (f32[48,1,1,6,256]{4,2,3,1,0:T(1,128)S(1)}, f32[48,1,1,6,256]{4,2,3,1,0:T(1,128)}, u32[]{:S(2)}) copy-start(f32[48,1,1,6,256]{4,2,3,1,0:T(1,128)} %param.10) | copy-start | bytes 884740
  1.5 8.4 %collective-permute-start = (f32[240,128]{1,0:T(8,128)S(1)}, f32[240,128]{1,0:T(8,128)S(1)}, u32[]{:S(2)}, u32[]{:S(2)}) collective-permute-start(f32[240,128]{1,0:T(8,128)S(1)} %pad_maximum_fusion), channel_id=1, source_target_pairs={{0,32},{64,96},{128,160},{192,224},{256,288},{320,352},{384,416},{... | collective-permute-start | bytes 368648 | tf_op jit(solution)/shard_map/ppermute | solution.py:502
  7.0 26.5 %collective-permute-start.1 = (f32[288,128]{1,0:T(8,128)}, f32[288,128]{1,0:T(8,128)S(1)}, u32[]{:S(2)}, u32[]{:S(2)}) collective-permute-start(f32[288,128]{1,0:T(8,128)} %bitcast.38), channel_id=1, source_target_pairs={{0,32},{64,96},{128,160},{192,224},{256,288},{320,352},{384,416},{... | collective-permute-start | bytes 442376 | tf_op jit(solution)/shard_map/ppermute | solution.py:503
  9.2 0.7 copy-start.4
  9.2 0.7 copy-start.5
  10.0 24.0 %collective-permute-start.3 = (f32[168,128]{1,0:T(8,128)S(1)}, f32[168,128]{1,0:T(8,128)S(1)}, u32[]{:S(2)}, u32[]{:S(2)}) collective-permute-start(f32[168,128]{1,0:T(8,128)S(1)} %slice.38), channel_id=1, source_target_pairs={{1,2},{3,4},{5,6},{7,8},{9,10},{11,12},{13,14},{15,16},{17,18},{19... | collective-permute-start | bytes 258056 | tf_op jit(solution)/shard_map/ppermute | solution.py:470
  14.6 19.4 %collective-permute-start.2 = (f32[168,128]{1,0:T(8,128)S(1)}, f32[168,128]{1,0:T(8,128)S(1)}, u32[]{:S(2)}, u32[]{:S(2)}) collective-permute-start(f32[168,128]{1,0:T(8,128)S(1)} %slice.38), channel_id=1, source_target_pairs={{32,96},{64,128},{160,224},{192,256},{288,352},{320,384},{416,480}... | collective-permute-start | bytes 258056 | tf_op jit(solution)/shard_map/ppermute | solution.py:471
  29.5 4.0 %copy-start.3 = (f32[2,6,1,1,12,256]{5,3,4,2,1,0:T(1,128)S(1)}, f32[2,6,1,1,12,256]{5,3,4,2,1,0:T(1,128)}, u32[]{:S(2)}) copy-start(f32[2,6,1,1,12,256]{5,3,4,2,1,0:T(1,128)} %param.9) | copy-start | bytes 442372
  34.9 12.5 %collective-permute-start.4 = (f32[60,8,128]{2,1,0:T(8,128)S(1)}, f32[60,8,128]{2,1,0:T(8,128)S(1)}, u32[]{:S(2)}, u32[]{:S(2)}) collective-permute-start(f32[60,8,128]{2,1,0:T(8,128)S(1)} %get-tuple-element.26), channel_id=1, source_target_pairs={{0,32},{64,96},{128,160},{192,224},{256,288},{320,352},{384,416},{... | collective-permute-start | bytes 737288 | tf_op jit(solution)/shard_map/ppermute | solution.py:474
  36.8 10.3 %collective-permute-start.5 = (f32[24,8,128]{2,1,0:T(8,128)S(1)}, f32[24,8,128]{2,1,0:T(8,128)S(1)}, u32[]{:S(2)}, u32[]{:S(2)}) collective-permute-start(f32[24,8,128]{2,1,0:T(8,128)S(1)} %get-tuple-element.27), channel_id=1, source_target_pairs={{32,96},{64,128},{160,224},{192,256},{288,352},{320,384},{416,480}... | collective-permute-start | bytes 294920 | tf_op jit(solution)/shard_map/ppermute | solution.py:471
  41.5 5.9 %collective-permute-start.6 = (f32[24,8,128]{2,1,0:T(8,128)S(1)}, f32[24,8,128]{2,1,0:T(8,128)S(1)}, u32[]{:S(2)}, u32[]{:S(2)}) collective-permute-start(f32[24,8,128]{2,1,0:T(8,128)S(1)} %get-tuple-element.29), channel_id=1, source_target_pairs={{1,2},{3,4},{5,6},{7,8},{9,10},{11,12},{13,14},{15,16},{17,18},{19... | collective-permute-start | bytes 294920 | tf_op jit(solution)/shard_map/ppermute | solution.py:470
  47.4 8.6 %copy-start = (f32[60,8,128]{2,1,0:T(8,128)}, f32[60,8,128]{2,1,0:T(8,128)S(1)}, u32[]{:S(2)}) copy-start(f32[60,8,128]{2,1,0:T(8,128)S(1)} %collective-permute-done.4.ti) | copy-start | bytes 737284
  47.6 2.3 %copy-start.6 = (s32[48]{0:T(128)S(1)}, s32[48]{0:T(128)}, u32[]{:S(2)}) copy-start(s32[48]{0:T(128)} %param.11) | copy-start | bytes 580
  47.7 13.7 %collective-permute-start.7 = (f32[60,8,128]{2,1,0:T(8,128)S(1)}, f32[60,8,128]{2,1,0:T(8,128)S(1)}, u32[]{:S(2)}, u32[]{:S(2)}) collective-permute-start(f32[60,8,128]{2,1,0:T(8,128)S(1)} %get-tuple-element.31), channel_id=1, source_target_pairs={{0,32},{64,96},{128,160},{192,224},{256,288},{320,352},{384,416},{... | collective-permute-start | bytes 737288 | tf_op jit(solution)/shard_map/ppermute | solution.py:474
  50.0 11.4 %collective-permute-start.8 = (f32[24,8,128]{2,1,0:T(8,128)S(1)}, f32[24,8,128]{2,1,0:T(8,128)S(1)}, u32[]{:S(2)}, u32[]{:S(2)}) collective-permute-start(f32[24,8,128]{2,1,0:T(8,128)S(1)} %get-tuple-element.32), channel_id=1, source_target_pairs={{32,96},{64,128},{160,224},{192,256},{288,352},{320,384},{416,480}... | collective-permute-start | bytes 294920 | tf_op jit(solution)/shard_map/ppermute | solution.py:471
  53.0 8.4 %collective-permute-start.9 = (f32[24,8,128]{2,1,0:T(8,128)S(1)}, f32[24,8,128]{2,1,0:T(8,128)S(1)}, u32[]{:S(2)}, u32[]{:S(2)}) collective-permute-start(f32[24,8,128]{2,1,0:T(8,128)S(1)} %get-tuple-element.34), channel_id=1, source_target_pairs={{1,2},{3,4},{5,6},{7,8},{9,10},{11,12},{13,14},{15,16},{17,18},{19... | collective-permute-start | bytes 294920 | tf_op jit(solution)/shard_map/ppermute | solution.py:470
  61.6 14.7 %collective-permute-start.10 = (f32[24,8,128]{2,1,0:T(8,128)S(1)}, f32[24,8,128]{2,1,0:T(8,128)S(1)}, u32[]{:S(2)}, u32[]{:S(2)}) collective-permute-start(f32[24,8,128]{2,1,0:T(8,128)S(1)} %get-tuple-element.36), channel_id=1, source_target_pairs={{0,32},{64,96},{128,160},{192,224},{256,288},{320,352},{384,416},{... | collective-permute-start | bytes 294920 | tf_op jit(solution)/shard_map/ppermute | solution.py:474
  65.3 11.1 %collective-permute-start.11 = (f32[24,8,128]{2,1,0:T(8,128)S(1)}, f32[24,8,128]{2,1,0:T(8,128)S(1)}, u32[]{:S(2)}, u32[]{:S(2)}) collective-permute-start(f32[24,8,128]{2,1,0:T(8,128)S(1)} %get-tuple-element.37), channel_id=1, source_target_pairs={{32,96},{64,128},{160,224},{192,256},{288,352},{320,384},{416,480}... | collective-permute-start | bytes 294920 | tf_op jit(solution)/shard_map/ppermute | solution.py:471
  67.7 2.2 %slice-start = ((f32[60,8,128]{2,1,0:T(8,128)}), f32[36,8,128]{2,1,0:T(8,128)S(1)}, s32[]{:S(2)}) async-start(f32[60,8,128]{2,1,0:T(8,128)} %copy-done), calls=%async_computation.2 | async-start | bytes 294912 | tf_op jit(solution)/shard_map/slice | solution.py:515
  67.7 8.7 %collective-permute-start.12 = (f32[24,8,128]{2,1,0:T(8,128)S(1)}, f32[24,8,128]{2,1,0:T(8,128)S(1)}, u32[]{:S(2)}, u32[]{:S(2)}) collective-permute-start(f32[24,8,128]{2,1,0:T(8,128)S(1)} %get-tuple-element.39), channel_id=1, source_target_pairs={{1,2},{3,4},{5,6},{7,8},{9,10},{11,12},{13,14},{15,16},{17,18},{19... | collective-permute-start | bytes 294920 | tf_op jit(solution)/shard_map/ppermute | solution.py:470

commit v7 on v4

--- a/solution.py
+++ b/solution.py
@@ -399,19 +399,20 @@
         out[pl.ds(spin, 8, stride=4), :] = total[8 * spin : 8 * spin + 8, : out.shape[1]]
 
 
-def sum_kernel(parts, out, copies):
+def sum_kernel(parts, copies):
     total = jnp.sum(parts[...], axis=0, keepdims=True)
-    out[...] = total
     copies[...] = jnp.broadcast_to(total, copies.shape)
 
 
-def correlate_kernel(time_rank, rows, partner, out):
+def correlate_kernel(time_rank, rows, partner, row, out):
     size = rows.shape[1]
+    mine = rows[pl.ds(time_rank[0], 1), :]
+    row[...] = mine
     onehot = (
         partner[...] == lax.broadcasted_iota(jnp.int32, (size, size), 0)
     ).astype(F32)
     contract = (((1,), (1,)), ((), ()))
-    own = jnp.broadcast_to(rows[pl.ds(time_rank[0], 1), :], (8, size))
+    own = jnp.broadcast_to(mine, (8, size))
     weighted = lax.dot_general(
         own, onehot, contract, precision=lax.Precision.HIGHEST, preferred_element_type=F32
     )
@@ -531,17 +532,18 @@
     both = jnp.concatenate([partner, partner + count]).reshape(1, 2 * count)
     both, partial_sums = lax.optimization_barrier((both, partial_sums))
     parts = lax.all_to_all(partial_sums, "space", 0, 0, tiled=True)
-    times, ranks = lax.axis_size("tm"), mesh_ranks()[:1]
-    row, copies = call(
-        sum_kernel,
-        [jax.ShapeDtypeStruct((n, 2 * count), F32) for n in (1, times)],
-        10**4,
-        (),
-        parts,
+    times = lax.axis_size("tm")
+    copies = call(
+        sum_kernel, jax.ShapeDtypeStruct((times, 2 * count), F32), 10**4, (), parts
     )
     rows = lax.all_to_all(copies, "tm", 0, 0, tiled=True)
-    correlator = call(
-        correlate_kernel, jax.ShapeDtypeStruct((1, times), F32), 10**5, ranks, rows, both
+    row, correlator = call(
+        correlate_kernel,
+        [jax.ShapeDtypeStruct((1, n), F32) for n in (2 * count, times)],
+        10**5,
+        mesh_ranks()[:1],
+        rows,
+        both,
     )
     return row.reshape(1, 1, 2 * count), correlator.reshape(1, 1, times)
 

time: 110 us -> 110 us (level)
  no operation moved by 1% of the time
where the time goes in v7:
time: 110 us; the launch traced here: 109 us
  starting transfers between devices  51.4 us (47%)
  blocking collectives  50.6 us (46%)
  Pallas kernels  5.11 us (5%)
    ppermute x4, starting transfers between devices, exchange(): to = lax.ppermute(t_outer, 'tm', swap('tm', 1))  28 us
    all_gather x4, blocking collectives, exchange(): zi = lax.all_gather(z_inner, 'space', axis_index_groups=pairs, tiled=True)  20.5 us
    all_to_all x1, blocking collectives, shards(): rows = lax.all_to_all(copies, 'tm', 0, 0, tiled=True)  17.9 us
    ppermute x4, starting transfers between devices, exchange(): ti = lax.ppermute(t_inner, 'tm', swap('tm', 0))  13.1 us
    all_to_all x1, blocking collectives, shards(): parts = lax.all_to_all(partial_sums, 'space', 0, 0, tiled=True)  12.2 us
    ppermute x4, starting transfers between devices, exchange(): zo = lax.ppermute(z_outer, 'space', swap('space', 1))  10.3 us
    pallas_call x12, Pallas kernels, call(): pl.pallas_call(kernel, out_shape=outs, in_specs=[smem] * len(scalars) + [...  5.11 us
  transfers between devices with their start and end apart: 12, of which 0 were waited for; matrix products, arithmetic and copies ran while one was open for 0% of the time, Pallas kernels for 2%

profile of v7, /device:TPU:1, one launch (start us, length us, event | category | flops | bytes accessed | tf_op | source)
XLA Modules:
  0.0 109.0 jit_solution(12035157309362437357)
XLA Ops:
  0.6 0.8 slice.6
  1.4 0.0 copy-start
  1.5 5.6 %collective-permute-start = (f32[168,128]{1,0:T(8,128)S(1)}, f32[168,128]{1,0:T(8,128)S(1)}, u32[]{:S(2)}, u32[]{:S(2)}) collective-permute-start(f32[168,128]{1,0:T(8,128)S(1)} %pad_maximum_fusion), channel_id=1, source_target_pairs={{0,32},{64,96},{128,160},{192,224},{256,288},{320,352},{384,416},{... | collective-permute-start | bytes 258056 | tf_op jit(solution)/shard_map/ppermute | solution.py:456
  7.1 14.2 %collective-permute-start.1 = (f32[168,128]{1,0:T(8,128)S(1)}, f32[168,128]{1,0:T(8,128)S(1)}, u32[]{:S(2)}, u32[]{:S(2)}) collective-permute-start(f32[168,128]{1,0:T(8,128)S(1)} %pad_maximum_fusion), channel_id=1, source_target_pairs={{32,64},{96,128},{160,192},{224,256},{288,320},{352,384},{416,448}... | collective-permute-start | bytes 258056 | tf_op jit(solution)/shard_map/ppermute | solution.py:457
  21.3 4.3 %collective-permute-start.2 = (f32[168,128]{1,0:T(8,128)S(1)}, f32[168,128]{1,0:T(8,128)S(1)}, u32[]{:S(2)}, u32[]{:S(2)}) collective-permute-start(f32[168,128]{1,0:T(8,128)S(1)} %pad_maximum_fusion), channel_id=1, source_target_pairs={{1,2},{3,4},{5,6},{7,8},{9,10},{11,12},{13,14},{15,16},{17,18},{19... | collective-permute-start | bytes 258056 | tf_op jit(solution)/shard_map/ppermute | solution.py:455
  25.7 0.0 copy-done.4
  25.7 0.0 copy-done.5
  25.7 0.1 pad_add_fusion.refs_2_
  25.8 0.6 shard_map.86
  26.4 0.4 shard_map.87.refs_3_
  26.8 3.7 %all_gather.12.refs_7_ = f32[336,128]{1,0:T(8,128)S(1)} all-gather(f32[168,128]{1,0:T(8,128)S(1)} %pad_maximum_fusion), channel_id=1, replica_groups={{0,1},{2,3},{4,5},{6,7},{8,9},{10,11},{12,13},{14,15},{16,17},{18,19},{..., dimensions={0}, use_global_device_ids=true | all-gather | bytes 258048 | tf_op jit(solution)/shard_map/all_gather | solution.py:454
  30.5 0.0 collective-permute-done.refs_5_
  30.5 0.0 collective-permute-done.1.refs_6_
  30.5 0.0 collective-permute-done.2.refs_8_
  30.5 0.9 shard_map.88
  31.3 1.9 %collective-permute-start.3 = (f32[24,8,128]{2,1,0:T(8,128)S(1)}, f32[24,8,128]{2,1,0:T(8,128)S(1)}, u32[]{:S(2)}, u32[]{:S(2)}) collective-permute-start(f32[24,8,128]{2,1,0:T(8,128)S(1)} %get-tuple-element.26), channel_id=1, source_target_pairs={{0,32},{64,96},{128,160},{192,224},{256,288},{320,352},{384,416},{... | collective-permute-start | bytes 294920 | tf_op jit(solution)/shard_map/ppermute | solution.py:456
  33.3 4.9 %collective-permute-start.4 = (f32[24,8,128]{2,1,0:T(8,128)S(1)}, f32[24,8,128]{2,1,0:T(8,128)S(1)}, u32[]{:S(2)}, u32[]{:S(2)}) collective-permute-start(f32[24,8,128]{2,1,0:T(8,128)S(1)} %get-tuple-element.27), channel_id=1, source_target_pairs={{32,64},{96,128},{160,192},{224,256},{288,320},{352,384},{416,448}... | collective-permute-start | bytes 294920 | tf_op jit(solution)/shard_map/ppermute | solution.py:457
  38.1 2.1 %collective-permute-start.5 = (f32[24,8,128]{2,1,0:T(8,128)S(1)}, f32[24,8,128]{2,1,0:T(8,128)S(1)}, u32[]{:S(2)}, u32[]{:S(2)}) collective-permute-start(f32[24,8,128]{2,1,0:T(8,128)S(1)} %get-tuple-element.29), channel_id=1, source_target_pairs={{1,2},{3,4},{5,6},{7,8},{9,10},{11,12},{13,14},{15,16},{17,18},{19... | collective-permute-start | bytes 294920 | tf_op jit(solution)/shard_map/ppermute | solution.py:455
  40.3 0.5 shard_map.89.local
  40.7 4.7 %all_gather.13.zi = f32[48,8,128]{2,1,0:T(8,128)S(1)} all-gather(f32[24,8,128]{2,1,0:T(8,128)S(1)} %get-tuple-element.28), channel_id=1, replica_groups={{0,1},{2,3},{4,5},{6,7},{8,9},{10,11},{12,13},{14,15},{16,17},{18,19},{..., dimensions={0}, use_global_device_ids=true | all-gather | bytes 294912 | tf_op jit(solution)/shard_map/all_gather | solution.py:454
  45.4 0.0 collective-permute-done.3.ti
  45.4 0.0 collective-permute-done.4.to
  45.4 0.0 collective-permute-done.5.zo
  45.4 0.2 shard_map.90
  45.6 2.5 %collective-permute-start.6 = (f32[24,8,128]{2,1,0:T(8,128)S(1)}, f32[24,8,128]{2,1,0:T(8,128)S(1)}, u32[]{:S(2)}, u32[]{:S(2)}) collective-permute-start(f32[24,8,128]{2,1,0:T(8,128)S(1)} %get-tuple-element.31), channel_id=1, source_target_pairs={{0,32},{64,96},{128,160},{192,224},{256,288},{320,352},{384,416},{... | collective-permute-start | bytes 294920 | tf_op jit(solution)/shard_map/ppermute | solution.py:456
  48.2 0.0 copy-start.6
  48.2 4.2 %collective-permute-start.7 = (f32[24,8,128]{2,1,0:T(8,128)S(1)}, f32[24,8,128]{2,1,0:T(8,128)S(1)}, u32[]{:S(2)}, u32[]{:S(2)}) collective-permute-start(f32[24,8,128]{2,1,0:T(8,128)S(1)} %get-tuple-element.32), channel_id=1, source_target_pairs={{32,64},{96,128},{160,192},{224,256},{288,320},{352,384},{416,448}... | collective-permute-start | bytes 294920 | tf_op jit(solution)/shard_map/ppermute | solution.py:457
  52.5 1.9 %collective-permute-start.8 = (f32[24,8,128]{2,1,0:T(8,128)S(1)}, f32[24,8,128]{2,1,0:T(8,128)S(1)}, u32[]{:S(2)}, u32[]{:S(2)}) collective-permute-start(f32[24,8,128]{2,1,0:T(8,128)S(1)} %get-tuple-element.34), channel_id=1, source_target_pairs={{1,2},{3,4},{5,6},{7,8},{9,10},{11,12},{13,14},{15,16},{17,18},{19... | collective-permute-start | bytes 294920 | tf_op jit(solution)/shard_map/ppermute | solution.py:455
  54.4 0.4 shard_map.91.local
  54.8 5.6 %all_gather.14.zi = f32[48,8,128]{2,1,0:T(8,128)S(1)} all-gather(f32[24,8,128]{2,1,0:T(8,128)S(1)} %get-tuple-element.33), channel_id=1, replica_groups={{0,1},{2,3},{4,5},{6,7},{8,9},{10,11},{12,13},{14,15},{16,17},{18,19},{..., dimensions={0}, use_global_device_ids=true | all-gather | bytes 294912 | tf_op jit(solution)/shard_map/all_gather | solution.py:454
  60.5 0.0 collective-permute-done.6.ti
  60.5 0.0 collective-permute-done.7.to
  60.5 0.0 collective-permute-done.8.zo
  60.5 0.2 shard_map.92
  60.7 4.7 %collective-permute-start.10 = (f32[24,8,128]{2,1,0:T(8,128)S(1)}, f32[24,8,128]{2,1,0:T(8,128)S(1)}, u32[]{:S(2)}, u32[]{:S(2)}) collective-permute-start(f32[24,8,128]{2,1,0:T(8,128)S(1)} %get-tuple-element.37), channel_id=1, source_target_pairs={{32,64},{96,128},{160,192},{224,256},{288,320},{352,384},{416,448}... | collective-permute-start | bytes 294920 | tf_op jit(solution)/shard_map/ppermute | solution.py:457
  65.4 1.9 %collective-permute-start.11 = (f32[24,8,128]{2,1,0:T(8,128)S(1)}, f32[24,8,128]{2,1,0:T(8,128)S(1)}, u32[]{:S(2)}, u32[]{:S(2)}) collective-permute-start(f32[24,8,128]{2,1,0:T(8,128)S(1)} %get-tuple-element.39), channel_id=1, source_target_pairs={{1,2},{3,4},{5,6},{7,8},{9,10},{11,12},{13,14},{15,16},{17,18},{19... | collective-permute-start | bytes 294920 | tf_op jit(solution)/shard_map/ppermute | solution.py:455
  67.3 3.0 %collective-permute-start.9 = (f32[24,8,128]{2,1,0:T(8,128)S(1)}, f32[24,8,128]{2,1,0:T(8,128)S(1)}, u32[]{:S(2)}, u32[]{:S(2)}) collective-permute-start(f32[24,8,128]{2,1,0:T(8,128)S(1)} %get-tuple-element.36), channel_id=1, source_target_pairs={{0,32},{64,96},{128,160},{192,224},{256,288},{320,352},{384,416},{... | collective-permute-start | bytes 294920 | tf_op jit(solution)/shard_map/ppermute | solution.py:456
  70.4 0.1 add_bitcast_fusion.partner
  70.5 0.1 shard_map.94.modes
  70.6 0.4 shard_map.93.local
  71.0 6.5 %all_gather.15.zi = f32[48,8,128]{2,1,0:T(8,128)S(1)} all-gather(f32[24,8,128]{2,1,0:T(8,128)S(1)} %get-tuple-element.38), channel_id=1, replica_groups={{0,1},{2,3},{4,5},{6,7},{8,9},{10,11},{12,13},{14,15},{16,17},{18,19},{..., dimensions={0}, use_global_device_ids=true | all-gather | bytes 294912 | tf_op jit(solution)/shard_map/all_gather | solution.py:454
  77.5 0.0 collective-permute-done.10.to
  77.6 0.0 collective-permute-done.11.zo
  77.6 0.0 collective-permute-done.9.ti
  77.6 0.4 shard_map.95
  78.0 12.2 %all_to_all.22 = f32[32,1,96]{2,1,0:T(1,128)S(1)} all-to-all(f32[32,1,96]{2,1,0:T(1,128)S(1)} %bitcast.27), channel_id=1, replica_groups=mesh['tm'=24,'space'=32] {'space'}, dimensions={0} | all-to-all | bytes 24576 | tf_op jit(solution)/shard_map/all_to_all | solution.py:534
  90.2 17.9 %all_to_all.23 = f32[24,1,96]{2,1,0:T(1,128)S(1)} all-to-all(f32[24,1,96]{2,1,0:T(1,128)S(1)} %bitcast.29), channel_id=1, replica_groups=mesh['tm'=24,'space'=32] {'tm'}, dimensions={0} | all-to-all | bytes 18432 | tf_op jit(solution)/shard_map/all_to_all | solution.py:539
  108.1 0.9 shard_map.97
  (13 shorter events, 0.0 us)
Async XLA Ops:
  0.6 0.8 copy-start.2
  1.4 24.3 %copy-start.4 = (s32[8]{0:T(128)S(1)}, s32[8]{0:T(128)}, u32[]{:S(2)}) copy-start(s32[8]{0:T(128)} %param.12) | copy-start | bytes 100
  1.4 24.3 %copy-start.5 = (s32[4]{0:T(128)S(1)}, s32[4]{0:T(128)}, u32[]{:S(2)}) copy-start(s32[4]{0:T(128)} %param.13) | copy-start | bytes 52
  1.4 24.3 %copy-start.3 = (f32[4,3,1,1,6,256]{5,3,4,2,1,0:T(1,128)S(1)}, f32[4,3,1,1,6,256]{5,3,4,2,1,0:T(1,128)}, u32[]{:S(2)}) copy-start(f32[4,3,1,1,6,256]{5,3,4,2,1,0:T(1,128)} %param.8) | copy-start | bytes 221188
  1.4 24.9 %copy-start = (f32[2,6,1,1,12,256]{5,3,4,2,1,0:T(1,128)S(1)}, f32[2,6,1,1,12,256]{5,3,4,2,1,0:T(1,128)}, u32[]{:S(2)}) copy-start(f32[2,6,1,1,12,256]{5,3,4,2,1,0:T(1,128)} %param.9) | copy-start | bytes 442372
  1.5 29.0 %collective-permute-start = (f32[168,128]{1,0:T(8,128)S(1)}, f32[168,128]{1,0:T(8,128)S(1)}, u32[]{:S(2)}, u32[]{:S(2)}) collective-permute-start(f32[168,128]{1,0:T(8,128)S(1)} %pad_maximum_fusion), channel_id=1, source_target_pairs={{0,32},{64,96},{128,160},{192,224},{256,288},{320,352},{384,416},{... | collective-permute-start | bytes 258056 | tf_op jit(solution)/shard_map/ppermute | solution.py:456
  7.1 23.4 %collective-permute-start.1 = (f32[168,128]{1,0:T(8,128)S(1)}, f32[168,128]{1,0:T(8,128)S(1)}, u32[]{:S(2)}, u32[]{:S(2)}) collective-permute-start(f32[168,128]{1,0:T(8,128)S(1)} %pad_maximum_fusion), channel_id=1, source_target_pairs={{32,64},{96,128},{160,192},{224,256},{288,320},{352,384},{416,448}... | collective-permute-start | bytes 258056 | tf_op jit(solution)/shard_map/ppermute | solution.py:457
  21.3 9.1 %collective-permute-start.2 = (f32[168,128]{1,0:T(8,128)S(1)}, f32[168,128]{1,0:T(8,128)S(1)}, u32[]{:S(2)}, u32[]{:S(2)}) collective-permute-start(f32[168,128]{1,0:T(8,128)S(1)} %pad_maximum_fusion), channel_id=1, source_target_pairs={{1,2},{3,4},{5,6},{7,8},{9,10},{11,12},{13,14},{15,16},{17,18},{19... | collective-permute-start | bytes 258056 | tf_op jit(solution)/shard_map/ppermute | solution.py:455
  31.3 14.1 %collective-permute-start.3 = (f32[24,8,128]{2,1,0:T(8,128)S(1)}, f32[24,8,128]{2,1,0:T(8,128)S(1)}, u32[]{:S(2)}, u32[]{:S(2)}) collective-permute-start(f32[24,8,128]{2,1,0:T(8,128)S(1)} %get-tuple-element.26), channel_id=1, source_target_pairs={{0,32},{64,96},{128,160},{192,224},{256,288},{320,352},{384,416},{... | collective-permute-start | bytes 294920 | tf_op jit(solution)/shard_map/ppermute | solution.py:456
  33.3 12.1 %collective-permute-start.4 = (f32[24,8,128]{2,1,0:T(8,128)S(1)}, f32[24,8,128]{2,1,0:T(8,128)S(1)}, u32[]{:S(2)}, u32[]{:S(2)}) collective-permute-start(f32[24,8,128]{2,1,0:T(8,128)S(1)} %get-tuple-element.27), channel_id=1, source_target_pairs={{32,64},{96,128},{160,192},{224,256},{288,320},{352,384},{416,448}... | collective-permute-start | bytes 294920 | tf_op jit(solution)/shard_map/ppermute | solution.py:457
  38.1 7.3 %collective-permute-start.5 = (f32[24,8,128]{2,1,0:T(8,128)S(1)}, f32[24,8,128]{2,1,0:T(8,128)S(1)}, u32[]{:S(2)}, u32[]{:S(2)}) collective-permute-start(f32[24,8,128]{2,1,0:T(8,128)S(1)} %get-tuple-element.29), channel_id=1, source_target_pairs={{1,2},{3,4},{5,6},{7,8},{9,10},{11,12},{13,14},{15,16},{17,18},{19... | collective-permute-start | bytes 294920 | tf_op jit(solution)/shard_map/ppermute | solution.py:455
  45.6 14.8 %collective-permute-start.6 = (f32[24,8,128]{2,1,0:T(8,128)S(1)}, f32[24,8,128]{2,1,0:T(8,128)S(1)}, u32[]{:S(2)}, u32[]{:S(2)}) collective-permute-start(f32[24,8,128]{2,1,0:T(8,128)S(1)} %get-tuple-element.31), channel_id=1, source_target_pairs={{0,32},{64,96},{128,160},{192,224},{256,288},{320,352},{384,416},{... | collective-permute-start | bytes 294920 | tf_op jit(solution)/shard_map/ppermute | solution.py:456
  48.2 6.2 %copy-start.6 = (s32[48]{0:T(128)S(1)}, s32[48]{0:T(128)}, u32[]{:S(2)}) copy-start(s32[48]{0:T(128)} %param.11) | copy-start | bytes 580
  48.2 12.3 %collective-permute-start.7 = (f32[24,8,128]{2,1,0:T(8,128)S(1)}, f32[24,8,128]{2,1,0:T(8,128)S(1)}, u32[]{:S(2)}, u32[]{:S(2)}) collective-permute-start(f32[24,8,128]{2,1,0:T(8,128)S(1)} %get-tuple-element.32), channel_id=1, source_target_pairs={{32,64},{96,128},{160,192},{224,256},{288,320},{352,384},{416,448}... | collective-permute-start | bytes 294920 | tf_op jit(solution)/shard_map/ppermute | solution.py:457
  52.5 8.0 %collective-permute-start.8 = (f32[24,8,128]{2,1,0:T(8,128)S(1)}, f32[24,8,128]{2,1,0:T(8,128)S(1)}, u32[]{:S(2)}, u32[]{:S(2)}) collective-permute-start(f32[24,8,128]{2,1,0:T(8,128)S(1)} %get-tuple-element.34), channel_id=1, source_target_pairs={{1,2},{3,4},{5,6},{7,8},{9,10},{11,12},{13,14},{15,16},{17,18},{19... | collective-permute-start | bytes 294920 | tf_op jit(solution)/shard_map/ppermute | solution.py:455
  60.5 10.0 %copy-start.1 = (f32[48,1,1,6,256]{4,2,3,1,0:T(1,128)S(1)}, f32[48,1,1,6,256]{4,2,3,1,0:T(1,128)}, u32[]{:S(2)}) copy-start(f32[48,1,1,6,256]{4,2,3,1,0:T(1,128)} %param.10) | copy-start | bytes 884740
  60.7 16.8 %collective-permute-start.10 = (f32[24,8,128]{2,1,0:T(8,128)S(1)}, f32[24,8,128]{2,1,0:T(8,128)S(1)}, u32[]{:S(2)}, u32[]{:S(2)}) collective-permute-start(f32[24,8,128]{2,1,0:T(8,128)S(1)} %get-tuple-element.37), channel_id=1, source_target_pairs={{32,64},{96,128},{160,192},{224,256},{288,320},{352,384},{416,448}... | collective-permute-start | bytes 294920 | tf_op jit(solution)/shard_map/ppermute | solution.py:457
  65.4 12.2 %collective-permute-start.11 = (f32[24,8,128]{2,1,0:T(8,128)S(1)}, f32[24,8,128]{2,1,0:T(8,128)S(1)}, u32[]{:S(2)}, u32[]{:S(2)}) collective-permute-start(f32[24,8,128]{2,1,0:T(8,128)S(1)} %get-tuple-element.39), channel_id=1, source_target_pairs={{1,2},{3,4},{5,6},{7,8},{9,10},{11,12},{13,14},{15,16},{17,18},{19... | collective-permute-start | bytes 294920 | tf_op jit(solution)/shard_map/ppermute | solution.py:455
  67.3 10.2 %collective-permute-start.9 = (f32[24,8,128]{2,1,0:T(8,128)S(1)}, f32[24,8,128]{2,1,0:T(8,128)S(1)}, u32[]{:S(2)}, u32[]{:S(2)}) collective-permute-start(f32[24,8,128]{2,1,0:T(8,128)S(1)} %get-tuple-element.36), channel_id=1, source_target_pairs={{0,32},{64,96},{128,160},{192,224},{256,288},{320,352},{384,416},{... | collective-permute-start | bytes 294920 | tf_op jit(solution)/shard_map/ppermute | solution.py:456
